TPU v7x, 512 devices: a whole 4x8x8 slice. The times are simulated.
512 devices in a mesh: rve: 128 (over z, y, core), blk: 4 (over x).
Axes of the slice: x: 4, y: 8, z: 8, core: 2. Of those that a mesh axis runs over, the one named last changes fastest.
Arguments:
- strain: bfloat16 [13824, 6], P(('rve', 'blk')), may hold values from -6 to 6
- fiber_coeff: bfloat16 [13824, 2048], P(('rve', 'blk')), may hold values from 0.049804688 to 0.8984375
- gradients: float32 [12, 13824], P(None, ('rve', 'blk')), may hold values from -6 to 6
- volume: float32 [13824], P(('rve', 'blk')), may hold values from 0.1 to 1
- corners: int32 [4, 13824], P(None, ('rve', 'blk')), may hold values from 0 to 65535, as said below
- rve_worker: int32 [13824], P(('rve', 'blk')), may hold values from 0 to 127, as said below
- rve_slot: int32 [13824], P(('rve', 'blk')), may hold values from 0 to 80, as said below
- slot_element: int32 [41472], P(('rve', 'blk')), may hold values from -1 to 13823, as said below
- state_table: float32 [41472, 3, 2048], P(('rve', 'blk')), may hold values from -6 to 6
- loading: bfloat16 [6, 3, 2048], replicated, may hold values from -6 to 6
- compliance: bfloat16 [2048, 2048], P('rve'), as said below
Outputs:
- new_states: float32 [41472, 3, 2048], P(('rve', 'blk'))
- node_forces: float32 [3, 65536], P(None, ('rve', 'blk'))
- node_blocks: float32 [9, 65536], P(None, ('rve', 'blk'))
Inputs may be any that keep to these rules, and one draw needn't show every extreme that they name: `rve_worker`: counting the elements of one blk index, each worker number holds between 9 and 81 RVEs, the most reached by some worker; the elements of one aligned block of 27 that name one worker number are never more than 1, a count reached in every draw. `rve_slot`: A worker's RVEs fill its slots from 0 upward; no two elements share a worker and slot. `slot_element`: entry (w * 4 + b) * 81 + s holds e exactly when rve_worker[e] = w, (e // 27) % 4 = b and rve_slot[e] = s; every other entry is -1. The corners of elements in aligned block k of 27 elements are nodes k * 128 to (k + 2) * 128 - 1, and in the last block nodes k * 128 to (k + 1) * 128 - 1. `compliance`: Symmetric.
All inputs are finite; a program needn't handle non-finite values.
Results may differ from a plain program's by a relative error of at most 0.0023.
Values may be sent and summed in bfloat16 or wider, within the bound.
No kernel may reach another device: no remote copies, remote signals or barrier semaphores. Data moves between devices by JAX's collectives and lax.ppermute only.
A program may use at most 64 MiB of HBM per device.

v0:
```python
import functools

import jax
import jax.numpy as jnp
from jax import lax
from jax.experimental import pallas as pl
from jax.experimental.pallas import tpu as pltpu
from jax.sharding import PartitionSpec as P

ITERS = 3
NODE_DEV = 128
COMPS = 6
SLICE = 256

highest = lax.Precision.HIGHEST
f32 = jnp.float32
bf16 = jnp.bfloat16


def round_up(value, step):
    return (value + step - 1) // step * step


def dot_nn(left, right):
    return lax.dot_general(left, right, (((1,), (0,)), ((), ())), preferred_element_type=f32)


def dot_nt(left, right):
    return lax.dot_general(left, right, (((1,), (1,)), ((), ())), preferred_element_type=f32)


def split_dot_nt(left, right):
    left_head = left.astype(bf16)
    left_rest = (left - left_head.astype(f32)).astype(bf16)
    right_head = right.astype(bf16)
    right_rest = (right - right_head.astype(f32)).astype(bf16)
    return dot_nt(left_head, right_head) + (
        dot_nt(left_head, right_rest) + dot_nt(left_rest, right_head)
    )


def prepare_kernel(pick_ref, unit_ref, arrived_ref, loading_ref, state_ref, press_ref, forcing_ref, fiber_ref, still):
    cap = state_ref.shape[1]
    rows = pick_ref.shape[0]
    nodes = state_ref.shape[2]
    pick = pick_ref[...]
    strain = (dot_nn(pick, arrived_ref[:, nodes:]) + unit_ref[...]).astype(bf16)
    still[...] = jnp.zeros_like(still)
    for start in range(0, nodes, SLICE):
        cols = pl.ds(start, SLICE)
        fiber = dot_nn(pick, arrived_ref[:, cols])
        fiber_ref[:, cols] = fiber
        for a in range(3):
            still[0:cap, :] = state_ref[a, :, cols]
            forcing = dot_nn(strain, loading_ref[a, :, cols])
            forcing_ref[a, :, cols] = forcing
            press_ref[a * rows : (a + 1) * rows, cols] = (
                forcing - fiber * jnp.tanh(still[...])
            ).astype(bf16)


def solve_kernel(
    press_ref, forcing_ref, fiber_ref, loading_ref, occupied_ref, state_ref, network_hbm,
    table_ref, result_ref, network, pressure, current, products, sems,
):
    rows = fiber_ref.shape[0]
    nodes = fiber_ref.shape[1]
    cap = state_ref.shape[1]
    steps = nodes // SLICE

    def fetch(j):
        cols = pl.ds(j * SLICE, SLICE)
        return pltpu.make_async_copy(network_hbm.at[cols, :], network.at[cols, :], sems.at[j])

    for j in range(steps):
        fetch(j).start()
    for iteration in range(ITERS):
        source = press_ref if iteration == 0 else pressure.at[(iteration - 1) % 2]
        for j in range(steps):
            cols = pl.ds(j * SLICE, SLICE)
            if iteration == 0:
                fetch(j).wait()
            moved = dot_nt(source[...], network[cols, :])
            if iteration < ITERS - 1:
                fiber = fiber_ref[:, cols]
                for a in range(3):
                    block = moved[a * rows : (a + 1) * rows]
                    pressure[iteration % 2, a * rows : (a + 1) * rows, cols] = (
                        forcing_ref[a, :, cols] - fiber * jnp.tanh(block)
                    ).astype(bf16)
            else:
                for a in range(3):
                    current[a, :, cols] = moved[a * rows : (a + 1) * rows]
    stress = jnp.zeros((rows, 8), f32)
    damp = jnp.zeros((rows, 8 * COMPS), f32)
    fiber = fiber_ref[...]
    for a in range(3):
        state = current[a]
        head = state.astype(bf16)
        rest = (state - head.astype(f32)).astype(bf16)
        stress += dot_nt(head, loading_ref[a]) + dot_nt(rest, loading_ref[a])
        basis = current[a, cap : cap + COMPS, :]
        products[...] = jnp.zeros_like(products)
        for k in range(COMPS):
            products[8 * k : 8 * k + COMPS, :] = basis * basis[k : k + 1]
        bend = jnp.tanh(state)
        damp += split_dot_nt(fiber * (1.0 - bend * bend), products[...])
        table_ref[a] = jnp.where(
            occupied_ref[...] > 0, current[a, 0:cap, :], state_ref[a]
        )
    result_ref[:, 0 : 8 * COMPS] = damp
    result_ref[:, 8 * COMPS : 8 * COMPS + 8] = stress
    result_ref[:, 8 * COMPS + 8 :] = jnp.zeros((rows, result_ref.shape[1] - 8 * COMPS - 8), f32)


def corner_kernel(arrived_ref, pick_ref, fixed_ref, grad_ref, volume_ref, node_ref, out_ref, work, *, scale):
    got = lax.dot_general(
        arrived_ref[...], pick_ref[...], (((0,), (0,)), ((), ())),
        preferred_element_type=f32, precision=highest,
    )
    work[...] = got
    volume = volume_ref[...] * scale
    gx = grad_ref[0:1, :]
    gy = grad_ref[1:2, :]
    gz = grad_ref[2:3, :]

    def tangent(j):
        return fixed_ref[8 * j : 8 * j + 8, :] - work[8 * j : 8 * j + 8, :]

    t = [tangent(j) for j in range(COMPS)]
    columns = (
        t[0] * gx + t[4] * gz + t[5] * gy,
        t[1] * gy + t[3] * gz + t[5] * gx,
        t[2] * gz + t[3] * gy + t[4] * gx,
        work[8 * COMPS : 8 * COMPS + 8, :],
    )

    def rows(m):
        return (
            m[0:1] * gx + m[4:5] * gz + m[5:6] * gy,
            m[1:2] * gy + m[3:4] * gz + m[5:6] * gx,
            m[2:3] * gz + m[3:4] * gy + m[4:5] * gx,
        )

    blocks = [rows(m) for m in columns]
    contrib = [blocks[3][a] for a in range(3)] + [blocks[c][a] for a in range(3) for c in range(3)]
    lanes = work.shape[1]
    work[0:16, :] = jnp.zeros((16, lanes), f32)
    for r, row in enumerate(contrib):
        work[r : r + 1, :] = row * volume
    node = node_ref[...]
    spread = (lax.broadcasted_iota(jnp.int32, (2 * NODE_DEV, lanes), 0) == node).astype(f32)
    out_ref[...] = lax.dot_general(
        work[0:16, :], spread, (((1,), (1,)), ((), ())),
        preferred_element_type=f32, precision=highest,
    )


def from_behind(block, axis, distance):
    devices = range(lax.axis_size(axis))
    route = [(i - distance, i) for i in devices if i - distance in devices]
    return lax.ppermute(block, axis, route)


def body(
    strain, fiber_coeff, gradients, volume, corners, rve_worker, rve_slot, slot_element,
    state_table, loading, compliance,
):
    elems = strain.shape[0]
    workers = lax.axis_size("rve")
    columns = lax.axis_size("blk")
    cap = state_table.shape[0]
    nodes = compliance.shape[1]
    rows = round_up(cap + COMPS, 8)

    network = lax.all_gather(compliance, "rve", axis=0, tiled=True)

    worker_ids = jnp.arange(workers)
    send_pick = (worker_ids[:, None] == rve_worker[None, :]).astype(bf16)
    element_rows = jnp.concatenate([fiber_coeff, jnp.pad(strain, ((0, 0), (0, 128 - COMPS)))], axis=1)
    outgoing = jnp.dot(send_pick, element_rows)
    arrived = lax.all_to_all(outgoing, "rve", split_axis=0, concat_axis=0, tiled=True)

    occupied = slot_element >= 0
    home = jnp.where(occupied, slot_element // (elems * columns), -1)
    home_wide = jnp.pad(home, (0, rows - cap), constant_values=-1)
    slot_pick = (home_wide[:, None] == worker_ids[None, :])
    unit = (jnp.arange(rows)[:, None] - cap == jnp.arange(128)[None, :]).astype(f32)
    loading_rows = jnp.transpose(loading, (1, 0, 2))
    loading_wide = jnp.pad(loading_rows, ((0, 0), (0, 128 - COMPS), (0, 0)))
    loading_eight = jnp.pad(loading_rows, ((0, 0), (0, 8 - COMPS), (0, 0)))
    states = jnp.transpose(state_table, (1, 0, 2))

    press, forcing, fiber = pl.pallas_call(
        prepare_kernel,
        out_shape=(
            jax.ShapeDtypeStruct((3 * rows, nodes), bf16),
            jax.ShapeDtypeStruct((3, rows, nodes), f32),
            jax.ShapeDtypeStruct((rows, nodes), f32),
        ),
        scratch_shapes=[pltpu.VMEM((rows, SLICE), f32)],
        name="prepare",
    )(slot_pick.astype(bf16), unit, arrived, loading_wide, states)

    vmem = pl.BlockSpec(memory_space=pltpu.VMEM)
    table, result = pl.pallas_call(
        solve_kernel,
        out_shape=(
            jax.ShapeDtypeStruct((3, cap, nodes), f32),
            jax.ShapeDtypeStruct((rows, 128), f32),
        ),
        in_specs=[vmem] * 6 + [pl.BlockSpec(memory_space=pl.ANY)],
        out_specs=(vmem, vmem),
        scratch_shapes=[
            pltpu.VMEM((nodes, nodes), bf16),
            pltpu.VMEM((2, 3 * rows, nodes), bf16),
            pltpu.VMEM((3, rows, nodes), f32),
            pltpu.VMEM((8 * COMPS, nodes), f32),
            pltpu.SemaphoreType.DMA((nodes // SLICE,)),
        ],
        name="solve",
    )(press, forcing, fiber, loading_eight, occupied.astype(jnp.int32)[:, None], states, network)
    new_table = jnp.transpose(table, (1, 0, 2))

    backward = jnp.dot(slot_pick.astype(f32).T, result, precision=highest)
    returned = lax.all_to_all(backward, "rve", split_axis=0, concat_axis=0, tiled=True)

    fixed = result[cap : cap + COMPS, 8 * COMPS : 8 * COMPS + COMPS]
    fixed_rows = jnp.pad(fixed, ((0, 0), (0, 2))).reshape(8 * COMPS, 1)
    corner_pick = jnp.tile(send_pick.astype(f32), (1, 4))
    grad_rows = jnp.transpose(gradients.reshape(4, 3, elems), (1, 0, 2)).reshape(3, 4 * elems)
    device_rank = lax.axis_index("rve") * columns + lax.axis_index("blk")
    local_node = (corners - device_rank * NODE_DEV).reshape(1, 4 * elems)
    assembled = pl.pallas_call(
        functools.partial(corner_kernel, scale=1.0 / (3 * nodes)),
        out_shape=jax.ShapeDtypeStruct((16, 2 * NODE_DEV), f32),
        scratch_shapes=[pltpu.VMEM((128, 4 * elems), f32)],
        name="corners",
    )(returned, corner_pick, fixed_rows, grad_rows, jnp.tile(volume, 4)[None, :], local_node)
    own_rows = assembled[:, :NODE_DEV] + from_behind(assembled[:, NODE_DEV:], ("rve", "blk"), 1)
    return (new_table, own_rows[:3], own_rows[3:12])


def solution(mesh):
    both = ("rve", "blk")
    return jax.shard_map(
        body,
        mesh=mesh,
        in_specs=(
            P(both, None),
            P(both, None),
            P(None, both),
            P(both),
            P(None, both),
            P(both),
            P(both),
            P(both),
            P(both, None, None),
            P(),
            P("rve", None),
        ),
        out_specs=(P(both, None, None), P(None, both), P(None, both)),
        check_vma=False,
    )
```

profile of v0, /device:TPU:64, one launch (start us, length us, event | category | flops | bytes accessed | tf_op | source)
XLA Modules:
  0.0 171.1 jit_solution(9725491866360296147)
XLA Ops:
  7.2 0.7 all-gather.2.cloned.1.call-update
  7.9 0.8 copy.32
  8.7 1.3 convolution_bitcast_fusion
  10.6 1.0 reduce
  11.6 1.4 reshape.59
  13.0 16.6 %all-to-all-start = ((bf16[128,2,1088]{2,1,0:T(2,128)(2,1)}), bf16[128,2,1088]{2,1,0:T(2,128)(2,1)S(1)}, u32[]{:S(2)}, u32[]{:S(2)}) async-start(bf16[128,2,1088]{2,1,0:T(2,128)(2,1)} %reshape.59), calls=%async_computation | async-start | bytes 1179648 | tf_op jit(solution)/shard_map/all_to_all | solution.py:182
  29.7 1.3 pad.22.loading_ref
  31.7 0.7 copy.35.occupied_ref
  33.1 0.7 fusion.8
  33.8 17.3 %all-to-all-done = bf16[128,2,1088]{2,1,0:T(2,128)(2,1)S(1)} async-done(((bf16[128,2,1088]{2,1,0:T(2,128)(2,1)}), bf16[128,2,1088]{2,1,0:T(2,128)(2,1)S(1)}, u32[]{:S(2)}, u32[]{:S(2)}) %all-to-all-start) | async-done | bytes 557088 | tf_op jit(solution)/shard_map/all_to_all | solution.py:182
  51.7 0.9 copy.43
  52.6 4.9 %prepare.1 = (bf16[264,2048]{1,0:T(8,128)(2,1)}, f32[3,88,2048]{2,1,0:T(8,128)}, f32[88,2048]{1,0:T(8,128)}) custom-call(bf16[88,128]{1,0:T(8,128)(2,1)} %get-tuple-element.13.pick_ref, f32[88,128]{1,0:T(8,128)} %get-tuple-element.14.unit_ref, bf16[128,2176]{1,0:T(8,128)(2,1)} %bitcast.22, bf16[3,128,2048]{2,1,0:T(8,128)(2,1)} %pad.22.loading_ref, ...), custom_call_target="tpu_custom_call" | custom-call | tf_op jit(solution)/shard_map/prepare/pallas_call | solution.py:194
  57.5 52.1 %all-gather.2.cloned.1.call-done.network_hbm = bf16[2048,2048]{1,0:T(8,128)(2,1)} async-done(((bf16[16,2048]{1,0:T(8,128)(2,1)}), bf16[2048,2048]{1,0:T(8,128)(2,1)}) %all-gather.2.cloned.1.call-update) | async-done | bytes 8388624 | tf_op jit(solution)/shard_map/all_gather | solution.py:176
  109.6 17.4 %solve.1 = (f32[3,81,2048]{2,1,0:T(8,128)}, f32[88,128]{1,0:T(8,128)}) custom-call(bf16[264,2048]{1,0:T(8,128)(2,1)} %get-tuple-element.8.press_ref, f32[3,88,2048]{2,1,0:T(8,128)} %get-tuple-element.9.forcing_ref, f32[88,2048]{1,0:T(8,128)} %get-tuple-element.10.fiber_ref, bf16[3,8,2048]{2,1,0:T(8,128)(2,1)} %pad.23.loading_ref, ...), custom_call_target="tpu_custom_call" | custom-call | tf_op jit(solution)/shard_map/solve/pallas_call | solution.py:206
  127.1 1.7 %fusion.7 = f32[128,128]{1,0:T(8,128)} fusion(f32[88,128]{1,0:T(8,128)} %get-tuple-element.12, s32[88]{0:T(128)S(1)} %pad.20), kind=kOutput, calls=%fused_computation.12 | convolution fusion | flops 17312768 | bytes 110944 | tf_op jit(solution)/shard_map/dot_general | solution.py:225
  128.8 10.1 %all-to-all-start.1 = ((f32[128,1,128]{2,1,0:T(1,128)}), f32[128,1,128]{2,1,0:T(1,128)S(1)}, u32[]{:S(2)}, u32[]{:S(2)}) async-start(f32[128,1,128]{2,1,0:T(1,128)} %bitcast.6), calls=%async_computation.1 | async-start | bytes 131072 | tf_op jit(solution)/shard_map/all_to_all | solution.py:226
  139.0 0.7 copy.38.pick_ref
  141.0 0.8 slice.15
  142.5 7.3 %all-to-all-done.1 = f32[128,1,128]{2,1,0:T(1,128)S(1)} async-done(((f32[128,1,128]{2,1,0:T(1,128)}), f32[128,1,128]{2,1,0:T(1,128)S(1)}, u32[]{:S(2)}, u32[]{:S(2)}) %all-to-all-start.1) | async-done | bytes 65568 | tf_op jit(solution)/shard_map/all_to_all | solution.py:226
  150.5 2.1 %corners.1 = f32[16,256]{1,0:T(8,128)} custom-call(f32[128,128]{1,0:T(8,128)} %bitcast.25, f32[128,108]{1,0:T(8,128)} %copy.38.pick_ref, f32[48,1]{1,0:T(8,128)} %reshape.58.fixed_ref, f32[3,108]{1,0:T(4,128)} %reshape.55.grad_ref, f32[1,108]{1,0:T(1,128)} %broadcast_in_dim_tile.3.volume_ref, s32[1,108]{1,0:T(1,128)} %reshape.56.node_ref), custom_call_target="tpu_custom_call" | custom-call | tf_op jit(solution)/shard_map/corners/pallas_call | solution.py:234
  152.5 0.7 slice.21
  153.2 3.4 %collective-permute-start = (f32[16,128]{1,0:T(8,128)S(1)}, f32[16,128]{1,0:T(8,128)S(1)}, u32[]{:S(2)}, u32[]{:S(2)}) collective-permute-start(f32[16,128]{1,0:T(8,128)S(1)} %slice.21), channel_id=1, source_target_pairs={{0,1},{1,2},{2,3},{3,4},{4,5},{5,6},{6,7},{7,8},{8,9},{9,10},{10,1... | collective-permute-start | bytes 24584 | tf_op jit(solution)/shard_map/ppermute | solution.py:162
  156.6 5.8 %collective-permute-done = f32[16,128]{1,0:T(8,128)S(1)} collective-permute-done((f32[16,128]{1,0:T(8,128)S(1)}, f32[16,128]{1,0:T(8,128)S(1)}, u32[]{:S(2)}, u32[]{:S(2)}) %collective-permute-start) | collective-permute-done | bytes 8224 | tf_op jit(solution)/shard_map/ppermute | solution.py:162
  162.4 0.7 slice_add_fusion
  (37 shorter events, 6.5 us)
Async XLA Ops:
  7.2 22.4 %copy-start.1 = (bf16[6,3,2048]{2,1,0:T(4,128)(2,1)S(1)}, bf16[6,3,2048]{2,1,0:T(4,128)(2,1)}, u32[]{:S(2)}) copy-start(bf16[6,3,2048]{2,1,0:T(4,128)(2,1)} %param.19) | copy-start | bytes 221188
  7.2 102.4 %all-gather.2.cloned.1.call-start = ((), (), s32[]{:S(2)}) async-start(), calls=%async_computation.2 | async-start | bytes 8454144 | tf_op jit(solution)/shard_map/all_gather | solution.py:176
  11.6 20.1 %copy-start.6 = (s32[81]{0:T(128)S(1)}, s32[81]{0:T(128)}, u32[]{:S(2)}) copy-start(s32[81]{0:T(128)} %param.17) | copy-start | bytes 976
  11.6 20.8 %copy-start.4 = (s32[4,27]{1,0:T(4,128)S(1)}, s32[4,27]{1,0:T(4,128)}, u32[]{:S(2)}) copy-start(s32[4,27]{1,0:T(4,128)} %param.15) | copy-start | bytes 1300
  13.0 38.1 %all-to-all-start = ((bf16[128,2,1088]{2,1,0:T(2,128)(2,1)}), bf16[128,2,1088]{2,1,0:T(2,128)(2,1)S(1)}, u32[]{:S(2)}, u32[]{:S(2)}) async-start(bf16[128,2,1088]{2,1,0:T(2,128)(2,1)} %reshape.59), calls=%async_computation | async-start | bytes 1179648 | tf_op jit(solution)/shard_map/all_to_all | solution.py:182
  109.6 29.3 %copy-start.3 = (s32[27]{0:T(128)S(1)}, s32[27]{0:T(128)}, u32[]{:S(2)}) copy-start(s32[27]{0:T(128)} %param.16) | copy-start | bytes 328
  109.6 30.2 %copy-start.2 = (f32[12,27]{1,0:T(8,128)S(1)}, f32[12,27]{1,0:T(8,128)}, u32[]{:S(2)}) copy-start(f32[12,27]{1,0:T(8,128)} %param.13) | copy-start | bytes 3892
  109.6 30.8 %copy-start.5 = (f32[27]{0:T(128)S(1)}, f32[27]{0:T(128)}, u32[]{:S(2)}) copy-start(f32[27]{0:T(128)} %param.14) | copy-start | bytes 328
  128.8 21.0 %all-to-all-start.1 = ((f32[128,1,128]{2,1,0:T(1,128)}), f32[128,1,128]{2,1,0:T(1,128)S(1)}, u32[]{:S(2)}, u32[]{:S(2)}) async-start(f32[128,1,128]{2,1,0:T(1,128)} %bitcast.6), calls=%async_computation.1 | async-start | bytes 131072 | tf_op jit(solution)/shard_map/all_to_all | solution.py:226
  149.8 0.6 copy-start
  153.2 9.2 %collective-permute-start = (f32[16,128]{1,0:T(8,128)S(1)}, f32[16,128]{1,0:T(8,128)S(1)}, u32[]{:S(2)}, u32[]{:S(2)}) collective-permute-start(f32[16,128]{1,0:T(8,128)S(1)} %slice.21), channel_id=1, source_target_pairs={{0,1},{1,2},{2,3},{3,4},{4,5},{5,6},{6,7},{7,8},{8,9},{9,10},{10,1... | collective-permute-start | bytes 24584 | tf_op jit(solution)/shard_map/ppermute | solution.py:162
Sparse Core Ops, SparseCore 0:
  11.1 98.4 all-gather.1
where the time goes:
time: 172 us; the launch traced here: 171 us
  waiting for transfers between devices  83.2 us (48%)
  starting transfers between devices  30.1 us (18%)
  Pallas kernels  24.4 us (14%)
  between operations  14.2 us (8%)
  local copies, waits for them, and re-layouts  13.6 us (8%)
  matrix products  3.08 us (2%)
  other arithmetic  2.51 us (1%)
    all_gather x1, waiting for transfers between devices, body(): network = lax.all_gather(compliance, 'rve', axis=0, tiled=True)  52.1 us
    pallas_call x1, Pallas kernels, body(): pl.pallas_call(solve_kernel, out_shape=(jax.ShapeDtypeStruct((3, cap, nod...  17.4 us
    all_to_all x1, waiting for transfers between devices, body(): lax.all_to_all(outgoing, 'rve', split_axis=0, concat_axis=0, tiled=True)  17.3 us
    all_to_all x1, starting transfers between devices, body(): lax.all_to_all(outgoing, 'rve', split_axis=0, concat_axis=0, tiled=True)  16.6 us
    all_to_all x1, starting transfers between devices, body(): lax.all_to_all(backward, 'rve', split_axis=0, concat_axis=0, tiled=True)  10.1 us
    all_to_all x1, waiting for transfers between devices, body(): lax.all_to_all(backward, 'rve', split_axis=0, concat_axis=0, tiled=True)  7.35 us
    ppermute x1, waiting for transfers between devices, from_behind(): return lax.ppermute(block, axis, route)  5.8 us
    pallas_call x1, Pallas kernels, body(): pl.pallas_call(prepare_kernel, out_shape=(jax.ShapeDtypeStruct((3 * rows,...  4.92 us
  transfers between devices with their start and end apart: 4, of which 4 were waited for; matrix products, arithmetic and copies ran while one was open for 8% of the time, Pallas kernels for 3%

commit v1 on v0

v1 whole, which is shorter than its diff:
```python
import functools

import jax
import jax.numpy as jnp
from jax import lax
from jax.experimental import pallas as pl
from jax.experimental.pallas import tpu as pltpu
from jax.sharding import PartitionSpec as P

ITERS = 3
NODE_DEV = 128
COMPS = 6
SLICE = 256
BLOCKS = 8
SENT = 5

highest = lax.Precision.HIGHEST
f32 = jnp.float32
bf16 = jnp.bfloat16


def round_up(value, step):
    return (value + step - 1) // step * step


def dot_nn(left, right):
    return lax.dot_general(left, right, (((1,), (0,)), ((), ())), preferred_element_type=f32)


def dot_nt(left, right):
    return lax.dot_general(left, right, (((1,), (1,)), ((), ())), preferred_element_type=f32)


def three_parts(value):
    head = value.astype(bf16)
    rest = value - head.astype(f32)
    middle = rest.astype(bf16)
    return head, middle, (rest - middle.astype(f32)).astype(bf16)


def prepare_kernel(pick_ref, unit_ref, arrived_ref, loading_ref, state_ref, press_ref, forcing_ref, fiber_ref, still):
    cap = state_ref.shape[1]
    rows = pick_ref.shape[0]
    nodes = state_ref.shape[2]
    pick = pick_ref[...]
    strain = (dot_nn(pick, arrived_ref[:, nodes:]) + unit_ref[...]).astype(bf16)
    still[...] = jnp.zeros_like(still)
    for start in range(0, nodes, SLICE):
        cols = pl.ds(start, SLICE)
        fiber = dot_nn(pick, arrived_ref[:, cols])
        fiber_ref[:, cols] = fiber
        for a in range(3):
            still[0:cap, :] = state_ref[a, :, cols]
            forcing = dot_nn(strain, loading_ref[a, :, cols])
            forcing_ref[a, :, cols] = forcing
            first = (forcing - fiber * jnp.tanh(still[...])).astype(bf16)
            press_ref[a * rows : (a + 1) * rows, cols] = first
            if nodes + start < press_ref.shape[1]:
                press_ref[a * rows : (a + 1) * rows, pl.ds(nodes + start, SLICE)] = first


def solve_kernel(
    side_ref, pick_ref, loading_ref, occupied_ref, press_hbm, forcing_hbm, fiber_hbm, state_hbm,
    mine_hbm, other_hbm, table_hbm, result_ref, back_ref,
    network, pressure, forcing, fiber, table, damp_sum, stress_sum, net_sems, in_sems, out_sems,
):
    rows = fiber.shape[0]
    nodes = fiber.shape[1]
    cap = table.shape[1]

    def fetch(i, side, source, k):
        return pltpu.make_async_copy(source.at[i], network.at[i, :, side], net_sems.at[i, k])

    inputs = (
        pltpu.make_async_copy(press_hbm, pressure.at[0], in_sems.at[0]),
        pltpu.make_async_copy(forcing_hbm, forcing, in_sems.at[1]),
        pltpu.make_async_copy(fiber_hbm, fiber, in_sems.at[2]),
        pltpu.make_async_copy(state_hbm, table, in_sems.at[3]),
    )
    inputs[0].start()
    arrival = [(1 + i) % BLOCKS for i in range(BLOCKS)]
    for side in range(2):

        @pl.when(side_ref[0] == side)
        def _():
            for i in arrival:
                fetch(i, side, mine_hbm, 0).start()
                fetch(i, 1 - side, other_hbm, 1).start()

    for copy in inputs[1:]:
        copy.start()

    def wait_network(i):
        fetch(i, 0, mine_hbm, 0).wait()
        fetch(i, 0, other_hbm, 1).wait()

    def net(i, start, blocks):
        cols = pl.ds(start * SLICE, blocks * SLICE)
        return network[i, :, :, :, cols].reshape(SLICE, blocks * SLICE)

    def stored(n):
        return pltpu.make_async_copy(
            table.at[:, :, pl.ds(n * SLICE, SLICE)],
            table_hbm.at[:, :, pl.ds(n * SLICE, SLICE)],
            out_sems.at[n],
        )

    damp_sum[...] = jnp.zeros_like(damp_sum)
    stress_sum[...] = jnp.zeros_like(stress_sum)
    inputs[0].wait()
    for i in arrival[:3]:
        wait_network(i)
    for iteration in range(ITERS):
        source = pressure.at[iteration]
        for step in range(BLOCKS):
            n = (step + 4) % BLOCKS
            cols = pl.ds(n * SLICE, SLICE)
            if iteration == 0 and step < BLOCKS - 3:
                wait_network(n)
            moved = dot_nt(source[:, pl.ds(n * SLICE, SENT * SLICE)], net(n, 0, SENT))
            for d in range(1, BLOCKS - SENT + 1):
                i = (n - d) % BLOCKS
                moved += dot_nn(source[:, pl.ds(i * SLICE, SLICE)], net(i, d, 1))
            if iteration == 0 and step == 0:
                inputs[1].wait()
                inputs[2].wait()
            damping = fiber[:, cols]
            bend = jnp.tanh(moved)
            if iteration < ITERS - 1:
                for a in range(3):
                    block = slice(a * rows, (a + 1) * rows)
                    value = (forcing[a, :, cols] - damping * bend[block]).astype(bf16)
                    pressure[iteration + 1, block, cols] = value
                    if n < SENT - 1:
                        pressure[iteration + 1, block, pl.ds(nodes + n * SLICE, SLICE)] = value
                continue
            if step == 0:
                inputs[3].wait()
            products = []
            for a in range(3):
                low = a * rows
                table[a, :, cols] = jnp.where(
                    occupied_ref[...] > 0, moved[low : low + cap], table[a, :, cols]
                )
                basis = moved[low + rows - 8 : low + rows]
                products += [basis * basis[k : k + 1] for k in range(1, COMPS + 1)]
            stored(n).start()
            products.append(jnp.zeros((256 - 24 * COMPS, SLICE), f32))
            weights = jnp.concatenate(products, axis=0).astype(bf16)
            damped = (jnp.concatenate([damping] * 3, axis=0) * (1.0 - bend * bend)).astype(bf16)
            damp_sum[...] += dot_nt(damped, weights)
            head = moved.astype(bf16)
            rest = (moved - head.astype(f32)).astype(bf16)
            load = loading_ref[:, cols]
            stress_sum[...] += dot_nt(head, load) + dot_nt(rest, load)

    def gathered(sums, shift):
        lanes = sums.shape[1]
        return (
            sums[0:rows]
            + pltpu.roll(sums[rows : 2 * rows], lanes - shift, 1)
            + pltpu.roll(sums[2 * rows : 3 * rows], lanes - 2 * shift, 1)
        )[:, 0:128]

    lane = lax.broadcasted_iota(jnp.int32, result_ref.shape, 1)
    stress = gathered(stress_sum[...], 8)
    damp = gathered(damp_sum[...], 8 * COMPS)
    result = jnp.where(lane < 8 * COMPS, damp, jnp.where(lane < 8 * COMPS + 8, stress, 0.0))
    result_ref[...] = result
    pick = pick_ref[...]
    head, middle, rest = three_parts(result)
    back_ref[...] = dot_nn(pick, head) + (dot_nn(pick, middle) + dot_nn(pick, rest))
    for n in range(BLOCKS):
        stored(n).wait()


def corner_kernel(own_ref, behind_ref, fixed_ref, own_data_ref, behind_data_ref, force_ref, block_ref, work, *, scale):
    lanes = work.shape[2]
    workers = own_ref.shape[0]
    total = jnp.zeros((16, NODE_DEV), f32)
    work[...] = jnp.zeros_like(work)
    for part, (arrived, data) in enumerate(((own_ref, own_data_ref), (behind_ref, behind_data_ref))):
        gx = data[0:1, :]
        gy = data[1:2, :]
        gz = data[2:3, :]
        volume = data[3:4, :] * scale
        node = data[4:5, :].astype(jnp.int32) - part * NODE_DEV
        worker = data[5:6, :].astype(jnp.int32)
        pick = (lax.broadcasted_iota(jnp.int32, (workers, lanes), 0) == worker).astype(f32)
        got = lax.dot_general(
            arrived[...], pick, (((0,), (0,)), ((), ())), preferred_element_type=f32, precision=highest
        )
        t = [fixed_ref[8 * j : 8 * j + 8, :] - got[8 * j : 8 * j + 8, :] for j in range(COMPS)]
        columns = (
            got[8 * COMPS : 8 * COMPS + 8, :],
            t[0] * gx + t[4] * gz + t[5] * gy,
            t[1] * gy + t[3] * gz + t[5] * gx,
            t[2] * gz + t[3] * gy + t[4] * gx,
        )
        for c, m in enumerate(columns):
            blocks = (
                m[1:2] * gx + m[5:6] * gz + m[6:7] * gy,
                m[2:3] * gy + m[4:5] * gz + m[6:7] * gx,
                m[3:4] * gz + m[4:5] * gy + m[5:6] * gx,
            )
            for a in range(3):
                r = a if c == 0 else 3 + 3 * a + c - 1
                work[part, r : r + 1, :] = blocks[a] * volume
        spread = (lax.broadcasted_iota(jnp.int32, (NODE_DEV, lanes), 0) == node).astype(f32)
        total += lax.dot_general(
            work[part], spread, (((1,), (1,)), ((), ())), preferred_element_type=f32, precision=highest
        )
    force_ref[...] = total[0:3]
    block_ref[...] = total[3:12]


def from_behind(block, axis, distance):
    devices = range(lax.axis_size(axis))
    route = [(i - distance, i) for i in devices if i - distance in devices]
    return lax.ppermute(block, axis, route)


RVE = ("z", "y", "core")
ALL = ("z", "y", "core", "blk")


def spread_network(compliance):
    rows, nodes = compliance.shape
    around = jnp.concatenate([compliance, compliance[:, : (SENT - 1) * SLICE]], axis=1)
    half = lax.dynamic_slice(around, (0, lax.axis_index("z") * SLICE), (rows, SENT * SLICE))
    count = lax.axis_size("y")
    line = lax.all_to_all(
        jnp.broadcast_to(half[None], (count,) + half.shape), "y", split_axis=0, concat_axis=0, tiled=True
    )
    plane = lax.all_gather(line.reshape(count * rows, SENT * SLICE), "z", axis=0, tiled=True)
    other = lax.ppermute(plane, "core", [(0, 1), (1, 0)])
    shape = (BLOCKS, count, rows, SENT * SLICE)
    return line, plane.reshape(shape), other.reshape(shape)


def body(
    strain, fiber_coeff, gradients, volume, corners, rve_worker, rve_slot, slot_element,
    state_table, loading, compliance,
):
    elems = strain.shape[0]
    workers = lax.axis_size(RVE)
    columns = lax.axis_size("blk")
    cap = state_table.shape[0]
    nodes = compliance.shape[1]
    rows = round_up(cap + COMPS, 8)

    line, mine, other = spread_network(compliance)

    worker_ids = jnp.arange(workers)
    send_pick = (worker_ids[:, None] == rve_worker[None, :]).astype(bf16)
    element_rows = jnp.concatenate([fiber_coeff, jnp.pad(strain, ((0, 0), (0, 128 - COMPS)))], axis=1)
    outgoing = jnp.dot(send_pick, element_rows)
    outgoing = lax.optimization_barrier((outgoing, line))[0]
    arrived = lax.all_to_all(outgoing, RVE, split_axis=0, concat_axis=0, tiled=True)

    device_rank = lax.axis_index(ALL)
    corner_data = jnp.concatenate(
        [
            jnp.transpose(gradients.reshape(4, 3, elems), (1, 0, 2)).reshape(3, 4 * elems),
            jnp.tile(volume, 4)[None, :],
            (corners - device_rank * NODE_DEV).reshape(1, 4 * elems).astype(f32),
            jnp.tile(rve_worker, 4)[None, :].astype(f32),
            jnp.zeros((2, 4 * elems), f32),
        ],
        axis=0,
    )
    behind_data = from_behind(corner_data, ALL, 1)

    occupied = slot_element >= 0
    home = jnp.where(occupied, slot_element // (elems * columns), -1)
    home_wide = jnp.pad(home, (0, rows - cap), constant_values=-1)
    slot_pick = (home_wide[:, None] == worker_ids[None, :]).astype(bf16)
    unit = (jnp.arange(rows)[:, None] - cap == jnp.arange(128)[None, :]).astype(f32)
    loading_rows = jnp.transpose(loading, (1, 0, 2))
    loading_wide = jnp.pad(loading_rows, ((0, 0), (0, 128 - COMPS), (0, 0)))
    loading_sums = jnp.pad(loading_rows, ((0, 0), (1, 1), (0, 0))).reshape(24, nodes)
    loading_sums = jnp.pad(loading_sums, ((8 * COMPS, 128 - 24 - 8 * COMPS), (0, 0)))
    states = jnp.transpose(state_table, (1, 0, 2))
    wide = nodes + (SENT - 1) * SLICE

    press, forcing, fiber = pl.pallas_call(
        prepare_kernel,
        out_shape=(
            jax.ShapeDtypeStruct((3 * rows, wide), bf16),
            jax.ShapeDtypeStruct((3, rows, nodes), f32),
            jax.ShapeDtypeStruct((rows, nodes), f32),
        ),
        scratch_shapes=[pltpu.VMEM((rows, SLICE), f32)],
        name="prepare",
    )(slot_pick, unit, arrived, loading_wide, states)

    vmem = pl.BlockSpec(memory_space=pltpu.VMEM)
    hbm = pl.BlockSpec(memory_space=pl.ANY)
    table, result, backward = pl.pallas_call(
        solve_kernel,
        out_shape=(
            jax.ShapeDtypeStruct((3, cap, nodes), f32),
            jax.ShapeDtypeStruct((rows, 128), f32),
            jax.ShapeDtypeStruct((workers, 128), f32),
        ),
        in_specs=[pl.BlockSpec(memory_space=pltpu.SMEM)] + [vmem] * 3 + [hbm] * 6,
        out_specs=(hbm, vmem, vmem),
        scratch_shapes=[
            pltpu.VMEM((BLOCKS, mine.shape[1], 2, mine.shape[2], SENT * SLICE), bf16),
            pltpu.VMEM((ITERS, 3 * rows, wide), bf16),
            pltpu.VMEM((3, rows, nodes), f32),
            pltpu.VMEM((rows, nodes), f32),
            pltpu.VMEM((3, cap, nodes), f32),
            pltpu.VMEM((3 * rows, 256), f32),
            pltpu.VMEM((3 * rows, 128), f32),
            pltpu.SemaphoreType.DMA((BLOCKS, 2)),
            pltpu.SemaphoreType.DMA((4,)),
            pltpu.SemaphoreType.DMA((BLOCKS,)),
        ],
        name="solve",
    )(
        lax.axis_index("core")[None].astype(jnp.int32), slot_pick.T, loading_sums,
        occupied.astype(jnp.int32)[:, None], press, forcing, fiber, states, mine, other,
    )
    new_table = jnp.transpose(table, (1, 0, 2))

    returned = lax.all_to_all(backward, RVE, split_axis=0, concat_axis=0, tiled=True)
    behind = from_behind(returned, ALL, 1)
    fixed = jnp.pad(result[cap : cap + COMPS, 8 * COMPS + 1 : 8 * COMPS + 1 + COMPS], ((0, 0), (1, 1)))
    forces, blocks = pl.pallas_call(
        functools.partial(corner_kernel, scale=1.0 / (3 * nodes)),
        out_shape=(
            jax.ShapeDtypeStruct((3, NODE_DEV), f32),
            jax.ShapeDtypeStruct((9, NODE_DEV), f32),
        ),
        scratch_shapes=[pltpu.VMEM((2, 16, 4 * elems), f32)],
        name="corners",
    )(returned, behind, fixed.reshape(8 * COMPS, 1), corner_data, behind_data)
    return (new_table, forces, blocks)


def solution(mesh):
    workers, columns = mesh.devices.shape
    mesh = jax.sharding.Mesh(mesh.devices.reshape(8, workers // 16, 2, columns), ALL)
    return jax.shard_map(
        body,
        mesh=mesh,
        in_specs=(
            P(ALL, None),
            P(ALL, None),
            P(None, ALL),
            P(ALL),
            P(None, ALL),
            P(ALL),
            P(ALL),
            P(ALL),
            P(ALL, None, None),
            P(),
            P(RVE, None),
        ),
        out_specs=(P(ALL, None, None), P(None, ALL), P(None, ALL)),
        check_vma=False,
    )
```

time: 172 us -> 178 us (1.035)
  blocking collectives: 0 us -> 20.3 us
  waiting for transfers between devices: 83.2 us -> 74.9 us
  starting transfers between devices: 30.1 us -> 27.3 us
  matrix products: 3.08 us -> 1.2 us
    all_to_all x0 -> x1, blocking collectives: none -> 20.3 us  [spread_network(): lax.all_to_all(jnp.broadcast_to(half[None], (count,) + half.shape), 'y',...]
    all_gather x1, waiting for transfers between devices: 52.1 us -> 44 us  [spread_network(): lax.all_gather(line.reshape(count * rows, SENT * SLICE), 'z', axis=0, til...]
    all_to_all x2, starting transfers between devices: 26.7 us -> 18.6 us  [the longest x1 11.3 us: body(): lax.all_to_all(outgoing, RVE, split_axis=0, concat_axis=0, tiled=True)]
    ppermute x1 -> x2, starting transfers between devices: 3.37 us -> 6.74 us  [from_behind(): return lax.ppermute(block, axis, route)]
    all_to_all x2, waiting for transfers between devices: 24.6 us -> 26.7 us  [the longest x1 15.7 us: body(): lax.all_to_all(outgoing, RVE, split_axis=0, concat_axis=0, tiled=True)]
    ppermute x0 -> x1, starting transfers between devices: none -> 1.91 us  [spread_network(): other = lax.ppermute(plane, 'core', [(0, 1), (1, 0)])]
    ppermute x1 -> x2, waiting for transfers between devices: 5.8 us -> 4.24 us  [from_behind(): return lax.ppermute(block, axis, route)]
    unnamed x19 -> x23, local copies, waits for them, and re-layouts: 4.44 us -> 5.86 us
  transfers between devices with their start and end apart: 4 -> 6, of which waited for: 4 -> 4; matrix products, arithmetic and copies ran while one was open for 8% -> 8% of each run, Pallas kernels for 3% -> 3%
where the time goes in v1:
time: 178 us
  waiting for transfers between devices  74.9 us (42%)
  starting transfers between devices  27.3 us (15%)
  Pallas kernels  24.4 us (14%)
  blocking collectives  20.3 us (11%)
  between operations  14.3 us (8%)
  local copies, waits for them, and re-layouts  12 us (7%)
  other arithmetic  3.17 us (2%)
    all_gather x1, waiting for transfers between devices, spread_network(): lax.all_gather(line.reshape(count * rows, SENT * SLICE), 'z', axis=0, til...  44 us
    all_to_all x1, blocking collectives, spread_network(): lax.all_to_all(jnp.broadcast_to(half[None], (count,) + half.shape), 'y',...  20.3 us
    pallas_call x1, Pallas kernels, body(): pl.pallas_call(solve_kernel, out_shape=(jax.ShapeDtypeStruct((3, cap, nod...  17.1 us
    all_to_all x1, waiting for transfers between devices, body(): lax.all_to_all(outgoing, RVE, split_axis=0, concat_axis=0, tiled=True)  15.7 us
    all_to_all x1, starting transfers between devices, body(): lax.all_to_all(outgoing, RVE, split_axis=0, concat_axis=0, tiled=True)  11.3 us
    all_to_all x1, waiting for transfers between devices, body(): lax.all_to_all(backward, RVE, split_axis=0, concat_axis=0, tiled=True)  10.9 us
    all_to_all x1, starting transfers between devices, body(): lax.all_to_all(backward, RVE, split_axis=0, concat_axis=0, tiled=True)  7.35 us
    ppermute x2, starting transfers between devices, from_behind(): return lax.ppermute(block, axis, route)  6.74 us
  transfers between devices with their start and end apart: 6, of which 4 were waited for; matrix products, arithmetic and copies ran while one was open for 8% of the time, Pallas kernels for 3%

profile of v1, /device:TPU:64, one launch (start us, length us, event | category | flops | bytes accessed | tf_op | source)
XLA Modules:
  0.0 177.6 jit_solution(15927752270774037736)
XLA Ops:
  7.2 0.8 slice.6
  8.0 0.8 fusion.11
  8.8 20.3 %all_to_all.27 = bf16[8,16,1280]{2,1,0:T(8,128)(2,1)} all-to-all(bf16[8,16,1280]{2,1,0:T(8,128)(2,1)S(1)} %broadcast_in_dim.28), channel_id=1, replica_groups=mesh['z'=8,'y'=8,'core'=2,'blk'=4] {'y'}, dimensions={0} | all-to-all | bytes 655360 | tf_op jit(solution)/shard_map/all_to_all | solution.py:232
  29.1 44.0 %all-gather.2.cloned.1.call-done = bf16[1024,1280]{1,0:T(8,128)(2,1)} async-done(((bf16[128,1280]{1,0:T(8,128)(2,1)}), bf16[1024,1280]{1,0:T(8,128)(2,1)}) %all-gather.2.cloned.1.call-update) | async-done | bytes 2621456 | tf_op jit(solution)/shard_map/all_gather | solution.py:235
  73.2 1.9 %collective-permute-start = (bf16[1024,1280]{1,0:T(8,128)(2,1)}, bf16[1024,1280]{1,0:T(8,128)(2,1)}, u32[]{:S(2)}, u32[]{:S(2)}) collective-permute-start(bf16[1024,1280]{1,0:T(8,128)(2,1)} %all-gather.2.cloned.1.call-done), channel_id=1, source_target_pairs={{0,4},{4,0},{1,5},{5,1},{2,6},{6,2},{3,7},{7,3},{8,12},{12,8},{9,1... | collective-permute-start | bytes 7864328 | tf_op jit(solution)/shard_map/ppermute | solution.py:236
  75.1 0.8 copy.31
  75.9 1.0 copy.41
  76.8 1.2 fusion.2
  78.5 1.0 reduce
  79.6 1.4 reshape.76
  80.9 11.3 %all-to-all-start.1 = ((bf16[128,2,1088]{2,1,0:T(2,128)(2,1)}), bf16[128,2,1088]{2,1,0:T(2,128)(2,1)S(1)}, u32[]{:S(2)}, u32[]{:S(2)}) async-start(bf16[128,2,1088]{2,1,0:T(2,128)(2,1)} %reshape.76), calls=%async_computation.1 | async-start | bytes 1179648 | tf_op jit(solution)/shard_map/all_to_all | solution.py:259
  92.3 1.3 pad.28.loading_ref
  93.6 0.9 pad.26.loading_ref
  96.6 15.7 %all-to-all-done.1 = bf16[128,2,1088]{2,1,0:T(2,128)(2,1)S(1)} async-done(((bf16[128,2,1088]{2,1,0:T(2,128)(2,1)}), bf16[128,2,1088]{2,1,0:T(2,128)(2,1)S(1)}, u32[]{:S(2)}, u32[]{:S(2)}) %all-to-all-start.1) | async-done | bytes 557088 | tf_op jit(solution)/shard_map/all_to_all | solution.py:259
  113.0 0.9 copy.40
  113.8 5.2 %prepare.1 = (bf16[264,3072]{1,0:T(8,128)(2,1)}, f32[3,88,2048]{2,1,0:T(8,128)}, f32[88,2048]{1,0:T(8,128)}) custom-call(bf16[88,128]{1,0:T(8,128)(2,1)} %get-tuple-element.21.pick_ref, f32[88,128]{1,0:T(8,128)} %get-tuple-element.22.unit_ref, bf16[128,2176]{1,0:T(8,128)(2,1)} %bitcast.26, bf16[3,128,2048]{2,1,0:T(8,128)(2,1)} %pad.28.loading_ref, ...), custom_call_target="tpu_custom_call" | custom-call | tf_op jit(solution)/shard_map/prepare/pallas_call | solution.py:286
  119.0 17.1 %solve.1 = (f32[3,81,2048]{2,1,0:T(8,128)}, f32[88,128]{1,0:T(8,128)}, f32[128,128]{1,0:T(8,128)}) custom-call(s32[1]{0:T(128)} %bitcast.side_ref, bf16[128,88]{1,0:T(8,128)(2,1)} %fusion.8.pick_ref, bf16[128,2048]{1,0:T(8,128)(2,1)} %pad.26.loading_ref, s32[81,1]{1,0:T(8,128)} %copy.33.occupied_ref, bf16[264,3072]{1,0:T(8,128)(2,1)} %get-tuple-element.13.press_hbm, ...), custom_call_target="tpu_custom_call" | custom-call | tf_op jit(solution)/shard_map/solve/pallas_call | solution.py:299
  136.1 7.3 %all-to-all-start.2 = ((f32[128,1,128]{2,1,0:T(1,128)}), f32[128,1,128]{2,1,0:T(1,128)S(1)}, u32[]{:S(2)}, u32[]{:S(2)}) async-start(f32[128,1,128]{2,1,0:T(1,128)} %bitcast.32), calls=%async_computation.2 | async-start | bytes 131072 | tf_op jit(solution)/shard_map/all_to_all | solution.py:327
  143.5 10.9 %all-to-all-done.2 = f32[128,1,128]{2,1,0:T(1,128)S(1)} async-done(((f32[128,1,128]{2,1,0:T(1,128)}), f32[128,1,128]{2,1,0:T(1,128)S(1)}, u32[]{:S(2)}, u32[]{:S(2)}) %all-to-all-start.2) | async-done | bytes 65568 | tf_op jit(solution)/shard_map/all_to_all | solution.py:327
  154.4 3.4 %collective-permute-start.1 = (f32[128,128]{1,0:T(8,128)S(1)}, f32[128,128]{1,0:T(8,128)S(1)}, u32[]{:S(2)}, u32[]{:S(2)}) collective-permute-start(f32[128,128]{1,0:T(8,128)S(1)} %bitcast.30), channel_id=1, source_target_pairs={{0,1},{1,2},{2,3},{3,4},{4,5},{5,6},{6,7},{7,8},{8,9},{9,10},{10,1... | collective-permute-start | bytes 196616 | tf_op jit(solution)/shard_map/ppermute | solution.py:220
  158.3 3.4 %collective-permute-start.2 = (f32[8,108]{1,0:T(8,128)S(1)}, f32[8,108]{1,0:T(8,128)S(1)}, u32[]{:S(2)}, u32[]{:S(2)}) collective-permute-start(f32[8,108]{1,0:T(8,128)S(1)} %concatenate.11.own_data_ref), channel_id=1, source_target_pairs={{0,1},{1,2},{2,3},{3,4},{4,5},{5,6},{6,7},{7,8},{8,9},{9,10},{10,1... | collective-permute-start | bytes 10376 | tf_op jit(solution)/shard_map/ppermute | solution.py:220
  161.6 0.8 slice.7
  163.2 4.2 %collective-permute-done.2.behind_data_ref = f32[8,108]{1,0:T(8,128)S(1)} collective-permute-done((f32[8,108]{1,0:T(8,128)S(1)}, f32[8,108]{1,0:T(8,128)S(1)}, u32[]{:S(2)}, u32[]{:S(2)}) %collective-permute-start.2) | collective-permute-done | bytes 3488 | tf_op jit(solution)/shard_map/ppermute | solution.py:220
  168.6 2.1 %corners.1 = (f32[3,128]{1,0:T(4,128)}, f32[9,128]{1,0:T(8,128)}) custom-call(f32[128,128]{1,0:T(8,128)} %bitcast.31, f32[128,128]{1,0:T(8,128)} %copy-done.1, f32[48,1]{1,0:T(8,128)} %reshape.75.fixed_ref, f32[8,108]{1,0:T(8,128)} %copy-done.2, f32[8,108]{1,0:T(8,128)} %copy-done.4), custom_call_target="tpu_custom_call" | custom-call | tf_op jit(solution)/shard_map/corners/pallas_call | solution.py:330
  (47 shorter events, 5.7 us)
Async XLA Ops:
  7.2 66.0 %all-gather.2.cloned.1.call-start = ((), (), s32[]{:S(2)}) async-start(), calls=%async_computation.3 | async-start | bytes 2949120 | tf_op jit(solution)/shard_map/all_gather | solution.py:235
  73.2 45.8 %collective-permute-start = (bf16[1024,1280]{1,0:T(8,128)(2,1)}, bf16[1024,1280]{1,0:T(8,128)(2,1)}, u32[]{:S(2)}, u32[]{:S(2)}) collective-permute-start(bf16[1024,1280]{1,0:T(8,128)(2,1)} %all-gather.2.cloned.1.call-done), channel_id=1, source_target_pairs={{0,4},{4,0},{1,5},{5,1},{2,6},{6,2},{3,7},{7,3},{8,12},{12,8},{9,1... | collective-permute-start | bytes 7864328 | tf_op jit(solution)/shard_map/ppermute | solution.py:236
  79.5 14.9 %copy-start.8 = (s32[81]{0:T(128)S(1)}, s32[81]{0:T(128)}, u32[]{:S(2)}) copy-start(s32[81]{0:T(128)} %param.17) | copy-start | bytes 976
  80.9 31.4 %all-to-all-start.1 = ((bf16[128,2,1088]{2,1,0:T(2,128)(2,1)}), bf16[128,2,1088]{2,1,0:T(2,128)(2,1)S(1)}, u32[]{:S(2)}, u32[]{:S(2)}) async-start(bf16[128,2,1088]{2,1,0:T(2,128)(2,1)} %reshape.76), calls=%async_computation.1 | async-start | bytes 1179648 | tf_op jit(solution)/shard_map/all_to_all | solution.py:259
  119.0 38.8 %copy-start.5 = (s32[4,27]{1,0:T(4,128)S(1)}, s32[4,27]{1,0:T(4,128)}, u32[]{:S(2)}) copy-start(s32[4,27]{1,0:T(4,128)} %param.15) | copy-start | bytes 1300
  119.0 38.8 %copy-start.6 = (s32[27]{0:T(128)S(1)}, s32[27]{0:T(128)}, u32[]{:S(2)}) copy-start(s32[27]{0:T(128)} %param.16) | copy-start | bytes 328
  119.0 38.9 %copy-start.3 = (f32[12,27]{1,0:T(8,128)S(1)}, f32[12,27]{1,0:T(8,128)}, u32[]{:S(2)}) copy-start(f32[12,27]{1,0:T(8,128)} %param.13) | copy-start | bytes 3892
  119.0 39.1 %copy-start.7 = (f32[27]{0:T(128)S(1)}, f32[27]{0:T(128)}, u32[]{:S(2)}) copy-start(f32[27]{0:T(128)} %param.14) | copy-start | bytes 328
  136.1 18.3 %all-to-all-start.2 = ((f32[128,1,128]{2,1,0:T(1,128)}), f32[128,1,128]{2,1,0:T(1,128)S(1)}, u32[]{:S(2)}, u32[]{:S(2)}) async-start(f32[128,1,128]{2,1,0:T(1,128)} %bitcast.32), calls=%async_computation.2 | async-start | bytes 131072 | tf_op jit(solution)/shard_map/all_to_all | solution.py:327
  154.4 13.0 %copy-start = (f32[128,1,128]{2,1,0:T(1,128)}, f32[128,1,128]{2,1,0:T(1,128)S(1)}, u32[]{:S(2)}) copy-start(f32[128,1,128]{2,1,0:T(1,128)S(1)} %all-to-all-done.2) | copy-start | bytes 196612
  154.4 13.0 %collective-permute-start.1 = (f32[128,128]{1,0:T(8,128)S(1)}, f32[128,128]{1,0:T(8,128)S(1)}, u32[]{:S(2)}, u32[]{:S(2)}) collective-permute-start(f32[128,128]{1,0:T(8,128)S(1)} %bitcast.30), channel_id=1, source_target_pairs={{0,1},{1,2},{2,3},{3,4},{4,5},{5,6},{6,7},{7,8},{8,9},{9,10},{10,1... | collective-permute-start | bytes 196616 | tf_op jit(solution)/shard_map/ppermute | solution.py:220
  158.2 9.2 %copy-start.2 = (f32[8,108]{1,0:T(8,128)}, f32[8,108]{1,0:T(8,128)S(1)}, u32[]{:S(2)}) copy-start(f32[8,108]{1,0:T(8,128)S(1)} %concatenate.11.own_data_ref) | copy-start | bytes 10372
  158.3 9.1 %collective-permute-start.2 = (f32[8,108]{1,0:T(8,128)S(1)}, f32[8,108]{1,0:T(8,128)S(1)}, u32[]{:S(2)}, u32[]{:S(2)}) collective-permute-start(f32[8,108]{1,0:T(8,128)S(1)} %concatenate.11.own_data_ref), channel_id=1, source_target_pairs={{0,1},{1,2},{2,3},{3,4},{4,5},{5,6},{6,7},{7,8},{8,9},{9,10},{10,1... | collective-permute-start | bytes 10376 | tf_op jit(solution)/shard_map/ppermute | solution.py:220
  167.4 0.6 copy-start.4
  168.0 0.6 copy-start.1
Sparse Core Ops, SparseCore 0:
  29.3 43.8 all-gather.1

commit v2 on v1

--- a/solution.py
+++ b/solution.py
@@ -233,9 +233,13 @@
         jnp.broadcast_to(half[None], (count,) + half.shape), "y", split_axis=0, concat_axis=0, tiled=True
     )
     plane = lax.all_gather(line.reshape(count * rows, SENT * SLICE), "z", axis=0, tiled=True)
+    return line, plane
+
+
+def swap_cores(plane, rows):
     other = lax.ppermute(plane, "core", [(0, 1), (1, 0)])
-    shape = (BLOCKS, count, rows, SENT * SLICE)
-    return line, plane.reshape(shape), other.reshape(shape)
+    shape = (BLOCKS, plane.shape[0] // (BLOCKS * rows), rows, SENT * SLICE)
+    return plane.reshape(shape), other.reshape(shape)
 
 
 def body(
@@ -249,7 +253,7 @@
     nodes = compliance.shape[1]
     rows = round_up(cap + COMPS, 8)
 
-    line, mine, other = spread_network(compliance)
+    line, plane = spread_network(compliance)
 
     worker_ids = jnp.arange(workers)
     send_pick = (worker_ids[:, None] == rve_worker[None, :]).astype(bf16)
@@ -293,6 +297,10 @@
         scratch_shapes=[pltpu.VMEM((rows, SLICE), f32)],
         name="prepare",
     )(slot_pick, unit, arrived, loading_wide, states)
+    plane, press, corner_data, behind_data, loading_sums, slot_give, occupied_rows = lax.optimization_barrier(
+        (plane, press, corner_data, behind_data, loading_sums, slot_pick.T, occupied.astype(jnp.int32)[:, None])
+    )
+    mine, other = swap_cores(plane, compliance.shape[0])
 
     vmem = pl.BlockSpec(memory_space=pltpu.VMEM)
     hbm = pl.BlockSpec(memory_space=pl.ANY)
@@ -319,8 +327,8 @@
         ],
         name="solve",
     )(
-        lax.axis_index("core")[None].astype(jnp.int32), slot_pick.T, loading_sums,
-        occupied.astype(jnp.int32)[:, None], press, forcing, fiber, states, mine, other,
+        lax.axis_index("core")[None].astype(jnp.int32), slot_give, loading_sums,
+        occupied_rows, press, forcing, fiber, states, mine, other,
     )
     new_table = jnp.transpose(table, (1, 0, 2))
 

time: 178 us -> 154 us (0.87)
  waiting for transfers between devices: 74.9 us -> 31.9 us
  blocking collectives: 20.3 us -> 43.2 us
  starting transfers between devices: 27.3 us -> 20.1 us
    all_gather x1, waiting for transfers between devices: 44 us -> 6.34 us  [spread_network(): lax.all_gather(line.reshape(count * rows, SENT * SLICE), 'z', axis=0, til...]
    all_to_all x0 -> x1, blocking collectives: none -> 22.9 us  [body(): lax.all_to_all(backward, RVE, split_axis=0, concat_axis=0, tiled=True)]
    all_to_all x1 -> x0, waiting for transfers between devices: 10.9 us -> none  [body(): lax.all_to_all(backward, RVE, split_axis=0, concat_axis=0, tiled=True)]
    all_to_all x1 -> x0, starting transfers between devices: 7.35 us -> none  [body(): lax.all_to_all(backward, RVE, split_axis=0, concat_axis=0, tiled=True)]
    ppermute x1, waiting for transfers between devices: 0.01 us -> 4.18 us  [swap_cores(): other = lax.ppermute(plane, 'core', [(0, 1), (1, 0)])]
    unnamed x23 -> x19, local copies, waits for them, and re-layouts: 5.86 us -> 5.88 us
  transfers between devices with their start and end apart: 6 -> 5, of which waited for: 4 -> 4; matrix products, arithmetic and copies ran while one was open for 8% -> 10% of each run, Pallas kernels for 3% -> 3%
where the time goes in v2:
time: 154 us; the launch traced here: 153 us
  blocking collectives  43.2 us (28%)
  waiting for transfers between devices  31.9 us (21%)
  Pallas kernels  24.5 us (16%)
  starting transfers between devices  20.1 us (13%)
  between operations  14.2 us (9%)
  local copies, waits for them, and re-layouts  13.4 us (9%)
  other arithmetic  4.55 us (3%)
    all_to_all x1, blocking collectives, body(): lax.all_to_all(backward, RVE, split_axis=0, concat_axis=0, tiled=True)  22.9 us
    all_to_all x1, blocking collectives, spread_network(): lax.all_to_all(jnp.broadcast_to(half[None], (count,) + half.shape), 'y',...  20.3 us
    pallas_call x1, Pallas kernels, body(): pl.pallas_call(solve_kernel, out_shape=(jax.ShapeDtypeStruct((3, cap, nod...  17.1 us
    all_to_all x1, waiting for transfers between devices, body(): lax.all_to_all(outgoing, RVE, split_axis=0, concat_axis=0, tiled=True)  16.5 us
    all_to_all x1, starting transfers between devices, body(): lax.all_to_all(outgoing, RVE, split_axis=0, concat_axis=0, tiled=True)  11.3 us
    ppermute x2, starting transfers between devices, from_behind(): return lax.ppermute(block, axis, route)  6.76 us
    all_gather x1, waiting for transfers between devices, spread_network(): lax.all_gather(line.reshape(count * rows, SENT * SLICE), 'z', axis=0, til...  6.34 us
    unnamed x19, local copies, waits for them, and re-layouts  5.88 us
  transfers between devices with their start and end apart: 5, of which 4 were waited for; matrix products, arithmetic and copies ran while one was open for 10% of the time, Pallas kernels for 3%

profile of v2, /device:TPU:64, one launch (start us, length us, event | category | flops | bytes accessed | tf_op | source)
XLA Modules:
  0.0 153.1 jit_solution(2350981921508868853)
XLA Ops:
  7.2 0.8 slice.6
  8.0 0.8 fusion.11
  8.8 20.3 %all_to_all.27 = bf16[8,16,1280]{2,1,0:T(8,128)(2,1)} all-to-all(bf16[8,16,1280]{2,1,0:T(8,128)(2,1)S(1)} %broadcast_in_dim.14), channel_id=1, replica_groups=mesh['z'=8,'y'=8,'core'=2,'blk'=4] {'y'}, dimensions={0} | all-to-all | bytes 655360 | tf_op jit(solution)/shard_map/all_to_all | solution.py:232
  32.3 3.4 %collective-permute-start = (f32[8,108]{1,0:T(8,128)S(1)}, f32[8,108]{1,0:T(8,128)S(1)}, u32[]{:S(2)}, u32[]{:S(2)}) collective-permute-start(f32[8,108]{1,0:T(8,128)S(1)} %concatenate.11.own_data_ref), channel_id=1, source_target_pairs={{0,1},{1,2},{2,3},{3,4},{4,5},{5,6},{6,7},{7,8},{8,9},{9,10},{10,1... | collective-permute-start | bytes 10376 | tf_op jit(solution)/shard_map/ppermute | solution.py:220
  35.7 0.8 copy.30
  36.5 1.2 fusion.2
  38.2 1.0 reduce
  39.2 1.4 reshape.76
  40.6 11.3 %all-to-all-start.1 = ((bf16[128,2,1088]{2,1,0:T(2,128)(2,1)}), bf16[128,2,1088]{2,1,0:T(2,128)(2,1)S(1)}, u32[]{:S(2)}, u32[]{:S(2)}) async-start(bf16[128,2,1088]{2,1,0:T(2,128)(2,1)} %reshape.76), calls=%async_computation.1 | async-start | bytes 1179648 | tf_op jit(solution)/shard_map/all_to_all | solution.py:263
  53.4 1.3 pad.26.loading_ref
  54.7 0.8 pad.28.loading_ref
  55.5 16.5 %all-to-all-done.1 = bf16[128,2,1088]{2,1,0:T(2,128)(2,1)S(1)} async-done(((bf16[128,2,1088]{2,1,0:T(2,128)(2,1)}), bf16[128,2,1088]{2,1,0:T(2,128)(2,1)S(1)}, u32[]{:S(2)}, u32[]{:S(2)}) %all-to-all-start.1) | async-done | bytes 557088 | tf_op jit(solution)/shard_map/all_to_all | solution.py:263
  72.7 0.9 copy.40
  73.6 5.3 %prepare.1 = (bf16[264,3072]{1,0:T(8,128)(2,1)}, f32[3,88,2048]{2,1,0:T(8,128)}, f32[88,2048]{1,0:T(8,128)}) custom-call(bf16[88,128]{1,0:T(8,128)(2,1)} %get-tuple-element.35.pick_ref, f32[88,128]{1,0:T(8,128)} %get-tuple-element.36.unit_ref, bf16[128,2176]{1,0:T(8,128)(2,1)} %bitcast.27, bf16[3,128,2048]{2,1,0:T(8,128)(2,1)} %pad.26.loading_ref, ...), custom_call_target="tpu_custom_call" | custom-call | tf_op jit(solution)/shard_map/prepare/pallas_call | solution.py:290
  78.8 6.3 %all-gather.2.cloned.1.call-done = bf16[1024,1280]{1,0:T(8,128)(2,1)} async-done(((bf16[128,1280]{1,0:T(8,128)(2,1)}), bf16[1024,1280]{1,0:T(8,128)(2,1)}) %all-gather.2.cloned.1.call-update) | async-done | bytes 2621456 | tf_op jit(solution)/shard_map/all_gather | solution.py:235
  85.2 2.1 %collective-permute-start.1 = (bf16[1024,1280]{1,0:T(8,128)(2,1)}, bf16[1024,1280]{1,0:T(8,128)(2,1)S(1)}, u32[]{:S(2)}, u32[]{:S(2)}) collective-permute-start(bf16[1024,1280]{1,0:T(8,128)(2,1)} %all-gather.2.cloned.1.call-done), channel_id=1, source_target_pairs={{0,4},{4,0},{1,5},{5,1},{2,6},{6,2},{3,7},{7,3},{8,12},{12,8},{9,1... | collective-permute-start | bytes 7864328 | tf_op jit(solution)/shard_map/ppermute | solution.py:240
  88.0 4.2 %collective-permute-done.1 = bf16[1024,1280]{1,0:T(8,128)(2,1)S(1)} collective-permute-done((bf16[1024,1280]{1,0:T(8,128)(2,1)}, bf16[1024,1280]{1,0:T(8,128)(2,1)S(1)}, u32[]{:S(2)}, u32[]{:S(2)}) %collective-permute-start.1) | collective-permute-done | bytes 2621472 | tf_op jit(solution)/shard_map/ppermute | solution.py:240
  92.2 1.5 copy-done
  93.7 17.1 %solve.1 = (f32[3,81,2048]{2,1,0:T(8,128)}, f32[88,128]{1,0:T(8,128)}, f32[128,128]{1,0:T(8,128)}) custom-call(s32[1]{0:T(128)} %bitcast.side_ref, bf16[128,88]{1,0:T(8,128)(2,1)} %fusion.8.pick_ref, bf16[128,2048]{1,0:T(8,128)(2,1)} %pad.28.loading_ref, s32[81,1]{1,0:T(8,128)} %copy.34.occupied_ref, bf16[264,3072]{1,0:T(8,128)(2,1)} %get-tuple-element.24.press_hbm, ...), custom_call_target="tpu_custom_call" | custom-call | tf_op jit(solution)/shard_map/solve/pallas_call | solution.py:307
  110.8 22.9 %all_to_all.28 = f32[128,1,128]{2,1,0:T(1,128)S(1)} all-to-all(f32[128,1,128]{2,1,0:T(1,128)} %bitcast.33), channel_id=1, replica_groups=mesh['z'=8,'y'=8,'core'=2,'blk'=4] {'z','y','core'}, dimensions={0} | all-to-all | bytes 131072 | tf_op jit(solution)/shard_map/all_to_all | solution.py:335
  133.7 3.4 %collective-permute-start.2 = (f32[128,128]{1,0:T(8,128)S(1)}, f32[128,128]{1,0:T(8,128)S(1)}, u32[]{:S(2)}, u32[]{:S(2)}) collective-permute-start(f32[128,128]{1,0:T(8,128)S(1)} %bitcast.31), channel_id=1, source_target_pairs={{0,1},{1,2},{2,3},{3,4},{4,5},{5,6},{6,7},{7,8},{8,9},{9,10},{10,1... | collective-permute-start | bytes 196616 | tf_op jit(solution)/shard_map/ppermute | solution.py:220
  137.1 0.8 slice.7
  138.6 4.9 %collective-permute-done.2.behind_ref = f32[128,128]{1,0:T(8,128)S(1)} collective-permute-done((f32[128,128]{1,0:T(8,128)S(1)}, f32[128,128]{1,0:T(8,128)S(1)}, u32[]{:S(2)}, u32[]{:S(2)}) %collective-permute-start.2) | collective-permute-done | bytes 65568 | tf_op jit(solution)/shard_map/ppermute | solution.py:220
  144.1 2.1 %corners.1 = (f32[3,128]{1,0:T(4,128)}, f32[9,128]{1,0:T(8,128)}) custom-call(f32[128,128]{1,0:T(8,128)} %bitcast.32, f32[128,128]{1,0:T(8,128)} %copy-done.3, f32[48,1]{1,0:T(8,128)} %reshape.75.fixed_ref, f32[8,108]{1,0:T(8,128)} %copy-done.4, f32[8,108]{1,0:T(8,128)} %copy-done.5), custom_call_target="tpu_custom_call" | custom-call | tf_op jit(solution)/shard_map/corners/pallas_call | solution.py:338
  (42 shorter events, 7.9 us)
Async XLA Ops:
  7.2 78.0 %all-gather.2.cloned.1.call-start = ((), (), s32[]{:S(2)}) async-start(), calls=%async_computation.3 | async-start | bytes 2949120 | tf_op jit(solution)/shard_map/all_gather | solution.py:235
  29.1 22.7 %copy-start.6 = (s32[81]{0:T(128)S(1)}, s32[81]{0:T(128)}, u32[]{:S(2)}) copy-start(s32[81]{0:T(128)} %param.17) | copy-start | bytes 976
  29.2 22.7 %copy-start.2 = (bf16[6,3,2048]{2,1,0:T(4,128)(2,1)S(1)}, bf16[6,3,2048]{2,1,0:T(4,128)(2,1)}, u32[]{:S(2)}) copy-start(bf16[6,3,2048]{2,1,0:T(4,128)(2,1)} %param.19) | copy-start | bytes 221188
  32.3 19.7 %copy-start.4 = (f32[8,108]{1,0:T(8,128)}, f32[8,108]{1,0:T(8,128)S(1)}, u32[]{:S(2)}) copy-start(f32[8,108]{1,0:T(8,128)S(1)} %concatenate.11.own_data_ref) | copy-start | bytes 10372
  32.3 46.5 %collective-permute-start = (f32[8,108]{1,0:T(8,128)S(1)}, f32[8,108]{1,0:T(8,128)S(1)}, u32[]{:S(2)}, u32[]{:S(2)}) collective-permute-start(f32[8,108]{1,0:T(8,128)S(1)} %concatenate.11.own_data_ref), channel_id=1, source_target_pairs={{0,1},{1,2},{2,3},{3,4},{4,5},{5,6},{6,7},{7,8},{8,9},{9,10},{10,1... | collective-permute-start | bytes 10376 | tf_op jit(solution)/shard_map/ppermute | solution.py:220
  40.6 31.4 %all-to-all-start.1 = ((bf16[128,2,1088]{2,1,0:T(2,128)(2,1)}), bf16[128,2,1088]{2,1,0:T(2,128)(2,1)S(1)}, u32[]{:S(2)}, u32[]{:S(2)}) async-start(bf16[128,2,1088]{2,1,0:T(2,128)(2,1)} %reshape.76), calls=%async_computation.1 | async-start | bytes 1179648 | tf_op jit(solution)/shard_map/all_to_all | solution.py:263
  78.8 32.0 %copy-start.5 = (f32[8,108]{1,0:T(8,128)}, f32[8,108]{1,0:T(8,128)S(1)}, u32[]{:S(2)}) copy-start(f32[8,108]{1,0:T(8,128)S(1)} %collective-permute-done.behind_data_ref) | copy-start | bytes 10372
  85.2 7.0 %collective-permute-start.1 = (bf16[1024,1280]{1,0:T(8,128)(2,1)}, bf16[1024,1280]{1,0:T(8,128)(2,1)S(1)}, u32[]{:S(2)}, u32[]{:S(2)}) collective-permute-start(bf16[1024,1280]{1,0:T(8,128)(2,1)} %all-gather.2.cloned.1.call-done), channel_id=1, source_target_pairs={{0,4},{4,0},{1,5},{5,1},{2,6},{6,2},{3,7},{7,3},{8,12},{12,8},{9,1... | collective-permute-start | bytes 7864328 | tf_op jit(solution)/shard_map/ppermute | solution.py:240
  92.2 1.5 copy-start
  133.7 9.8 %copy-start.1 = (f32[128,1,128]{2,1,0:T(1,128)}, f32[128,1,128]{2,1,0:T(1,128)S(1)}, u32[]{:S(2)}) copy-start(f32[128,1,128]{2,1,0:T(1,128)S(1)} %all_to_all.28) | copy-start | bytes 196612
  133.7 9.8 %collective-permute-start.2 = (f32[128,128]{1,0:T(8,128)S(1)}, f32[128,128]{1,0:T(8,128)S(1)}, u32[]{:S(2)}, u32[]{:S(2)}) collective-permute-start(f32[128,128]{1,0:T(8,128)S(1)} %bitcast.31), channel_id=1, source_target_pairs={{0,1},{1,2},{2,3},{3,4},{4,5},{5,6},{6,7},{7,8},{8,9},{9,10},{10,1... | collective-permute-start | bytes 196616 | tf_op jit(solution)/shard_map/ppermute | solution.py:220
  143.5 0.6 copy-start.3
Sparse Core Ops, SparseCore 0:
  29.3 55.8 all-gather.1

commit v3 on v1

--- a/solution.py
+++ b/solution.py
@@ -13,6 +13,7 @@
 SLICE = 256
 BLOCKS = 8
 SENT = 5
+PARTS = 2
 
 highest = lax.Precision.HIGHEST
 f32 = jnp.float32
@@ -60,16 +61,21 @@
 
 
 def solve_kernel(
-    side_ref, pick_ref, loading_ref, occupied_ref, press_hbm, forcing_hbm, fiber_hbm, state_hbm,
-    mine_hbm, other_hbm, table_hbm, result_ref, back_ref,
-    network, pressure, forcing, fiber, table, damp_sum, stress_sum, net_sems, in_sems, out_sems,
+    side_ref, pick_ref, loading_ref, occupied_ref, press_hbm, forcing_hbm, fiber_hbm, state_hbm, *refs,
 ):
+    shares = refs[: 2 * PARTS]
+    (
+        table_hbm, result_ref, back_ref, network, pressure, forcing, fiber, table, damp_sum, stress_sum,
+        net_sems, in_sems, out_sems,
+    ) = refs[2 * PARTS :]
     rows = fiber.shape[0]
     nodes = fiber.shape[1]
     cap = table.shape[1]
-
-    def fetch(i, side, source, k):
-        return pltpu.make_async_copy(source.at[i], network.at[i, :, side], net_sems.at[i, k])
+    lines = network.shape[1] // PARTS
+
+    def fetch(i, side, k):
+        place = network.at[i, pl.ds(k % PARTS * lines, lines), side]
+        return pltpu.make_async_copy(shares[k].at[i], place, net_sems.at[i, k])
 
     inputs = (
         pltpu.make_async_copy(press_hbm, pressure.at[0], in_sems.at[0]),
@@ -84,15 +90,15 @@
         @pl.when(side_ref[0] == side)
         def _():
             for i in arrival:
-                fetch(i, side, mine_hbm, 0).start()
-                fetch(i, 1 - side, other_hbm, 1).start()
+                for k in range(2 * PARTS):
+                    fetch(i, side if k < PARTS else 1 - side, k).start()
 
     for copy in inputs[1:]:
         copy.start()
 
     def wait_network(i):
-        fetch(i, 0, mine_hbm, 0).wait()
-        fetch(i, 0, other_hbm, 1).wait()
+        for k in range(2 * PARTS):
+            fetch(i, 0, k).wait()
 
     def net(i, start, blocks):
         cols = pl.ds(start * SLICE, blocks * SLICE)
@@ -232,10 +238,18 @@
     line = lax.all_to_all(
         jnp.broadcast_to(half[None], (count,) + half.shape), "y", split_axis=0, concat_axis=0, tiled=True
     )
-    plane = lax.all_gather(line.reshape(count * rows, SENT * SLICE), "z", axis=0, tiled=True)
-    other = lax.ppermute(plane, "core", [(0, 1), (1, 0)])
-    shape = (BLOCKS, count, rows, SENT * SLICE)
-    return line, plane.reshape(shape), other.reshape(shape)
+    line = line.reshape(count * rows, SENT * SLICE)
+    part = count * rows // PARTS
+    planes = [
+        lax.all_gather(line[p * part : (p + 1) * part], "z", axis=0, tiled=True) for p in range(PARTS)
+    ]
+    return line, planes
+
+
+def swap_cores(planes, rows):
+    others = [lax.ppermute(plane, "core", [(0, 1), (1, 0)]) for plane in planes]
+    shape = (BLOCKS, planes[0].shape[0] // (BLOCKS * rows), rows, SENT * SLICE)
+    return [block.reshape(shape) for block in planes + others]
 
 
 def body(
@@ -249,7 +263,7 @@
     nodes = compliance.shape[1]
     rows = round_up(cap + COMPS, 8)
 
-    line, mine, other = spread_network(compliance)
+    line, planes = spread_network(compliance)
 
     worker_ids = jnp.arange(workers)
     send_pick = (worker_ids[:, None] == rve_worker[None, :]).astype(bf16)
@@ -257,19 +271,6 @@
     outgoing = jnp.dot(send_pick, element_rows)
     outgoing = lax.optimization_barrier((outgoing, line))[0]
     arrived = lax.all_to_all(outgoing, RVE, split_axis=0, concat_axis=0, tiled=True)
-
-    device_rank = lax.axis_index(ALL)
-    corner_data = jnp.concatenate(
-        [
-            jnp.transpose(gradients.reshape(4, 3, elems), (1, 0, 2)).reshape(3, 4 * elems),
-            jnp.tile(volume, 4)[None, :],
-            (corners - device_rank * NODE_DEV).reshape(1, 4 * elems).astype(f32),
-            jnp.tile(rve_worker, 4)[None, :].astype(f32),
-            jnp.zeros((2, 4 * elems), f32),
-        ],
-        axis=0,
-    )
-    behind_data = from_behind(corner_data, ALL, 1)
 
     occupied = slot_element >= 0
     home = jnp.where(occupied, slot_element // (elems * columns), -1)
@@ -293,9 +294,29 @@
         scratch_shapes=[pltpu.VMEM((rows, SLICE), f32)],
         name="prepare",
     )(slot_pick, unit, arrived, loading_wide, states)
+    gradients, volume, corners, rve_worker = lax.optimization_barrier(
+        (press, gradients, volume, corners, rve_worker)
+    )[1:]
+    device_rank = lax.axis_index(ALL)
+    corner_data = jnp.concatenate(
+        [
+            jnp.transpose(gradients.reshape(4, 3, elems), (1, 0, 2)).reshape(3, 4 * elems),
+            jnp.tile(volume, 4)[None, :],
+            (corners - device_rank * NODE_DEV).reshape(1, 4 * elems).astype(f32),
+            jnp.tile(rve_worker, 4)[None, :].astype(f32),
+            jnp.zeros((2, 4 * elems), f32),
+        ],
+        axis=0,
+    )
+    behind_data = from_behind(corner_data, ALL, 1)
+
+    planes, press, corner_data, behind_data, loading_sums, slot_give, occupied_rows = lax.optimization_barrier(
+        (planes, press, corner_data, behind_data, loading_sums, slot_pick.T, occupied.astype(jnp.int32)[:, None])
+    )
+    shares = swap_cores(planes, compliance.shape[0])
 
     vmem = pl.BlockSpec(memory_space=pltpu.VMEM)
-    hbm = pl.BlockSpec(memory_space=pl.ANY)
+    hbm = pl.BlockSpec(memory_space=pltpu.HBM)
     table, result, backward = pl.pallas_call(
         solve_kernel,
         out_shape=(
@@ -303,30 +324,31 @@
             jax.ShapeDtypeStruct((rows, 128), f32),
             jax.ShapeDtypeStruct((workers, 128), f32),
         ),
-        in_specs=[pl.BlockSpec(memory_space=pltpu.SMEM)] + [vmem] * 3 + [hbm] * 6,
+        in_specs=[pl.BlockSpec(memory_space=pltpu.SMEM)] + [vmem] * 3 + [hbm] * (4 + 2 * PARTS),
         out_specs=(hbm, vmem, vmem),
         scratch_shapes=[
-            pltpu.VMEM((BLOCKS, mine.shape[1], 2, mine.shape[2], SENT * SLICE), bf16),
+            pltpu.VMEM((BLOCKS, PARTS * shares[0].shape[1], 2, shares[0].shape[2], SENT * SLICE), bf16),
             pltpu.VMEM((ITERS, 3 * rows, wide), bf16),
             pltpu.VMEM((3, rows, nodes), f32),
             pltpu.VMEM((rows, nodes), f32),
             pltpu.VMEM((3, cap, nodes), f32),
             pltpu.VMEM((3 * rows, 256), f32),
             pltpu.VMEM((3 * rows, 128), f32),
-            pltpu.SemaphoreType.DMA((BLOCKS, 2)),
+            pltpu.SemaphoreType.DMA((BLOCKS, 2 * PARTS)),
             pltpu.SemaphoreType.DMA((4,)),
             pltpu.SemaphoreType.DMA((BLOCKS,)),
         ],
         name="solve",
     )(
-        lax.axis_index("core")[None].astype(jnp.int32), slot_pick.T, loading_sums,
-        occupied.astype(jnp.int32)[:, None], press, forcing, fiber, states, mine, other,
+        lax.axis_index("core")[None].astype(jnp.int32), slot_give, loading_sums,
+        occupied_rows, press, forcing, fiber, states, *shares,
     )
     new_table = jnp.transpose(table, (1, 0, 2))
 
     returned = lax.all_to_all(backward, RVE, split_axis=0, concat_axis=0, tiled=True)
+    fixed = jnp.pad(result[cap : cap + COMPS, 8 * COMPS + 1 : 8 * COMPS + 1 + COMPS], ((0, 0), (1, 1)))
+    fixed, returned = lax.optimization_barrier((fixed.reshape(8 * COMPS, 1), returned))
     behind = from_behind(returned, ALL, 1)
-    fixed = jnp.pad(result[cap : cap + COMPS, 8 * COMPS + 1 : 8 * COMPS + 1 + COMPS], ((0, 0), (1, 1)))
     forces, blocks = pl.pallas_call(
         functools.partial(corner_kernel, scale=1.0 / (3 * nodes)),
         out_shape=(
@@ -334,8 +356,9 @@
             jax.ShapeDtypeStruct((9, NODE_DEV), f32),
         ),
         scratch_shapes=[pltpu.VMEM((2, 16, 4 * elems), f32)],
+        compiler_params=pltpu.CompilerParams(vmem_limit_bytes=8 << 20),
         name="corners",
-    )(returned, behind, fixed.reshape(8 * COMPS, 1), corner_data, behind_data)
+    )(returned, behind, fixed, corner_data, behind_data)
     return (new_table, forces, blocks)
 
 

time: 178 us -> 191 us (1.073)
  waiting for transfers between devices: 74.9 us -> 83.9 us
  starting transfers between devices: 27.3 us -> 34.2 us
    ppermute x2, waiting for transfers between devices: 4.24 us -> 11.2 us  [from_behind(): return lax.ppermute(block, axis, route)]
    all_to_all x1, starting transfers between devices: 7.35 us -> 11.6 us  [body(): lax.all_to_all(backward, RVE, split_axis=0, concat_axis=0, tiled=True)]
    ppermute x1 -> x2, starting transfers between devices: 1.91 us -> 4.49 us  [swap_cores(): others = [lax.ppermute(plane, 'core', [(0, 1), (1, 0)]) for plane in planes]]
    ppermute x1 -> x2, waiting for transfers between devices: 0.01 us -> 1.95 us  [swap_cores(): others = [lax.ppermute(plane, 'core', [(0, 1), (1, 0)]) for plane in planes]]
    unnamed x23 -> x25, local copies, waits for them, and re-layouts: 5.86 us -> 4.27 us
    all_gather x1 -> x2, waiting for transfers between devices: 44 us -> 42.7 us  [spread_network(): lax.all_gather(line[p * part:(p + 1) * part], 'z', axis=0, tiled=True)]
  transfers between devices with their start and end apart: 6 -> 8, of which waited for: 4 -> 6; matrix products, arithmetic and copies ran while one was open for 8% -> 6% of each run, Pallas kernels for 3% -> 3%
where the time goes in v3:
time: 191 us
  waiting for transfers between devices  83.9 us (44%)
  starting transfers between devices  34.2 us (18%)
  Pallas kernels  23.8 us (12%)
  blocking collectives  20.2 us (11%)
  between operations  14.3 us (7%)
  local copies, waits for them, and re-layouts  10.6 us (6%)
  other arithmetic  3.2 us (2%)
    all_gather x2, waiting for transfers between devices, spread_network(): lax.all_gather(line[p * part:(p + 1) * part], 'z', axis=0, tiled=True)  42.7 us
    all_to_all x1, blocking collectives, spread_network(): lax.all_to_all(jnp.broadcast_to(half[None], (count,) + half.shape), 'y',...  20.2 us
    pallas_call x1, Pallas kernels, body(): pl.pallas_call(solve_kernel, out_shape=(jax.ShapeDtypeStruct((3, cap, nod...  17.4 us
    all_to_all x1, waiting for transfers between devices, body(): lax.all_to_all(outgoing, RVE, split_axis=0, concat_axis=0, tiled=True)  17.3 us
    all_to_all x1, starting transfers between devices, body(): lax.all_to_all(backward, RVE, split_axis=0, concat_axis=0, tiled=True)  11.6 us
    all_to_all x1, starting transfers between devices, body(): lax.all_to_all(outgoing, RVE, split_axis=0, concat_axis=0, tiled=True)  11.3 us
    ppermute x2, waiting for transfers between devices, from_behind(): return lax.ppermute(block, axis, route)  11.2 us
    all_to_all x1, waiting for transfers between devices, body(): lax.all_to_all(backward, RVE, split_axis=0, concat_axis=0, tiled=True)  9.98 us
  transfers between devices with their start and end apart: 8, of which 6 were waited for; matrix products, arithmetic and copies ran while one was open for 6% of the time, Pallas kernels for 3%

profile of v3, /device:TPU:64, one launch (start us, length us, event | category | flops | bytes accessed | tf_op | source)
XLA Modules:
  0.0 190.6 jit_solution(6302415684928813288)
XLA Ops:
  7.2 0.8 slice.18
  8.0 0.8 fusion.11
  8.9 20.2 %all_to_all.28 = bf16[8,16,1280]{2,1,0:T(8,128)(2,1)S(1)} all-to-all(bf16[8,16,1280]{2,1,0:T(8,128)(2,1)S(1)} %broadcast_in_dim.14), channel_id=1, replica_groups=mesh['z'=8,'y'=8,'core'=2,'blk'=4] {'y'}, dimensions={0} | all-to-all | bytes 655360 | tf_op jit(solution)/shard_map/all_to_all | solution.py:238
  31.5 1.0 reduce
  32.6 1.4 reshape.83
  34.0 11.3 %all-to-all-start.1 = ((bf16[128,2,1088]{2,1,0:T(2,128)(2,1)}), bf16[128,2,1088]{2,1,0:T(2,128)(2,1)S(1)}, u32[]{:S(2)}, u32[]{:S(2)}) async-start(bf16[128,2,1088]{2,1,0:T(2,128)(2,1)} %reshape.83), calls=%async_computation.1 | async-start | bytes 1179648 | tf_op jit(solution)/shard_map/all_to_all | solution.py:273
  45.4 1.3 pad.26.loading_ref
  48.1 17.3 %all-to-all-done.1 = bf16[128,2,1088]{2,1,0:T(2,128)(2,1)S(1)} async-done(((bf16[128,2,1088]{2,1,0:T(2,128)(2,1)}), bf16[128,2,1088]{2,1,0:T(2,128)(2,1)S(1)}, u32[]{:S(2)}, u32[]{:S(2)}) %all-to-all-start.1) | async-done | bytes 557088 | tf_op jit(solution)/shard_map/all_to_all | solution.py:273
  66.0 0.9 copy.40
  66.9 5.2 %prepare.1 = (bf16[264,3072]{1,0:T(8,128)(2,1)}, f32[3,88,2048]{2,1,0:T(8,128)}, f32[88,2048]{1,0:T(8,128)}) custom-call(bf16[88,128]{1,0:T(8,128)(2,1)} %get-tuple-element.49.pick_ref, f32[88,128]{1,0:T(8,128)} %get-tuple-element.50.unit_ref, bf16[128,2176]{1,0:T(8,128)(2,1)} %bitcast.30, bf16[3,128,2048]{2,1,0:T(8,128)(2,1)} %pad.26.loading_ref, ...), custom_call_target="tpu_custom_call" | custom-call | tf_op jit(solution)/shard_map/prepare/pallas_call | solution.py:287
  72.6 3.4 %collective-permute-start = (f32[8,108]{1,0:T(8,128)S(1)}, f32[8,108]{1,0:T(8,128)S(1)}, u32[]{:S(2)}, u32[]{:S(2)}) collective-permute-start(f32[8,108]{1,0:T(8,128)S(1)} %concatenate.11.own_data_ref), channel_id=1, source_target_pairs={{0,1},{1,2},{2,3},{3,4},{4,5},{5,6},{6,7},{7,8},{8,9},{9,10},{10,1... | collective-permute-start | bytes 10376 | tf_op jit(solution)/shard_map/ppermute | solution.py:226
  76.0 0.9 pad.28.loading_ref
  76.8 4.9 %collective-permute-done.behind_data_ref = f32[8,108]{1,0:T(8,128)S(1)} collective-permute-done((f32[8,108]{1,0:T(8,128)S(1)}, f32[8,108]{1,0:T(8,128)S(1)}, u32[]{:S(2)}, u32[]{:S(2)}) %collective-permute-start) | collective-permute-done | bytes 3488 | tf_op jit(solution)/shard_map/ppermute | solution.py:226
  81.7 42.7 %all-gather.5.cloned.1.call-done = bf16[512,1280]{1,0:T(8,128)(2,1)} async-done(((bf16[64,1280]{1,0:T(8,128)(2,1)}), bf16[512,1280]{1,0:T(8,128)(2,1)}) %all-gather.5.cloned.1.call-update) | async-done | bytes 1310736 | tf_op jit(solution)/shard_map/all_gather | solution.py:244
  124.5 1.9 %collective-permute-start.1 = (bf16[512,1280]{1,0:T(8,128)(2,1)}, bf16[512,1280]{1,0:T(8,128)(2,1)S(1)}, u32[]{:S(2)}, u32[]{:S(2)}) collective-permute-start(bf16[512,1280]{1,0:T(8,128)(2,1)} %all-gather.3.cloned.1.call-done), channel_id=1, source_target_pairs={{0,4},{4,0},{1,5},{5,1},{2,6},{6,2},{3,7},{7,3},{8,12},{12,8},{9,1... | collective-permute-start | bytes 3932168 | tf_op jit(solution)/shard_map/ppermute | solution.py:250
  126.4 2.6 %collective-permute-start.2 = (bf16[512,1280]{1,0:T(8,128)(2,1)}, bf16[512,1280]{1,0:T(8,128)(2,1)S(1)}, u32[]{:S(2)}, u32[]{:S(2)}) collective-permute-start(bf16[512,1280]{1,0:T(8,128)(2,1)} %all-gather.5.cloned.1.call-done), channel_id=1, source_target_pairs={{0,4},{4,0},{1,5},{5,1},{2,6},{6,2},{3,7},{7,3},{8,12},{12,8},{9,1... | collective-permute-start | bytes 3932168 | tf_op jit(solution)/shard_map/ppermute | solution.py:250
  129.7 1.9 %collective-permute-done.2 = bf16[512,1280]{1,0:T(8,128)(2,1)S(1)} collective-permute-done((bf16[512,1280]{1,0:T(8,128)(2,1)}, bf16[512,1280]{1,0:T(8,128)(2,1)S(1)}, u32[]{:S(2)}, u32[]{:S(2)}) %collective-permute-start.2) | collective-permute-done | bytes 1310752 | tf_op jit(solution)/shard_map/ppermute | solution.py:250
  131.6 1.1 copy-done.1
  132.8 17.4 %solve.1 = (f32[3,81,2048]{2,1,0:T(8,128)}, f32[88,128]{1,0:T(8,128)}, f32[128,128]{1,0:T(8,128)}) custom-call(s32[1]{0:T(128)} %bitcast.side_ref, bf16[128,88]{1,0:T(8,128)(2,1)} %fusion.8.pick_ref, bf16[128,2048]{1,0:T(8,128)(2,1)} %pad.28.loading_ref, s32[81,1]{1,0:T(8,128)} %copy.34.occupied_ref, bf16[264,3072]{1,0:T(8,128)(2,1)} %get-tuple-element.33.press_hbm, ...), custom_call_target="tpu_custom_call" | custom-call | tf_op jit(solution)/shard_map/solve/pallas_call | solution.py:320
  150.2 11.6 %all-to-all-start.2 = ((f32[128,1,128]{2,1,0:T(1,128)}), f32[128,1,128]{2,1,0:T(1,128)S(1)}, u32[]{:S(2)}, u32[]{:S(2)}) async-start(f32[128,1,128]{2,1,0:T(1,128)} %bitcast.39), calls=%async_computation.2 | async-start | bytes 131072 | tf_op jit(solution)/shard_map/all_to_all | solution.py:348
  162.7 10.0 %all-to-all-done.2 = f32[128,1,128]{2,1,0:T(1,128)S(1)} async-done(((f32[128,1,128]{2,1,0:T(1,128)}), f32[128,1,128]{2,1,0:T(1,128)S(1)}, u32[]{:S(2)}, u32[]{:S(2)}) %all-to-all-start.2) | async-done | bytes 65568 | tf_op jit(solution)/shard_map/all_to_all | solution.py:348
  172.7 3.4 %collective-permute-start.3 = (f32[128,128]{1,0:T(8,128)S(1)}, f32[128,128]{1,0:T(8,128)S(1)}, u32[]{:S(2)}, u32[]{:S(2)}) collective-permute-start(f32[128,128]{1,0:T(8,128)S(1)} %bitcast.25), channel_id=1, source_target_pairs={{0,1},{1,2},{2,3},{3,4},{4,5},{5,6},{6,7},{7,8},{8,9},{9,10},{10,1... | collective-permute-start | bytes 196616 | tf_op jit(solution)/shard_map/ppermute | solution.py:226
  176.2 6.3 %collective-permute-done.3.behind_ref = f32[128,128]{1,0:T(8,128)S(1)} collective-permute-done((f32[128,128]{1,0:T(8,128)S(1)}, f32[128,128]{1,0:T(8,128)S(1)}, u32[]{:S(2)}, u32[]{:S(2)}) %collective-permute-start.3) | collective-permute-done | bytes 65568 | tf_op jit(solution)/shard_map/ppermute | solution.py:226
  182.5 1.2 corners.1
  (56 shorter events, 6.7 us)
Async XLA Ops:
  7.2 23.4 %copy-start.5 = (bf16[27,6]{0,1:T(8,128)(2,1)S(1)}, bf16[27,6]{0,1:T(8,128)(2,1)}, u32[]{:S(2)}) copy-start(bf16[27,6]{0,1:T(8,128)(2,1)} %param.11) | copy-start | bytes 976
  7.2 23.5 %copy-start.7 = (s32[27]{0:T(128)S(1)}, s32[27]{0:T(128)}, u32[]{:S(2)}) copy-start(s32[27]{0:T(128)} %param.16) | copy-start | bytes 328
  7.2 23.5 %copy-start.2 = (bf16[27,2048]{1,0:T(8,128)(2,1)S(1)}, bf16[27,2048]{1,0:T(8,128)(2,1)}, u32[]{:S(2)}) copy-start(bf16[27,2048]{1,0:T(8,128)(2,1)} %param.12) | copy-start | bytes 331780
  7.2 74.5 %all-gather.3.cloned.1.call-start = ((), (), s32[]{:S(2)}) async-start(), calls=%async_computation.3 | async-start | bytes 1474560 | tf_op jit(solution)/shard_map/all_gather | solution.py:244
  29.8 94.6 %all-gather.5.cloned.1.call-start = ((), (), s32[]{:S(2)}) async-start(), calls=%async_computation.4 | async-start | bytes 1474560 | tf_op jit(solution)/shard_map/all_gather | solution.py:244
  31.5 13.7 %copy-start.3 = (bf16[6,3,2048]{2,1,0:T(4,128)(2,1)S(1)}, bf16[6,3,2048]{2,1,0:T(4,128)(2,1)}, u32[]{:S(2)}) copy-start(bf16[6,3,2048]{2,1,0:T(4,128)(2,1)} %param.19) | copy-start | bytes 221188
  31.5 13.8 %copy-start.9 = (s32[81]{0:T(128)S(1)}, s32[81]{0:T(128)}, u32[]{:S(2)}) copy-start(s32[81]{0:T(128)} %param.17) | copy-start | bytes 976
  34.0 31.4 %all-to-all-start.1 = ((bf16[128,2,1088]{2,1,0:T(2,128)(2,1)}), bf16[128,2,1088]{2,1,0:T(2,128)(2,1)S(1)}, u32[]{:S(2)}, u32[]{:S(2)}) async-start(bf16[128,2,1088]{2,1,0:T(2,128)(2,1)} %reshape.83), calls=%async_computation.1 | async-start | bytes 1179648 | tf_op jit(solution)/shard_map/all_to_all | solution.py:273
  66.9 5.3 %copy-start.6 = (s32[4,27]{1,0:T(4,128)S(1)}, s32[4,27]{1,0:T(4,128)}, u32[]{:S(2)}) copy-start(s32[4,27]{1,0:T(4,128)} %param.15) | copy-start | bytes 1300
  66.9 5.4 %copy-start.8 = (f32[27]{0:T(128)S(1)}, f32[27]{0:T(128)}, u32[]{:S(2)}) copy-start(f32[27]{0:T(128)} %param.14) | copy-start | bytes 328
  66.9 5.5 %copy-start.4 = (f32[12,27]{1,0:T(8,128)S(1)}, f32[12,27]{1,0:T(8,128)}, u32[]{:S(2)}) copy-start(f32[12,27]{1,0:T(8,128)} %param.13) | copy-start | bytes 3892
  72.6 9.1 %collective-permute-start = (f32[8,108]{1,0:T(8,128)S(1)}, f32[8,108]{1,0:T(8,128)S(1)}, u32[]{:S(2)}, u32[]{:S(2)}) collective-permute-start(f32[8,108]{1,0:T(8,128)S(1)} %concatenate.11.own_data_ref), channel_id=1, source_target_pairs={{0,1},{1,2},{2,3},{3,4},{4,5},{5,6},{6,7},{7,8},{8,9},{9,10},{10,1... | collective-permute-start | bytes 10376 | tf_op jit(solution)/shard_map/ppermute | solution.py:226
  124.5 5.2 %collective-permute-start.1 = (bf16[512,1280]{1,0:T(8,128)(2,1)}, bf16[512,1280]{1,0:T(8,128)(2,1)S(1)}, u32[]{:S(2)}, u32[]{:S(2)}) collective-permute-start(bf16[512,1280]{1,0:T(8,128)(2,1)} %all-gather.3.cloned.1.call-done), channel_id=1, source_target_pairs={{0,4},{4,0},{1,5},{5,1},{2,6},{6,2},{3,7},{7,3},{8,12},{12,8},{9,1... | collective-permute-start | bytes 3932168 | tf_op jit(solution)/shard_map/ppermute | solution.py:250
  126.4 5.3 %collective-permute-start.2 = (bf16[512,1280]{1,0:T(8,128)(2,1)}, bf16[512,1280]{1,0:T(8,128)(2,1)S(1)}, u32[]{:S(2)}, u32[]{:S(2)}) collective-permute-start(bf16[512,1280]{1,0:T(8,128)(2,1)} %all-gather.5.cloned.1.call-done), channel_id=1, source_target_pairs={{0,4},{4,0},{1,5},{5,1},{2,6},{6,2},{3,7},{7,3},{8,12},{12,8},{9,1... | collective-permute-start | bytes 3932168 | tf_op jit(solution)/shard_map/ppermute | solution.py:250
  129.7 2.0 %copy-start = (bf16[512,1280]{1,0:T(8,128)(2,1)}, bf16[512,1280]{1,0:T(8,128)(2,1)S(1)}, u32[]{:S(2)}) copy-start(bf16[512,1280]{1,0:T(8,128)(2,1)S(1)} %collective-permute-done.1) | copy-start | bytes 3932164
  131.6 1.1 copy-start.1
  150.2 22.5 %all-to-all-start.2 = ((f32[128,1,128]{2,1,0:T(1,128)}), f32[128,1,128]{2,1,0:T(1,128)S(1)}, u32[]{:S(2)}, u32[]{:S(2)}) async-start(f32[128,1,128]{2,1,0:T(1,128)} %bitcast.39), calls=%async_computation.2 | async-start | bytes 131072 | tf_op jit(solution)/shard_map/all_to_all | solution.py:348
  172.7 9.8 %collective-permute-start.3 = (f32[128,128]{1,0:T(8,128)S(1)}, f32[128,128]{1,0:T(8,128)S(1)}, u32[]{:S(2)}, u32[]{:S(2)}) collective-permute-start(f32[128,128]{1,0:T(8,128)S(1)} %bitcast.25), channel_id=1, source_target_pairs={{0,1},{1,2},{2,3},{3,4},{4,5},{5,6},{6,7},{7,8},{8,9},{9,10},{10,1... | collective-permute-start | bytes 196616 | tf_op jit(solution)/shard_map/ppermute | solution.py:226
Sparse Core Ops, SparseCore 0:
  30.0 50.0 all-gather.2
  82.1 42.3 all-gather.4

commit v4 on v3

--- a/solution.py
+++ b/solution.py
@@ -13,7 +13,7 @@
 SLICE = 256
 BLOCKS = 8
 SENT = 5
-PARTS = 2
+PIECES = 5
 
 highest = lax.Precision.HIGHEST
 f32 = jnp.float32
@@ -63,19 +63,28 @@
 def solve_kernel(
     side_ref, pick_ref, loading_ref, occupied_ref, press_hbm, forcing_hbm, fiber_hbm, state_hbm, *refs,
 ):
-    shares = refs[: 2 * PARTS]
+    shares = refs[: 2 * PIECES]
     (
         table_hbm, result_ref, back_ref, network, pressure, forcing, fiber, table, damp_sum, stress_sum,
         net_sems, in_sems, out_sems,
-    ) = refs[2 * PARTS :]
+    ) = refs[2 * PIECES :]
     rows = fiber.shape[0]
     nodes = fiber.shape[1]
     cap = table.shape[1]
-    lines = network.shape[1] // PARTS
-
-    def fetch(i, side, k):
-        place = network.at[i, pl.ds(k % PARTS * lines, lines), side]
-        return pltpu.make_async_copy(shares[k].at[i], place, net_sems.at[i, k])
+    half_rows = network.shape[3] // 2
+    width = network.shape[4] // 2
+
+    def fetch(k):
+        depth = shares[k].shape[0]
+        turn = (0, 3, 1, 2, 2)[k % PIECES]
+        side = side_ref[0] if k < PIECES else 1 - side_ref[0]
+        quarter = (side_ref[1] + turn) % 4
+        place = network.at[
+            pl.ds(BLOCKS // 2 if k % PIECES == PIECES - 1 else 0, depth), :, side,
+            pl.ds(pl.multiple_of(quarter // 2 * half_rows, half_rows), half_rows),
+            pl.ds(pl.multiple_of(quarter % 2 * width, width), width),
+        ]
+        return pltpu.make_async_copy(shares[k], place, net_sems.at[k])
 
     inputs = (
         pltpu.make_async_copy(press_hbm, pressure.at[0], in_sems.at[0]),
@@ -84,21 +93,10 @@
         pltpu.make_async_copy(state_hbm, table, in_sems.at[3]),
     )
     inputs[0].start()
-    arrival = [(1 + i) % BLOCKS for i in range(BLOCKS)]
-    for side in range(2):
-
-        @pl.when(side_ref[0] == side)
-        def _():
-            for i in arrival:
-                for k in range(2 * PARTS):
-                    fetch(i, side if k < PARTS else 1 - side, k).start()
-
+    for k in range(2 * PIECES):
+        fetch(k).start()
     for copy in inputs[1:]:
         copy.start()
-
-    def wait_network(i):
-        for k in range(2 * PARTS):
-            fetch(i, 0, k).wait()
 
     def net(i, start, blocks):
         cols = pl.ds(start * SLICE, blocks * SLICE)
@@ -114,15 +112,13 @@
     damp_sum[...] = jnp.zeros_like(damp_sum)
     stress_sum[...] = jnp.zeros_like(stress_sum)
     inputs[0].wait()
-    for i in arrival[:3]:
-        wait_network(i)
+    for k in range(2 * PIECES):
+        fetch(k).wait()
     for iteration in range(ITERS):
         source = pressure.at[iteration]
         for step in range(BLOCKS):
-            n = (step + 4) % BLOCKS
+            n = step
             cols = pl.ds(n * SLICE, SLICE)
-            if iteration == 0 and step < BLOCKS - 3:
-                wait_network(n)
             moved = dot_nt(source[:, pl.ds(n * SLICE, SENT * SLICE)], net(n, 0, SENT))
             for d in range(1, BLOCKS - SENT + 1):
                 i = (n - d) % BLOCKS
@@ -232,24 +228,26 @@
 
 def spread_network(compliance):
     rows, nodes = compliance.shape
+    ring = lax.axis_size("blk")
+    width = SENT * SLICE // 2
     around = jnp.concatenate([compliance, compliance[:, : (SENT - 1) * SLICE]], axis=1)
-    half = lax.dynamic_slice(around, (0, lax.axis_index("z") * SLICE), (rows, SENT * SLICE))
-    count = lax.axis_size("y")
-    line = lax.all_to_all(
-        jnp.broadcast_to(half[None], (count,) + half.shape), "y", split_axis=0, concat_axis=0, tiled=True
-    )
-    line = line.reshape(count * rows, SENT * SLICE)
-    part = count * rows // PARTS
-    planes = [
-        lax.all_gather(line[p * part : (p + 1) * part], "z", axis=0, tiled=True) for p in range(PARTS)
-    ]
-    return line, planes
-
-
-def swap_cores(planes, rows):
-    others = [lax.ppermute(plane, "core", [(0, 1), (1, 0)]) for plane in planes]
-    shape = (BLOCKS, planes[0].shape[0] // (BLOCKS * rows), rows, SENT * SLICE)
-    return [block.reshape(shape) for block in planes + others]
+    quarter = lax.axis_index("blk")
+    start = (quarter // 2 * (rows // 2), lax.axis_index("z") * SLICE + quarter % 2 * width)
+    part = lax.dynamic_slice(around, start, (rows // 2, width))
+    depth, lines = lax.axis_size("z"), lax.axis_size("y")
+    own = lax.all_to_all(
+        jnp.broadcast_to(part[None], (depth * lines,) + part.shape), ("z", "y"),
+        split_axis=0, concat_axis=0, tiled=True,
+    ).reshape((depth, lines) + part.shape)
+
+    def pass_on(value, step):
+        return lax.ppermute(value, "blk", [(i, (i + step) % ring) for i in range(ring)])
+
+    before = pass_on(own, 1)
+    after = pass_on(own, -1)
+    across = [pass_on(before[: depth // 2], 1), pass_on(after[depth // 2 :], -1)]
+    pieces = [own, before, after] + across
+    return own, pieces + [lax.ppermute(piece, "core", [(0, 1), (1, 0)]) for piece in pieces]
 
 
 def body(
@@ -263,13 +261,13 @@
     nodes = compliance.shape[1]
     rows = round_up(cap + COMPS, 8)
 
-    line, planes = spread_network(compliance)
+    own, shares = spread_network(compliance)
 
     worker_ids = jnp.arange(workers)
     send_pick = (worker_ids[:, None] == rve_worker[None, :]).astype(bf16)
     element_rows = jnp.concatenate([fiber_coeff, jnp.pad(strain, ((0, 0), (0, 128 - COMPS)))], axis=1)
     outgoing = jnp.dot(send_pick, element_rows)
-    outgoing = lax.optimization_barrier((outgoing, line))[0]
+    outgoing = lax.optimization_barrier((outgoing, own))[0]
     arrived = lax.all_to_all(outgoing, RVE, split_axis=0, concat_axis=0, tiled=True)
 
     occupied = slot_element >= 0
@@ -310,10 +308,9 @@
     )
     behind_data = from_behind(corner_data, ALL, 1)
 
-    planes, press, corner_data, behind_data, loading_sums, slot_give, occupied_rows = lax.optimization_barrier(
-        (planes, press, corner_data, behind_data, loading_sums, slot_pick.T, occupied.astype(jnp.int32)[:, None])
-    )
-    shares = swap_cores(planes, compliance.shape[0])
+    press, corner_data, behind_data, loading_sums, slot_give, occupied_rows = lax.optimization_barrier(
+        (press, corner_data, behind_data, loading_sums, slot_pick.T, occupied.astype(jnp.int32)[:, None])
+    )
 
     vmem = pl.BlockSpec(memory_space=pltpu.VMEM)
     hbm = pl.BlockSpec(memory_space=pltpu.HBM)
@@ -324,23 +321,23 @@
             jax.ShapeDtypeStruct((rows, 128), f32),
             jax.ShapeDtypeStruct((workers, 128), f32),
         ),
-        in_specs=[pl.BlockSpec(memory_space=pltpu.SMEM)] + [vmem] * 3 + [hbm] * (4 + 2 * PARTS),
+        in_specs=[pl.BlockSpec(memory_space=pltpu.SMEM)] + [vmem] * 3 + [hbm] * (4 + 2 * PIECES),
         out_specs=(hbm, vmem, vmem),
         scratch_shapes=[
-            pltpu.VMEM((BLOCKS, PARTS * shares[0].shape[1], 2, shares[0].shape[2], SENT * SLICE), bf16),
+            pltpu.VMEM((BLOCKS, lax.axis_size("y"), 2, compliance.shape[0], SENT * SLICE), bf16),
             pltpu.VMEM((ITERS, 3 * rows, wide), bf16),
             pltpu.VMEM((3, rows, nodes), f32),
             pltpu.VMEM((rows, nodes), f32),
             pltpu.VMEM((3, cap, nodes), f32),
             pltpu.VMEM((3 * rows, 256), f32),
             pltpu.VMEM((3 * rows, 128), f32),
-            pltpu.SemaphoreType.DMA((BLOCKS, 2 * PARTS)),
+            pltpu.SemaphoreType.DMA((2 * PIECES,)),
             pltpu.SemaphoreType.DMA((4,)),
             pltpu.SemaphoreType.DMA((BLOCKS,)),
         ],
         name="solve",
     )(
-        lax.axis_index("core")[None].astype(jnp.int32), slot_give, loading_sums,
+        jnp.stack([lax.axis_index("core"), lax.axis_index("blk")]).astype(jnp.int32), slot_give, loading_sums,
         occupied_rows, press, forcing, fiber, states, *shares,
     )
     new_table = jnp.transpose(table, (1, 0, 2))

time: 191 us -> 162 us (0.85)
  starting transfers between devices: 34.2 us -> 64.6 us
  waiting for transfers between devices: 83.9 us -> 54.5 us
  blocking collectives: 20.2 us -> 0 us
  between operations: 14.3 us -> 1.04 us
  local copies, waits for them, and re-layouts: 10.6 us -> 13.1 us
    all_gather x2 -> x0, waiting for transfers between devices: 42.7 us -> none  [spread_network(): lax.all_gather(line[p * part:(p + 1) * part], 'z', axis=0, tiled=True)]
    all_to_all x0 -> x1, waiting for transfers between devices: none -> 20.6 us  [spread_network(): lax.all_to_all(jnp.broadcast_to(part[None], (depth * lines,) + part.shape...]
    ppermute x2 -> x9, starting transfers between devices: 4.49 us -> 24.8 us  [the longest x4 14.1 us: pass_on(): lax.ppermute(value, 'blk', [(i, (i + step) % ring) for i in range(ring)])]
    all_to_all x1 -> x0, blocking collectives: 20.2 us -> none  [spread_network(): lax.all_to_all(jnp.broadcast_to(half[None], (count,) + half.shape), 'y',...]
    all_to_all x1, waiting for transfers between devices: 17.3 us -> 0.01 us  [body(): lax.all_to_all(outgoing, RVE, split_axis=0, concat_axis=0, tiled=True)]
    all_to_all x0 -> x1, starting transfers between devices: none -> 15.8 us  [spread_network(): lax.all_to_all(jnp.broadcast_to(part[None], (depth * lines,) + part.shape...]
    ppermute x2 -> x9, waiting for transfers between devices: 1.95 us -> 12.2 us  [the longest x4 12.2 us: pass_on(): lax.ppermute(value, 'blk', [(i, (i + step) % ring) for i in range(ring)])]
    all_to_all x1, starting transfers between devices: 11.3 us -> 7.3 us  [body(): lax.all_to_all(outgoing, RVE, split_axis=0, concat_axis=0, tiled=True)]
  transfers between devices with their start and end apart: 8 -> 14, of which waited for: 6 -> 5; matrix products, arithmetic and copies ran while one was open for 6% -> 7% of each run, Pallas kernels for 3% -> 3%
where the time goes in v4:
time: 162 us; the launch traced here: 161 us
  starting transfers between devices  64.6 us (40%)
  waiting for transfers between devices  54.5 us (34%)
  Pallas kernels  23.6 us (15%)
  local copies, waits for them, and re-layouts  13.1 us (8%)
  other arithmetic  3.67 us (2%)
    all_to_all x1, waiting for transfers between devices, spread_network(): lax.all_to_all(jnp.broadcast_to(part[None], (depth * lines,) + part.shape...  20.6 us
    pallas_call x1, Pallas kernels, body(): pl.pallas_call(solve_kernel, out_shape=(jax.ShapeDtypeStruct((3, cap, nod...  17.3 us
    all_to_all x1, starting transfers between devices, spread_network(): lax.all_to_all(jnp.broadcast_to(part[None], (depth * lines,) + part.shape...  15.8 us
    ppermute x4, starting transfers between devices, pass_on(): lax.ppermute(value, 'blk', [(i, (i + step) % ring) for i in range(ring)])  14.1 us
    all_to_all x1, starting transfers between devices, body(): lax.all_to_all(backward, RVE, split_axis=0, concat_axis=0, tiled=True)  12.9 us
    ppermute x4, waiting for transfers between devices, pass_on(): lax.ppermute(value, 'blk', [(i, (i + step) % ring) for i in range(ring)])  12.2 us
    ppermute x2, waiting for transfers between devices, from_behind(): return lax.ppermute(block, axis, route)  11.7 us
    ppermute x5, starting transfers between devices, spread_network(): lax.ppermute(piece, 'core', [(0, 1), (1, 0)])  10.7 us
  transfers between devices with their start and end apart: 14, of which 5 were waited for; matrix products, arithmetic and copies ran while one was open for 7% of the time, Pallas kernels for 3%

profile of v4, /device:TPU:64, one launch (start us, length us, event | category | flops | bytes accessed | tf_op | source)
XLA Modules:
  0.0 160.9 jit_solution(1786190358683925631)
XLA Ops:
  3.1 15.8 %all-to-all-start = ((bf16[64,8,640]{2,1,0:T(8,128)(2,1)}), bf16[64,8,640]{2,1,0:T(8,128)(2,1)S(1)}, u32[]{:S(2)}, u32[]{:S(2)}) async-start(bf16[64,8,640]{2,1,0:T(8,128)(2,1)} %broadcast_in_dim.11), calls=%async_computation | async-start | bytes 1310720 | tf_op jit(solution)/shard_map/all_to_all | solution.py:238
  19.3 20.6 %all-to-all-done = bf16[64,8,640]{2,1,0:T(8,128)(2,1)S(1)} async-done(((bf16[64,8,640]{2,1,0:T(8,128)(2,1)}), bf16[64,8,640]{2,1,0:T(8,128)(2,1)S(1)}, u32[]{:S(2)}, u32[]{:S(2)}) %all-to-all-start) | async-done | bytes 655392 | tf_op jit(solution)/shard_map/all_to_all | solution.py:238
  41.5 1.4 reshape.68
  42.9 7.3 %all-to-all-start.1 = ((bf16[128,2,1088]{2,1,0:T(2,128)(2,1)}), bf16[128,2,1088]{2,1,0:T(2,128)(2,1)S(1)}, u32[]{:S(2)}, u32[]{:S(2)}) async-start(bf16[128,2,1088]{2,1,0:T(2,128)(2,1)} %reshape.68), calls=%async_computation.1 | async-start | bytes 1179648 | tf_op jit(solution)/shard_map/all_to_all | solution.py:271
  50.2 4.6 %collective-permute-start.2 = (bf16[8,8,8,640]{3,2,1,0:T(8,128)(2,1)S(1)}, bf16[8,8,8,640]{3,2,1,0:T(8,128)(2,1)S(1)}, u32[]{:S(2)}, u32[]{:S(2)}) collective-permute-start(bf16[8,8,8,640]{3,2,1,0:T(8,128)(2,1)S(1)} %bitcast.25), channel_id=1, source_target_pairs={{0,3},{1,0},{2,1},{3,2},{4,7},{5,4},{6,5},{7,6},{8,11},{9,8},{10,9... | collective-permute-start | bytes 1966088 | tf_op jit(solution)/shard_map/ppermute | solution.py:244
  54.8 1.9 %collective-permute-start.1 = (bf16[8,8,8,640]{3,2,1,0:T(8,128)(2,1)S(1)}, bf16[8,8,8,640]{3,2,1,0:T(8,128)(2,1)}, u32[]{:S(2)}, u32[]{:S(2)}) collective-permute-start(bf16[8,8,8,640]{3,2,1,0:T(8,128)(2,1)S(1)} %bitcast.26), channel_id=1, source_target_pairs={{0,1},{1,2},{2,3},{3,0},{4,5},{5,6},{6,7},{7,4},{8,9},{9,10},{10,1... | collective-permute-start | bytes 1966088 | tf_op jit(solution)/shard_map/ppermute | solution.py:244
  56.9 12.2 %collective-permute-done.2.refs_2_ = bf16[8,8,8,640]{3,2,1,0:T(8,128)(2,1)S(1)} collective-permute-done((bf16[8,8,8,640]{3,2,1,0:T(8,128)(2,1)S(1)}, bf16[8,8,8,640]{3,2,1,0:T(8,128)(2,1)S(1)}, u32[]{:S(2)}, u32[]{:S(2)}) %collective-permute-start.2) | collective-permute-done | bytes 655392 | tf_op jit(solution)/shard_map/ppermute | solution.py:244
  69.9 5.6 %collective-permute-start.4 = (bf16[4,8,8,640]{3,2,1,0:T(8,128)(2,1)}, bf16[4,8,8,640]{3,2,1,0:T(8,128)(2,1)S(1)}, u32[]{:S(2)}, u32[]{:S(2)}) collective-permute-start(bf16[4,8,8,640]{3,2,1,0:T(8,128)(2,1)} %slice.17), channel_id=1, source_target_pairs={{0,3},{1,0},{2,1},{3,2},{4,7},{5,4},{6,5},{7,6},{8,11},{9,8},{10,9... | collective-permute-start | bytes 983048 | tf_op jit(solution)/shard_map/ppermute | solution.py:244
  76.2 1.3 pad.26.loading_ref
  77.6 1.9 %collective-permute-start.5 = (bf16[8,8,8,640]{3,2,1,0:T(8,128)(2,1)S(1)}, bf16[8,8,8,640]{3,2,1,0:T(8,128)(2,1)}, u32[]{:S(2)}, u32[]{:S(2)}) collective-permute-start(bf16[8,8,8,640]{3,2,1,0:T(8,128)(2,1)S(1)} %bitcast.27), channel_id=1, source_target_pairs={{0,4},{4,0},{1,5},{5,1},{2,6},{6,2},{3,7},{7,3},{8,12},{12,8},{9,1... | collective-permute-start | bytes 1966088 | tf_op jit(solution)/shard_map/ppermute | solution.py:250
  79.5 1.7 %slice.16 = bf16[4,8,8,640]{3,2,1,0:T(8,128)(2,1)} slice(bf16[8,8,8,640]{3,2,1,0:T(8,128)(2,1)} %collective-permute-done.1.refs_1_), slice={[0:4], [0:8], [0:8], [0:640]} | slice | bytes 655360 | tf_op jit(solution)/shard_map/slice | solution.py:248
  81.2 1.9 %collective-permute-start.3 = (bf16[4,8,8,640]{3,2,1,0:T(8,128)(2,1)}, bf16[4,8,8,640]{3,2,1,0:T(8,128)(2,1)}, u32[]{:S(2)}, u32[]{:S(2)}) collective-permute-start(bf16[4,8,8,640]{3,2,1,0:T(8,128)(2,1)} %slice.16), channel_id=1, source_target_pairs={{0,1},{1,2},{2,3},{3,0},{4,5},{5,6},{6,7},{7,4},{8,9},{9,10},{10,1... | collective-permute-start | bytes 983048 | tf_op jit(solution)/shard_map/ppermute | solution.py:244
  83.1 2.4 %collective-permute-start.7 = (bf16[8,8,8,640]{3,2,1,0:T(8,128)(2,1)S(1)}, bf16[8,8,8,640]{3,2,1,0:T(8,128)(2,1)}, u32[]{:S(2)}, u32[]{:S(2)}) collective-permute-start(bf16[8,8,8,640]{3,2,1,0:T(8,128)(2,1)S(1)} %collective-permute-done.2.refs_2_), channel_id=1, source_target_pairs={{0,4},{4,0},{1,5},{5,1},{2,6},{6,2},{3,7},{7,3},{8,12},{12,8},{9,1... | collective-permute-start | bytes 1966088 | tf_op jit(solution)/shard_map/ppermute | solution.py:250
  85.5 1.9 %collective-permute-start.6 = (bf16[8,8,8,640]{3,2,1,0:T(8,128)(2,1)}, bf16[8,8,8,640]{3,2,1,0:T(8,128)(2,1)}, u32[]{:S(2)}, u32[]{:S(2)}) collective-permute-start(bf16[8,8,8,640]{3,2,1,0:T(8,128)(2,1)} %collective-permute-done.1.refs_1_), channel_id=1, source_target_pairs={{0,4},{4,0},{1,5},{5,1},{2,6},{6,2},{3,7},{7,3},{8,12},{12,8},{9,1... | collective-permute-start | bytes 1966088 | tf_op jit(solution)/shard_map/ppermute | solution.py:250
  89.1 5.1 %prepare.1 = (bf16[264,3072]{1,0:T(8,128)(2,1)}, f32[3,88,2048]{2,1,0:T(8,128)}, f32[88,2048]{1,0:T(8,128)}) custom-call(bf16[88,128]{1,0:T(8,128)(2,1)} %get-tuple-element.45.pick_ref, f32[88,128]{1,0:T(8,128)} %get-tuple-element.46.unit_ref, bf16[128,2176]{1,0:T(8,128)(2,1)} %bitcast.30, bf16[3,128,2048]{2,1,0:T(8,128)(2,1)} %pad.26.loading_ref, ...), custom_call_target="tpu_custom_call" | custom-call | tf_op jit(solution)/shard_map/prepare/pallas_call | solution.py:285
  94.7 1.9 %collective-permute-start = (f32[8,108]{1,0:T(8,128)S(1)}, f32[8,108]{1,0:T(8,128)S(1)}, u32[]{:S(2)}, u32[]{:S(2)}) collective-permute-start(f32[8,108]{1,0:T(8,128)S(1)} %concatenate.11.own_data_ref), channel_id=1, source_target_pairs={{0,1},{1,2},{2,3},{3,4},{4,5},{5,6},{6,7},{7,8},{8,9},{9,10},{10,1... | collective-permute-start | bytes 10376 | tf_op jit(solution)/shard_map/ppermute | solution.py:222
  97.5 2.4 %collective-permute-start.9 = (bf16[4,8,8,640]{3,2,1,0:T(8,128)(2,1)S(1)}, bf16[4,8,8,640]{3,2,1,0:T(8,128)(2,1)S(1)}, u32[]{:S(2)}, u32[]{:S(2)}) collective-permute-start(bf16[4,8,8,640]{3,2,1,0:T(8,128)(2,1)S(1)} %collective-permute-done.4.refs_4_), channel_id=1, source_target_pairs={{0,4},{4,0},{1,5},{5,1},{2,6},{6,2},{3,7},{7,3},{8,12},{12,8},{9,1... | collective-permute-start | bytes 983048 | tf_op jit(solution)/shard_map/ppermute | solution.py:250
  99.9 3.9 %collective-permute-done.behind_data_ref = f32[8,108]{1,0:T(8,128)S(1)} collective-permute-done((f32[8,108]{1,0:T(8,128)S(1)}, f32[8,108]{1,0:T(8,128)S(1)}, u32[]{:S(2)}, u32[]{:S(2)}) %collective-permute-start) | collective-permute-done | bytes 3488 | tf_op jit(solution)/shard_map/ppermute | solution.py:222
  103.8 2.1 %collective-permute-start.8 = (bf16[4,8,8,640]{3,2,1,0:T(8,128)(2,1)}, bf16[4,8,8,640]{3,2,1,0:T(8,128)(2,1)S(1)}, u32[]{:S(2)}, u32[]{:S(2)}) collective-permute-start(bf16[4,8,8,640]{3,2,1,0:T(8,128)(2,1)} %collective-permute-done.3.refs_3_), channel_id=1, source_target_pairs={{0,4},{4,0},{1,5},{5,1},{2,6},{6,2},{3,7},{7,3},{8,12},{12,8},{9,1... | collective-permute-start | bytes 983048 | tf_op jit(solution)/shard_map/ppermute | solution.py:250
  108.7 17.3 %solve.1 = (f32[3,81,2048]{2,1,0:T(8,128)}, f32[88,128]{1,0:T(8,128)}, f32[128,128]{1,0:T(8,128)}) custom-call(s32[2]{0:T(128)} %pad_add_fusion.side_ref, bf16[128,88]{1,0:T(8,128)(2,1)} %fusion.8.pick_ref, bf16[128,2048]{1,0:T(8,128)(2,1)} %pad.28.loading_ref, s32[81,1]{1,0:T(8,128)} %copy.34.occupied_ref, bf16[264,3072]{1,0:T(8,128)(2,1)} %get-tuple-element.33.press_hbm, ...), custom_call_target="tpu_custom_call" | custom-call | tf_op jit(solution)/shard_map/solve/pallas_call | solution.py:317
  126.0 12.9 %all-to-all-start.2 = ((f32[128,1,128]{2,1,0:T(1,128)}), f32[128,1,128]{2,1,0:T(1,128)S(1)}, u32[]{:S(2)}, u32[]{:S(2)}) async-start(f32[128,1,128]{2,1,0:T(1,128)} %bitcast.33), calls=%async_computation.2 | async-start | bytes 131072 | tf_op jit(solution)/shard_map/all_to_all | solution.py:345
  139.8 10.0 %all-to-all-done.2 = f32[128,1,128]{2,1,0:T(1,128)S(1)} async-done(((f32[128,1,128]{2,1,0:T(1,128)}), f32[128,1,128]{2,1,0:T(1,128)S(1)}, u32[]{:S(2)}, u32[]{:S(2)}) %all-to-all-start.2) | async-done | bytes 65568 | tf_op jit(solution)/shard_map/all_to_all | solution.py:345
  149.8 1.9 %collective-permute-start.10 = (f32[128,128]{1,0:T(8,128)S(1)}, f32[128,128]{1,0:T(8,128)S(1)}, u32[]{:S(2)}, u32[]{:S(2)}) collective-permute-start(f32[128,128]{1,0:T(8,128)S(1)} %bitcast.21), channel_id=1, source_target_pairs={{0,1},{1,2},{2,3},{3,4},{4,5},{5,6},{6,7},{7,8},{8,9},{9,10},{10,1... | collective-permute-start | bytes 196616 | tf_op jit(solution)/shard_map/ppermute | solution.py:222
  151.8 7.8 %collective-permute-done.10.behind_ref = f32[128,128]{1,0:T(8,128)S(1)} collective-permute-done((f32[128,128]{1,0:T(8,128)S(1)}, f32[128,128]{1,0:T(8,128)S(1)}, u32[]{:S(2)}, u32[]{:S(2)}) %collective-permute-start.10) | collective-permute-done | bytes 65568 | tf_op jit(solution)/shard_map/ppermute | solution.py:222
  (73 shorter events, 13.9 us)
Async XLA Ops:
  0.6 18.3 %copy-start.8 = (bf16[27,6]{0,1:T(8,128)(2,1)S(1)}, bf16[27,6]{0,1:T(8,128)(2,1)}, u32[]{:S(2)}) copy-start(bf16[27,6]{0,1:T(8,128)(2,1)} %param.11) | copy-start | bytes 976
  0.6 18.4 %copy-start.10 = (s32[27]{0:T(128)S(1)}, s32[27]{0:T(128)}, u32[]{:S(2)}) copy-start(s32[27]{0:T(128)} %param.16) | copy-start | bytes 328
  0.7 18.4 %copy-start.5 = (bf16[27,2048]{1,0:T(8,128)(2,1)S(1)}, bf16[27,2048]{1,0:T(8,128)(2,1)}, u32[]{:S(2)}) copy-start(bf16[27,2048]{1,0:T(8,128)(2,1)} %param.12) | copy-start | bytes 331780
  3.1 36.8 %all-to-all-start = ((bf16[64,8,640]{2,1,0:T(8,128)(2,1)}), bf16[64,8,640]{2,1,0:T(8,128)(2,1)S(1)}, u32[]{:S(2)}, u32[]{:S(2)}) async-start(bf16[64,8,640]{2,1,0:T(8,128)(2,1)} %broadcast_in_dim.11), calls=%async_computation | async-start | bytes 1310720 | tf_op jit(solution)/shard_map/all_to_all | solution.py:238
  18.9 37.8 %copy-start.12 = (s32[81]{0:T(128)S(1)}, s32[81]{0:T(128)}, u32[]{:S(2)}) copy-start(s32[81]{0:T(128)} %param.17) | copy-start | bytes 976
  18.9 37.9 %copy-start.6 = (bf16[6,3,2048]{2,1,0:T(4,128)(2,1)S(1)}, bf16[6,3,2048]{2,1,0:T(4,128)(2,1)}, u32[]{:S(2)}) copy-start(bf16[6,3,2048]{2,1,0:T(4,128)(2,1)} %param.19) | copy-start | bytes 221188
  39.9 37.6 %copy-start = (bf16[64,8,640]{2,1,0:T(8,128)(2,1)}, bf16[64,8,640]{2,1,0:T(8,128)(2,1)S(1)}, u32[]{:S(2)}) copy-start(bf16[64,8,640]{2,1,0:T(8,128)(2,1)S(1)} %all-to-all-done) | copy-start | bytes 1966084
  42.9 44.6 %all-to-all-start.1 = ((bf16[128,2,1088]{2,1,0:T(2,128)(2,1)}), bf16[128,2,1088]{2,1,0:T(2,128)(2,1)S(1)}, u32[]{:S(2)}, u32[]{:S(2)}) async-start(bf16[128,2,1088]{2,1,0:T(2,128)(2,1)} %reshape.68), calls=%async_computation.1 | async-start | bytes 1179648 | tf_op jit(solution)/shard_map/all_to_all | solution.py:271
  50.2 18.9 %collective-permute-start.2 = (bf16[8,8,8,640]{3,2,1,0:T(8,128)(2,1)S(1)}, bf16[8,8,8,640]{3,2,1,0:T(8,128)(2,1)S(1)}, u32[]{:S(2)}, u32[]{:S(2)}) collective-permute-start(bf16[8,8,8,640]{3,2,1,0:T(8,128)(2,1)S(1)} %bitcast.25), channel_id=1, source_target_pairs={{0,3},{1,0},{2,1},{3,2},{4,7},{5,4},{6,5},{7,6},{8,11},{9,8},{10,9... | collective-permute-start | bytes 1966088 | tf_op jit(solution)/shard_map/ppermute | solution.py:244
  54.8 24.7 %collective-permute-start.1 = (bf16[8,8,8,640]{3,2,1,0:T(8,128)(2,1)S(1)}, bf16[8,8,8,640]{3,2,1,0:T(8,128)(2,1)}, u32[]{:S(2)}, u32[]{:S(2)}) collective-permute-start(bf16[8,8,8,640]{3,2,1,0:T(8,128)(2,1)S(1)} %bitcast.26), channel_id=1, source_target_pairs={{0,1},{1,2},{2,3},{3,0},{4,5},{5,6},{6,7},{7,4},{8,9},{9,10},{10,1... | collective-permute-start | bytes 1966088 | tf_op jit(solution)/shard_map/ppermute | solution.py:244
  69.1 19.1 %copy-start.1 = (bf16[8,8,8,640]{3,2,1,0:T(8,128)(2,1)}, bf16[8,8,8,640]{3,2,1,0:T(8,128)(2,1)S(1)}, u32[]{:S(2)}) copy-start(bf16[8,8,8,640]{3,2,1,0:T(8,128)(2,1)S(1)} %collective-permute-done.2.refs_2_) | copy-start | bytes 1966084
  69.9 24.7 %collective-permute-start.4 = (bf16[4,8,8,640]{3,2,1,0:T(8,128)(2,1)}, bf16[4,8,8,640]{3,2,1,0:T(8,128)(2,1)S(1)}, u32[]{:S(2)}, u32[]{:S(2)}) collective-permute-start(bf16[4,8,8,640]{3,2,1,0:T(8,128)(2,1)} %slice.17), channel_id=1, source_target_pairs={{0,3},{1,0},{2,1},{3,2},{4,7},{5,4},{6,5},{7,6},{8,11},{9,8},{10,9... | collective-permute-start | bytes 983048 | tf_op jit(solution)/shard_map/ppermute | solution.py:244
  77.6 30.3 %collective-permute-start.5 = (bf16[8,8,8,640]{3,2,1,0:T(8,128)(2,1)S(1)}, bf16[8,8,8,640]{3,2,1,0:T(8,128)(2,1)}, u32[]{:S(2)}, u32[]{:S(2)}) collective-permute-start(bf16[8,8,8,640]{3,2,1,0:T(8,128)(2,1)S(1)} %bitcast.27), channel_id=1, source_target_pairs={{0,4},{4,0},{1,5},{5,1},{2,6},{6,2},{3,7},{7,3},{8,12},{12,8},{9,1... | collective-permute-start | bytes 1966088 | tf_op jit(solution)/shard_map/ppermute | solution.py:250
  81.2 16.3 %collective-permute-start.3 = (bf16[4,8,8,640]{3,2,1,0:T(8,128)(2,1)}, bf16[4,8,8,640]{3,2,1,0:T(8,128)(2,1)}, u32[]{:S(2)}, u32[]{:S(2)}) collective-permute-start(bf16[4,8,8,640]{3,2,1,0:T(8,128)(2,1)} %slice.16), channel_id=1, source_target_pairs={{0,1},{1,2},{2,3},{3,0},{4,5},{5,6},{6,7},{7,4},{8,9},{9,10},{10,1... | collective-permute-start | bytes 983048 | tf_op jit(solution)/shard_map/ppermute | solution.py:244
  83.1 24.7 %collective-permute-start.7 = (bf16[8,8,8,640]{3,2,1,0:T(8,128)(2,1)S(1)}, bf16[8,8,8,640]{3,2,1,0:T(8,128)(2,1)}, u32[]{:S(2)}, u32[]{:S(2)}) collective-permute-start(bf16[8,8,8,640]{3,2,1,0:T(8,128)(2,1)S(1)} %collective-permute-done.2.refs_2_), channel_id=1, source_target_pairs={{0,4},{4,0},{1,5},{5,1},{2,6},{6,2},{3,7},{7,3},{8,12},{12,8},{9,1... | collective-permute-start | bytes 1966088 | tf_op jit(solution)/shard_map/ppermute | solution.py:250
  85.5 22.3 %collective-permute-start.6 = (bf16[8,8,8,640]{3,2,1,0:T(8,128)(2,1)}, bf16[8,8,8,640]{3,2,1,0:T(8,128)(2,1)}, u32[]{:S(2)}, u32[]{:S(2)}) collective-permute-start(bf16[8,8,8,640]{3,2,1,0:T(8,128)(2,1)} %collective-permute-done.1.refs_1_), channel_id=1, source_target_pairs={{0,4},{4,0},{1,5},{5,1},{2,6},{6,2},{3,7},{7,3},{8,12},{12,8},{9,1... | collective-permute-start | bytes 1966088 | tf_op jit(solution)/shard_map/ppermute | solution.py:250
  89.1 5.3 %copy-start.11 = (f32[27]{0:T(128)S(1)}, f32[27]{0:T(128)}, u32[]{:S(2)}) copy-start(f32[27]{0:T(128)} %param.14) | copy-start | bytes 328
  89.1 5.4 %copy-start.7 = (f32[12,27]{1,0:T(8,128)S(1)}, f32[12,27]{1,0:T(8,128)}, u32[]{:S(2)}) copy-start(f32[12,27]{1,0:T(8,128)} %param.13) | copy-start | bytes 3892
  94.6 13.2 %copy-start.2 = (bf16[4,8,8,640]{3,2,1,0:T(8,128)(2,1)}, bf16[4,8,8,640]{3,2,1,0:T(8,128)(2,1)S(1)}, u32[]{:S(2)}) copy-start(bf16[4,8,8,640]{3,2,1,0:T(8,128)(2,1)S(1)} %collective-permute-done.4.refs_4_) | copy-start | bytes 983044
  94.7 9.1 %collective-permute-start = (f32[8,108]{1,0:T(8,128)S(1)}, f32[8,108]{1,0:T(8,128)S(1)}, u32[]{:S(2)}, u32[]{:S(2)}) collective-permute-start(f32[8,108]{1,0:T(8,128)S(1)} %concatenate.11.own_data_ref), channel_id=1, source_target_pairs={{0,1},{1,2},{2,3},{3,4},{4,5},{5,6},{6,7},{7,8},{8,9},{9,10},{10,1... | collective-permute-start | bytes 10376 | tf_op jit(solution)/shard_map/ppermute | solution.py:222
  97.5 10.3 %collective-permute-start.9 = (bf16[4,8,8,640]{3,2,1,0:T(8,128)(2,1)S(1)}, bf16[4,8,8,640]{3,2,1,0:T(8,128)(2,1)S(1)}, u32[]{:S(2)}, u32[]{:S(2)}) collective-permute-start(bf16[4,8,8,640]{3,2,1,0:T(8,128)(2,1)S(1)} %collective-permute-done.4.refs_4_), channel_id=1, source_target_pairs={{0,4},{4,0},{1,5},{5,1},{2,6},{6,2},{3,7},{7,3},{8,12},{12,8},{9,1... | collective-permute-start | bytes 983048 | tf_op jit(solution)/shard_map/ppermute | solution.py:250
  103.8 4.1 %collective-permute-start.8 = (bf16[4,8,8,640]{3,2,1,0:T(8,128)(2,1)}, bf16[4,8,8,640]{3,2,1,0:T(8,128)(2,1)S(1)}, u32[]{:S(2)}, u32[]{:S(2)}) collective-permute-start(bf16[4,8,8,640]{3,2,1,0:T(8,128)(2,1)} %collective-permute-done.3.refs_3_), channel_id=1, source_target_pairs={{0,4},{4,0},{1,5},{5,1},{2,6},{6,2},{3,7},{7,3},{8,12},{12,8},{9,1... | collective-permute-start | bytes 983048 | tf_op jit(solution)/shard_map/ppermute | solution.py:250
  126.0 23.9 %all-to-all-start.2 = ((f32[128,1,128]{2,1,0:T(1,128)}), f32[128,1,128]{2,1,0:T(1,128)S(1)}, u32[]{:S(2)}, u32[]{:S(2)}) async-start(f32[128,1,128]{2,1,0:T(1,128)} %bitcast.33), calls=%async_computation.2 | async-start | bytes 131072 | tf_op jit(solution)/shard_map/all_to_all | solution.py:345
  149.8 9.8 %collective-permute-start.10 = (f32[128,128]{1,0:T(8,128)S(1)}, f32[128,128]{1,0:T(8,128)S(1)}, u32[]{:S(2)}, u32[]{:S(2)}) collective-permute-start(f32[128,128]{1,0:T(8,128)S(1)} %bitcast.21), channel_id=1, source_target_pairs={{0,1},{1,2},{2,3},{3,4},{4,5},{5,6},{6,7},{7,8},{8,9},{9,10},{10,1... | collective-permute-start | bytes 196616 | tf_op jit(solution)/shard_map/ppermute | solution.py:222
  (3 other events, 6.7 us)

commit v5 on v4

--- a/solution.py
+++ b/solution.py
@@ -13,7 +13,7 @@
 SLICE = 256
 BLOCKS = 8
 SENT = 5
-PIECES = 5
+PIECES = ((0, 0), (3, 0), (3, 1), (1, 0), (1, 1), (2, 0), (2, 1))
 
 highest = lax.Precision.HIGHEST
 f32 = jnp.float32
@@ -63,11 +63,11 @@
 def solve_kernel(
     side_ref, pick_ref, loading_ref, occupied_ref, press_hbm, forcing_hbm, fiber_hbm, state_hbm, *refs,
 ):
-    shares = refs[: 2 * PIECES]
+    shares = refs[: 2 * len(PIECES)]
     (
         table_hbm, result_ref, back_ref, network, pressure, forcing, fiber, table, damp_sum, stress_sum,
         net_sems, in_sems, out_sems,
-    ) = refs[2 * PIECES :]
+    ) = refs[2 * len(PIECES) :]
     rows = fiber.shape[0]
     nodes = fiber.shape[1]
     cap = table.shape[1]
@@ -76,11 +76,11 @@
 
     def fetch(k):
         depth = shares[k].shape[0]
-        turn = (0, 3, 1, 2, 2)[k % PIECES]
-        side = side_ref[0] if k < PIECES else 1 - side_ref[0]
+        turn, late = PIECES[k % len(PIECES)]
+        side = side_ref[0] if k < len(PIECES) else 1 - side_ref[0]
         quarter = (side_ref[1] + turn) % 4
         place = network.at[
-            pl.ds(BLOCKS // 2 if k % PIECES == PIECES - 1 else 0, depth), :, side,
+            pl.ds(late * (BLOCKS // 2), depth), :, side,
             pl.ds(pl.multiple_of(quarter // 2 * half_rows, half_rows), half_rows),
             pl.ds(pl.multiple_of(quarter % 2 * width, width), width),
         ]
@@ -93,7 +93,7 @@
         pltpu.make_async_copy(state_hbm, table, in_sems.at[3]),
     )
     inputs[0].start()
-    for k in range(2 * PIECES):
+    for k in range(2 * len(PIECES)):
         fetch(k).start()
     for copy in inputs[1:]:
         copy.start()
@@ -112,7 +112,7 @@
     damp_sum[...] = jnp.zeros_like(damp_sum)
     stress_sum[...] = jnp.zeros_like(stress_sum)
     inputs[0].wait()
-    for k in range(2 * PIECES):
+    for k in range(2 * len(PIECES)):
         fetch(k).wait()
     for iteration in range(ITERS):
         source = pressure.at[iteration]
@@ -226,7 +226,7 @@
 ALL = ("z", "y", "core", "blk")
 
 
-def spread_network(compliance):
+def spread_network(compliance, ready):
     rows, nodes = compliance.shape
     ring = lax.axis_size("blk")
     width = SENT * SLICE // 2
@@ -243,11 +243,18 @@
     def pass_on(value, step):
         return lax.ppermute(value, "blk", [(i, (i + step) % ring) for i in range(ring)])
 
-    before = pass_on(own, 1)
-    after = pass_on(own, -1)
-    across = [pass_on(before[: depth // 2], 1), pass_on(after[depth // 2 :], -1)]
-    pieces = [own, before, after] + across
-    return own, pieces + [lax.ppermute(piece, "core", [(0, 1), (1, 0)]) for piece in pieces]
+    own, ready = lax.optimization_barrier((own, ready))
+    near, far = own[: depth // 2], own[depth // 2 :]
+    before_near, after_far = pass_on(near, 1), pass_on(far, -1)
+    pieces = [own, before_near, pass_on(far, 1), pass_on(near, -1), after_far]
+    pieces += [pass_on(before_near, 1), pass_on(after_far, -1)]
+    return pieces, ready
+
+
+def swap_cores(pieces, ready):
+    last = list(lax.optimization_barrier((pieces[-2], pieces[-1], ready))[:2])
+    pieces = pieces[:-2] + last
+    return pieces + [lax.ppermute(piece, "core", [(0, 1), (1, 0)]) for piece in pieces]
 
 
 def body(
@@ -261,14 +268,24 @@
     nodes = compliance.shape[1]
     rows = round_up(cap + COMPS, 8)
 
-    own, shares = spread_network(compliance)
-
+    device_rank = lax.axis_index(ALL)
     worker_ids = jnp.arange(workers)
+
     send_pick = (worker_ids[:, None] == rve_worker[None, :]).astype(bf16)
     element_rows = jnp.concatenate([fiber_coeff, jnp.pad(strain, ((0, 0), (0, 128 - COMPS)))], axis=1)
-    outgoing = jnp.dot(send_pick, element_rows)
-    outgoing = lax.optimization_barrier((outgoing, own))[0]
-    arrived = lax.all_to_all(outgoing, RVE, split_axis=0, concat_axis=0, tiled=True)
+    outgoing = jnp.dot(send_pick, element_rows).reshape(workers, 2, (nodes + 128) // 2)
+
+    corner_data = jnp.concatenate(
+        [
+            jnp.transpose(gradients.reshape(4, 3, elems), (1, 0, 2)).reshape(3, 4 * elems),
+            jnp.tile(volume, 4)[None, :],
+            (corners - device_rank * NODE_DEV).reshape(1, 4 * elems).astype(f32),
+            jnp.tile(rve_worker, 4)[None, :].astype(f32),
+            jnp.zeros((2, 4 * elems), f32),
+        ],
+        axis=0,
+    )
+    behind_data = from_behind(corner_data, ALL, 1)
 
     occupied = slot_element >= 0
     home = jnp.where(occupied, slot_element // (elems * columns), -1)
@@ -281,6 +298,20 @@
     loading_sums = jnp.pad(loading_sums, ((8 * COMPS, 128 - 24 - 8 * COMPS), (0, 0)))
     states = jnp.transpose(state_table, (1, 0, 2))
     wide = nodes + (SENT - 1) * SLICE
+    place = jnp.stack([lax.axis_index("core"), lax.axis_index("blk")]).astype(jnp.int32)
+
+    pieces, ready = spread_network(
+        compliance,
+        (
+            outgoing, corner_data, behind_data, slot_pick, slot_pick.T, occupied.astype(jnp.int32)[:, None],
+            unit, loading_wide, loading_sums, place,
+        ),
+    )
+    (
+        outgoing, corner_data, behind_data, slot_pick, slot_give, occupied_rows,
+        unit, loading_wide, loading_sums, place,
+    ) = ready
+    arrived = lax.all_to_all(outgoing, RVE, split_axis=0, concat_axis=0, tiled=True).reshape(workers, nodes + 128)
 
     press, forcing, fiber = pl.pallas_call(
         prepare_kernel,
@@ -292,26 +323,7 @@
         scratch_shapes=[pltpu.VMEM((rows, SLICE), f32)],
         name="prepare",
     )(slot_pick, unit, arrived, loading_wide, states)
-    gradients, volume, corners, rve_worker = lax.optimization_barrier(
-        (press, gradients, volume, corners, rve_worker)
-    )[1:]
-    device_rank = lax.axis_index(ALL)
-    corner_data = jnp.concatenate(
-        [
-            jnp.transpose(gradients.reshape(4, 3, elems), (1, 0, 2)).reshape(3, 4 * elems),
-            jnp.tile(volume, 4)[None, :],
-            (corners - device_rank * NODE_DEV).reshape(1, 4 * elems).astype(f32),
-            jnp.tile(rve_worker, 4)[None, :].astype(f32),
-            jnp.zeros((2, 4 * elems), f32),
-        ],
-        axis=0,
-    )
-    behind_data = from_behind(corner_data, ALL, 1)
-
-    press, corner_data, behind_data, loading_sums, slot_give, occupied_rows = lax.optimization_barrier(
-        (press, corner_data, behind_data, loading_sums, slot_pick.T, occupied.astype(jnp.int32)[:, None])
-    )
-
+    shares = swap_cores(pieces, press)
     vmem = pl.BlockSpec(memory_space=pltpu.VMEM)
     hbm = pl.BlockSpec(memory_space=pltpu.HBM)
     table, result, backward = pl.pallas_call(
@@ -321,7 +333,7 @@
             jax.ShapeDtypeStruct((rows, 128), f32),
             jax.ShapeDtypeStruct((workers, 128), f32),
         ),
-        in_specs=[pl.BlockSpec(memory_space=pltpu.SMEM)] + [vmem] * 3 + [hbm] * (4 + 2 * PIECES),
+        in_specs=[pl.BlockSpec(memory_space=pltpu.SMEM)] + [vmem] * 3 + [hbm] * (4 + 2 * len(PIECES)),
         out_specs=(hbm, vmem, vmem),
         scratch_shapes=[
             pltpu.VMEM((BLOCKS, lax.axis_size("y"), 2, compliance.shape[0], SENT * SLICE), bf16),
@@ -331,13 +343,13 @@
             pltpu.VMEM((3, cap, nodes), f32),
             pltpu.VMEM((3 * rows, 256), f32),
             pltpu.VMEM((3 * rows, 128), f32),
-            pltpu.SemaphoreType.DMA((2 * PIECES,)),
+            pltpu.SemaphoreType.DMA((2 * len(PIECES),)),
             pltpu.SemaphoreType.DMA((4,)),
             pltpu.SemaphoreType.DMA((BLOCKS,)),
         ],
         name="solve",
     )(
-        jnp.stack([lax.axis_index("core"), lax.axis_index("blk")]).astype(jnp.int32), slot_give, loading_sums,
+        place, slot_give, loading_sums,
         occupied_rows, press, forcing, fiber, states, *shares,
     )
     new_table = jnp.transpose(table, (1, 0, 2))

time: 162 us -> 157 us (0.969)
  waiting for transfers between devices: 54.5 us -> 38.6 us
  starting transfers between devices: 64.6 us -> 76.3 us
    ppermute x4 -> x6, waiting for transfers between devices: 12.2 us -> 4.03 us  [pass_on(): lax.ppermute(value, 'blk', [(i, (i + step) % ring) for i in range(ring)])]
    ppermute x4 -> x6, starting transfers between devices: 14.1 us -> 19.2 us  [pass_on(): lax.ppermute(value, 'blk', [(i, (i + step) % ring) for i in range(ring)])]
    all_to_all x1, waiting for transfers between devices: 20.6 us -> 16.1 us  [spread_network(): lax.all_to_all(jnp.broadcast_to(part[None], (depth * lines,) + part.shape...]
    ppermute x5 -> x7, starting transfers between devices: 10.7 us -> 15.1 us  [swap_cores(): lax.ppermute(piece, 'core', [(0, 1), (1, 0)])]
    ppermute x2, waiting for transfers between devices: 11.7 us -> 7.79 us  [from_behind(): return lax.ppermute(block, axis, route)]
    unnamed x31 -> x30, local copies, waits for them, and re-layouts: 3.95 us -> 0.74 us
    slice x2 -> x1, local copies, waits for them, and re-layouts: 2.55 us -> 0.06 us  [spread_network(): near, far = (own[:depth // 2], own[depth // 2:])]
    optimization_barrier x1 -> x2, local copies, waits for them, and re-layouts: 0.72 us -> 2.67 us  [spread_network(): own, ready = lax.optimization_barrier((own, ready))]
  transfers between devices with their start and end apart: 14 -> 18, of which waited for: 5 -> 6; matrix products, arithmetic and copies ran while one was open for 7% -> 7% of each run, Pallas kernels for 3% -> 3%
where the time goes in v5:
time: 157 us; the launch traced here: 156 us
  starting transfers between devices  76.3 us (49%)
  waiting for transfers between devices  38.6 us (25%)
  Pallas kernels  23.7 us (15%)
  local copies, waits for them, and re-layouts  12.1 us (8%)
  other arithmetic  4.08 us (3%)
    ppermute x6, starting transfers between devices, pass_on(): lax.ppermute(value, 'blk', [(i, (i + step) % ring) for i in range(ring)])  19.2 us
    pallas_call x1, Pallas kernels, body(): pl.pallas_call(solve_kernel, out_shape=(jax.ShapeDtypeStruct((3, cap, nod...  17.3 us
    all_to_all x1, waiting for transfers between devices, spread_network(): lax.all_to_all(jnp.broadcast_to(part[None], (depth * lines,) + part.shape...  16.1 us
    all_to_all x1, starting transfers between devices, spread_network(): lax.all_to_all(jnp.broadcast_to(part[None], (depth * lines,) + part.shape...  15.8 us
    ppermute x7, starting transfers between devices, swap_cores(): lax.ppermute(piece, 'core', [(0, 1), (1, 0)])  15.1 us
    all_to_all x1, starting transfers between devices, body(): lax.all_to_all(backward, RVE, split_axis=0, concat_axis=0, tiled=True)  13.7 us
    all_to_all x1, waiting for transfers between devices, body(): lax.all_to_all(backward, RVE, split_axis=0, concat_axis=0, tiled=True)  10 us
    ppermute x2, waiting for transfers between devices, from_behind(): return lax.ppermute(block, axis, route)  7.79 us
  transfers between devices with their start and end apart: 18, of which 6 were waited for; matrix products, arithmetic and copies ran while one was open for 7% of the time, Pallas kernels for 3%

profile of v5, /device:TPU:64, one launch (start us, length us, event | category | flops | bytes accessed | tf_op | source)
XLA Modules:
  0.0 156.2 jit_solution(9090208688073852639)
XLA Ops:
  3.8 3.4 %collective-permute-start = (f32[8,108]{1,0:T(8,128)S(1)}, f32[8,108]{1,0:T(8,128)S(1)}, u32[]{:S(2)}, u32[]{:S(2)}) collective-permute-start(f32[8,108]{1,0:T(8,128)S(1)} %concatenate.11.own_data_ref), channel_id=1, source_target_pairs={{0,1},{1,2},{2,3},{3,4},{4,5},{5,6},{6,7},{7,8},{8,9},{9,10},{10,1... | collective-permute-start | bytes 10376 | tf_op jit(solution)/shard_map/ppermute | solution.py:222
  9.6 15.8 %all-to-all-start = ((bf16[64,8,640]{2,1,0:T(8,128)(2,1)}), bf16[64,8,640]{2,1,0:T(8,128)(2,1)S(1)}, u32[]{:S(2)}, u32[]{:S(2)}) async-start(bf16[64,8,640]{2,1,0:T(8,128)(2,1)} %broadcast_in_dim.11), calls=%async_computation | async-start | bytes 1310720 | tf_op jit(solution)/shard_map/all_to_all | solution.py:238
  30.2 16.1 %all-to-all-done = bf16[64,8,640]{2,1,0:T(8,128)(2,1)S(1)} async-done(((bf16[64,8,640]{2,1,0:T(8,128)(2,1)}), bf16[64,8,640]{2,1,0:T(8,128)(2,1)S(1)}, u32[]{:S(2)}, u32[]{:S(2)}) %all-to-all-start) | async-done | bytes 655392 | tf_op jit(solution)/shard_map/all_to_all | solution.py:238
  46.3 1.9 %copy.29 = bf16[128,2,1088]{2,1,0:T(2,128)(2,1)} copy(bf16[128,2,1088]{0,2,1:T(8,128)(2,1)S(1)} %bitcast.26) | data formatting | bytes 1114112 | tf_op jit(solution)/shard_map/optimization_barrier | solution.py:246
  48.3 7.2 %all-to-all-start.1 = ((bf16[128,2,1088]{2,1,0:T(2,128)(2,1)}), bf16[128,2,1088]{2,1,0:T(2,128)(2,1)S(1)}, u32[]{:S(2)}, u32[]{:S(2)}) async-start(bf16[128,2,1088]{2,1,0:T(2,128)(2,1)} %copy.29), calls=%async_computation.1 | async-start | bytes 1179648 | tf_op jit(solution)/shard_map/all_to_all | solution.py:314
  55.6 4.4 %collective-permute-start.4 = (bf16[4,8,8,640]{3,2,1,0:T(8,128)(2,1)S(1)}, bf16[4,8,8,640]{3,2,1,0:T(8,128)(2,1)S(1)}, u32[]{:S(2)}, u32[]{:S(2)}) collective-permute-start(bf16[4,8,8,640]{3,2,1,0:T(8,128)(2,1)S(1)} %get-tuple-element.49), channel_id=1, source_target_pairs={{0,3},{1,0},{2,1},{3,2},{4,7},{5,4},{6,5},{7,6},{8,11},{9,8},{10,9... | collective-permute-start | bytes 983048 | tf_op jit(solution)/shard_map/ppermute | solution.py:244
  60.0 1.9 %collective-permute-start.1 = (bf16[4,8,8,640]{3,2,1,0:T(8,128)(2,1)S(1)}, bf16[4,8,8,640]{3,2,1,0:T(8,128)(2,1)S(1)}, u32[]{:S(2)}, u32[]{:S(2)}) collective-permute-start(bf16[4,8,8,640]{3,2,1,0:T(8,128)(2,1)S(1)} %get-tuple-element.50), channel_id=1, source_target_pairs={{0,1},{1,2},{2,3},{3,0},{4,5},{5,6},{6,7},{7,4},{8,9},{9,10},{10,1... | collective-permute-start | bytes 983048 | tf_op jit(solution)/shard_map/ppermute | solution.py:244
  61.9 2.9 %collective-permute-start.2 = (bf16[4,8,8,640]{3,2,1,0:T(8,128)(2,1)S(1)}, bf16[4,8,8,640]{3,2,1,0:T(8,128)(2,1)}, u32[]{:S(2)}, u32[]{:S(2)}) collective-permute-start(bf16[4,8,8,640]{3,2,1,0:T(8,128)(2,1)S(1)} %get-tuple-element.49), channel_id=1, source_target_pairs={{0,1},{1,2},{2,3},{3,0},{4,5},{5,6},{6,7},{7,4},{8,9},{9,10},{10,1... | collective-permute-start | bytes 983048 | tf_op jit(solution)/shard_map/ppermute | solution.py:244
  64.8 4.2 %collective-permute-start.3 = (bf16[4,8,8,640]{3,2,1,0:T(8,128)(2,1)S(1)}, bf16[4,8,8,640]{3,2,1,0:T(8,128)(2,1)S(1)}, u32[]{:S(2)}, u32[]{:S(2)}) collective-permute-start(bf16[4,8,8,640]{3,2,1,0:T(8,128)(2,1)S(1)} %get-tuple-element.50), channel_id=1, source_target_pairs={{0,3},{1,0},{2,1},{3,2},{4,7},{5,4},{6,5},{7,6},{8,11},{9,8},{10,9... | collective-permute-start | bytes 983048 | tf_op jit(solution)/shard_map/ppermute | solution.py:244
  69.0 3.9 %collective-permute-start.6 = (bf16[4,8,8,640]{3,2,1,0:T(8,128)(2,1)S(1)}, bf16[4,8,8,640]{3,2,1,0:T(8,128)(2,1)}, u32[]{:S(2)}, u32[]{:S(2)}) collective-permute-start(bf16[4,8,8,640]{3,2,1,0:T(8,128)(2,1)S(1)} %collective-permute-done.4.refs_4_), channel_id=1, source_target_pairs={{0,3},{1,0},{2,1},{3,2},{4,7},{5,4},{6,5},{7,6},{8,11},{9,8},{10,9... | collective-permute-start | bytes 983048 | tf_op jit(solution)/shard_map/ppermute | solution.py:244
  73.7 1.9 %collective-permute-start.5 = (bf16[4,8,8,640]{3,2,1,0:T(8,128)(2,1)S(1)}, bf16[4,8,8,640]{3,2,1,0:T(8,128)(2,1)}, u32[]{:S(2)}, u32[]{:S(2)}) collective-permute-start(bf16[4,8,8,640]{3,2,1,0:T(8,128)(2,1)S(1)} %collective-permute-done.1.refs_1_), channel_id=1, source_target_pairs={{0,1},{1,2},{2,3},{3,0},{4,5},{5,6},{6,7},{7,4},{8,9},{9,10},{10,1... | collective-permute-start | bytes 983048 | tf_op jit(solution)/shard_map/ppermute | solution.py:244
  75.6 1.9 %collective-permute-start.11 = (bf16[4,8,8,640]{3,2,1,0:T(8,128)(2,1)S(1)}, bf16[4,8,8,640]{3,2,1,0:T(8,128)(2,1)}, u32[]{:S(2)}, u32[]{:S(2)}) collective-permute-start(bf16[4,8,8,640]{3,2,1,0:T(8,128)(2,1)S(1)} %collective-permute-done.4.refs_4_), channel_id=1, source_target_pairs={{0,4},{4,0},{1,5},{5,1},{2,6},{6,2},{3,7},{7,3},{8,12},{12,8},{9,1... | collective-permute-start | bytes 983048 | tf_op jit(solution)/shard_map/ppermute | solution.py:257
  77.5 3.3 %collective-permute-done.2.refs_2_ = bf16[4,8,8,640]{3,2,1,0:T(8,128)(2,1)} collective-permute-done((bf16[4,8,8,640]{3,2,1,0:T(8,128)(2,1)S(1)}, bf16[4,8,8,640]{3,2,1,0:T(8,128)(2,1)}, u32[]{:S(2)}, u32[]{:S(2)}) %collective-permute-start.2) | collective-permute-done | bytes 327712 | tf_op jit(solution)/shard_map/ppermute | solution.py:244
  80.8 1.9 %collective-permute-start.7 = (bf16[8,8,8,640]{3,2,1,0:T(8,128)(2,1)S(1)}, bf16[8,8,8,640]{3,2,1,0:T(8,128)(2,1)S(1)}, u32[]{:S(2)}, u32[]{:S(2)}) collective-permute-start(bf16[8,8,8,640]{3,2,1,0:T(8,128)(2,1)S(1)} %bitcast.24), channel_id=1, source_target_pairs={{0,4},{4,0},{1,5},{5,1},{2,6},{6,2},{3,7},{7,3},{8,12},{12,8},{9,1... | collective-permute-start | bytes 1966088 | tf_op jit(solution)/shard_map/ppermute | solution.py:257
  82.8 2.4 %collective-permute-start.9 = (bf16[4,8,8,640]{3,2,1,0:T(8,128)(2,1)}, bf16[4,8,8,640]{3,2,1,0:T(8,128)(2,1)}, u32[]{:S(2)}, u32[]{:S(2)}) collective-permute-start(bf16[4,8,8,640]{3,2,1,0:T(8,128)(2,1)} %collective-permute-done.2.refs_2_), channel_id=1, source_target_pairs={{0,4},{4,0},{1,5},{5,1},{2,6},{6,2},{3,7},{7,3},{8,12},{12,8},{9,1... | collective-permute-start | bytes 983048 | tf_op jit(solution)/shard_map/ppermute | solution.py:257
  87.2 5.2 %prepare.1 = (bf16[264,3072]{1,0:T(8,128)(2,1)}, f32[3,88,2048]{2,1,0:T(8,128)}, f32[88,2048]{1,0:T(8,128)}) custom-call(bf16[88,128]{1,0:T(8,128)(2,1)} %get-tuple-element.30.pick_ref, f32[88,128]{1,0:T(8,128)} %get-tuple-element.31.unit_ref, bf16[128,2176]{1,0:T(8,128)(2,1)} %copy.31.arrived_ref, bf16[3,128,2048]{2,1,0:T(8,128)(2,1)} %pad.26.loading_ref, ...), custom_call_target="tpu_custom_call" | custom-call | tf_op jit(solution)/shard_map/prepare/pallas_call | solution.py:316
  92.4 1.9 %collective-permute-start.8 = (bf16[4,8,8,640]{3,2,1,0:T(8,128)(2,1)S(1)}, bf16[4,8,8,640]{3,2,1,0:T(8,128)(2,1)S(1)}, u32[]{:S(2)}, u32[]{:S(2)}) collective-permute-start(bf16[4,8,8,640]{3,2,1,0:T(8,128)(2,1)S(1)} %collective-permute-done.1.refs_1_), channel_id=1, source_target_pairs={{0,4},{4,0},{1,5},{5,1},{2,6},{6,2},{3,7},{7,3},{8,12},{12,8},{9,1... | collective-permute-start | bytes 983048 | tf_op jit(solution)/shard_map/ppermute | solution.py:257
  94.4 2.4 %collective-permute-start.10 = (bf16[4,8,8,640]{3,2,1,0:T(8,128)(2,1)S(1)}, bf16[4,8,8,640]{3,2,1,0:T(8,128)(2,1)S(1)}, u32[]{:S(2)}, u32[]{:S(2)}) collective-permute-start(bf16[4,8,8,640]{3,2,1,0:T(8,128)(2,1)S(1)} %copy-done.5), channel_id=1, source_target_pairs={{0,4},{4,0},{1,5},{5,1},{2,6},{6,2},{3,7},{7,3},{8,12},{12,8},{9,1... | collective-permute-start | bytes 983048 | tf_op jit(solution)/shard_map/ppermute | solution.py:257
  96.8 1.9 %collective-permute-start.12 = (bf16[4,8,8,640]{3,2,1,0:T(8,128)(2,1)}, bf16[4,8,8,640]{3,2,1,0:T(8,128)(2,1)S(1)}, u32[]{:S(2)}, u32[]{:S(2)}) collective-permute-start(bf16[4,8,8,640]{3,2,1,0:T(8,128)(2,1)} %collective-permute-done.5.refs_5_), channel_id=1, source_target_pairs={{0,4},{4,0},{1,5},{5,1},{2,6},{6,2},{3,7},{7,3},{8,12},{12,8},{9,1... | collective-permute-start | bytes 983048 | tf_op jit(solution)/shard_map/ppermute | solution.py:257
  98.7 2.6 %collective-permute-start.13 = (bf16[4,8,8,640]{3,2,1,0:T(8,128)(2,1)}, bf16[4,8,8,640]{3,2,1,0:T(8,128)(2,1)}, u32[]{:S(2)}, u32[]{:S(2)}) collective-permute-start(bf16[4,8,8,640]{3,2,1,0:T(8,128)(2,1)} %collective-permute-done.6.refs_6_), channel_id=1, source_target_pairs={{0,4},{4,0},{1,5},{5,1},{2,6},{6,2},{3,7},{7,3},{8,12},{12,8},{9,1... | collective-permute-start | bytes 983048 | tf_op jit(solution)/shard_map/ppermute | solution.py:257
  103.3 17.3 %solve.1 = (f32[3,81,2048]{2,1,0:T(8,128)}, f32[88,128]{1,0:T(8,128)}, f32[128,128]{1,0:T(8,128)}) custom-call(s32[2]{0:T(128)} %pad_add_fusion.side_ref, bf16[128,88]{1,0:T(8,128)(2,1)} %fusion.8.pick_ref, bf16[128,2048]{1,0:T(8,128)(2,1)} %pad.28.loading_ref, s32[81,1]{1,0:T(8,128)} %copy.32.occupied_ref, bf16[264,3072]{1,0:T(8,128)(2,1)} %get-tuple-element.34.press_hbm, ...), custom_call_target="tpu_custom_call" | custom-call | tf_op jit(solution)/shard_map/solve/pallas_call | solution.py:329
  120.5 13.7 %all-to-all-start.2 = ((f32[128,1,128]{2,1,0:T(1,128)}), f32[128,1,128]{2,1,0:T(1,128)S(1)}, u32[]{:S(2)}, u32[]{:S(2)}) async-start(f32[128,1,128]{2,1,0:T(1,128)} %bitcast.30), calls=%async_computation.2 | async-start | bytes 131072 | tf_op jit(solution)/shard_map/all_to_all | solution.py:357
  135.2 10.0 %all-to-all-done.2 = f32[128,1,128]{2,1,0:T(1,128)S(1)} async-done(((f32[128,1,128]{2,1,0:T(1,128)}), f32[128,1,128]{2,1,0:T(1,128)S(1)}, u32[]{:S(2)}, u32[]{:S(2)}) %all-to-all-start.2) | async-done | bytes 65568 | tf_op jit(solution)/shard_map/all_to_all | solution.py:357
  147.2 7.8 %collective-permute-done.14.behind_ref = f32[128,128]{1,0:T(8,128)S(1)} collective-permute-done((f32[128,128]{1,0:T(8,128)S(1)}, f32[128,128]{1,0:T(8,128)S(1)}, u32[]{:S(2)}, u32[]{:S(2)}) %collective-permute-start.14) | collective-permute-done | bytes 65568 | tf_op jit(solution)/shard_map/ppermute | solution.py:222
  (80 shorter events, 19.1 us)
Async XLA Ops:
  0.6 26.4 %copy-start.12 = (s32[27]{0:T(128)S(1)}, s32[27]{0:T(128)}, u32[]{:S(2)}) copy-start(s32[27]{0:T(128)} %param.16) | copy-start | bytes 328
  0.6 24.8 %copy-start.13 = (s32[81]{0:T(128)S(1)}, s32[81]{0:T(128)}, u32[]{:S(2)}) copy-start(s32[81]{0:T(128)} %param.17) | copy-start | bytes 976
  0.7 24.8 %copy-start.11 = (bf16[27,6]{0,1:T(8,128)(2,1)S(1)}, bf16[27,6]{0,1:T(8,128)(2,1)}, u32[]{:S(2)}) copy-start(bf16[27,6]{0,1:T(8,128)(2,1)} %param.11) | copy-start | bytes 976
  0.7 24.9 %copy-start.10 = (bf16[6,3,2048]{2,1,0:T(4,128)(2,1)S(1)}, bf16[6,3,2048]{2,1,0:T(4,128)(2,1)}, u32[]{:S(2)}) copy-start(bf16[6,3,2048]{2,1,0:T(4,128)(2,1)} %param.19) | copy-start | bytes 221188
  0.7 26.4 %copy-start.9 = (bf16[27,2048]{1,0:T(8,128)(2,1)S(1)}, bf16[27,2048]{1,0:T(8,128)(2,1)}, u32[]{:S(2)}) copy-start(bf16[27,2048]{1,0:T(8,128)(2,1)} %param.12) | copy-start | bytes 331780
  3.8 26.4 %collective-permute-start = (f32[8,108]{1,0:T(8,128)S(1)}, f32[8,108]{1,0:T(8,128)S(1)}, u32[]{:S(2)}, u32[]{:S(2)}) collective-permute-start(f32[8,108]{1,0:T(8,128)S(1)} %concatenate.11.own_data_ref), channel_id=1, source_target_pairs={{0,1},{1,2},{2,3},{3,4},{4,5},{5,6},{6,7},{7,8},{8,9},{9,10},{10,1... | collective-permute-start | bytes 10376 | tf_op jit(solution)/shard_map/ppermute | solution.py:222
  9.6 36.7 %all-to-all-start = ((bf16[64,8,640]{2,1,0:T(8,128)(2,1)}), bf16[64,8,640]{2,1,0:T(8,128)(2,1)S(1)}, u32[]{:S(2)}, u32[]{:S(2)}) async-start(bf16[64,8,640]{2,1,0:T(8,128)(2,1)} %broadcast_in_dim.11), calls=%async_computation | async-start | bytes 1310720 | tf_op jit(solution)/shard_map/all_to_all | solution.py:238
  46.3 39.8 %copy-start = (bf16[64,8,640]{2,1,0:T(8,128)(2,1)}, bf16[64,8,640]{2,1,0:T(8,128)(2,1)S(1)}, u32[]{:S(2)}) copy-start(bf16[64,8,640]{2,1,0:T(8,128)(2,1)S(1)} %all-to-all-done) | copy-start | bytes 1966084
  48.3 36.9 %all-to-all-start.1 = ((bf16[128,2,1088]{2,1,0:T(2,128)(2,1)}), bf16[128,2,1088]{2,1,0:T(2,128)(2,1)S(1)}, u32[]{:S(2)}, u32[]{:S(2)}) async-start(bf16[128,2,1088]{2,1,0:T(2,128)(2,1)} %copy.29), calls=%async_computation.1 | async-start | bytes 1179648 | tf_op jit(solution)/shard_map/all_to_all | solution.py:314
  55.6 13.4 %collective-permute-start.4 = (bf16[4,8,8,640]{3,2,1,0:T(8,128)(2,1)S(1)}, bf16[4,8,8,640]{3,2,1,0:T(8,128)(2,1)S(1)}, u32[]{:S(2)}, u32[]{:S(2)}) collective-permute-start(bf16[4,8,8,640]{3,2,1,0:T(8,128)(2,1)S(1)} %get-tuple-element.49), channel_id=1, source_target_pairs={{0,3},{1,0},{2,1},{3,2},{4,7},{5,4},{6,5},{7,6},{8,11},{9,8},{10,9... | collective-permute-start | bytes 983048 | tf_op jit(solution)/shard_map/ppermute | solution.py:244
  60.0 13.7 %collective-permute-start.1 = (bf16[4,8,8,640]{3,2,1,0:T(8,128)(2,1)S(1)}, bf16[4,8,8,640]{3,2,1,0:T(8,128)(2,1)S(1)}, u32[]{:S(2)}, u32[]{:S(2)}) collective-permute-start(bf16[4,8,8,640]{3,2,1,0:T(8,128)(2,1)S(1)} %get-tuple-element.50), channel_id=1, source_target_pairs={{0,1},{1,2},{2,3},{3,0},{4,5},{5,6},{6,7},{7,4},{8,9},{9,10},{10,1... | collective-permute-start | bytes 983048 | tf_op jit(solution)/shard_map/ppermute | solution.py:244
  61.9 18.9 %collective-permute-start.2 = (bf16[4,8,8,640]{3,2,1,0:T(8,128)(2,1)S(1)}, bf16[4,8,8,640]{3,2,1,0:T(8,128)(2,1)}, u32[]{:S(2)}, u32[]{:S(2)}) collective-permute-start(bf16[4,8,8,640]{3,2,1,0:T(8,128)(2,1)S(1)} %get-tuple-element.49), channel_id=1, source_target_pairs={{0,1},{1,2},{2,3},{3,0},{4,5},{5,6},{6,7},{7,4},{8,9},{9,10},{10,1... | collective-permute-start | bytes 983048 | tf_op jit(solution)/shard_map/ppermute | solution.py:244
  64.8 17.9 %collective-permute-start.3 = (bf16[4,8,8,640]{3,2,1,0:T(8,128)(2,1)S(1)}, bf16[4,8,8,640]{3,2,1,0:T(8,128)(2,1)S(1)}, u32[]{:S(2)}, u32[]{:S(2)}) collective-permute-start(bf16[4,8,8,640]{3,2,1,0:T(8,128)(2,1)S(1)} %get-tuple-element.50), channel_id=1, source_target_pairs={{0,3},{1,0},{2,1},{3,2},{4,7},{5,4},{6,5},{7,6},{8,11},{9,8},{10,9... | collective-permute-start | bytes 983048 | tf_op jit(solution)/shard_map/ppermute | solution.py:244
  69.0 23.4 %collective-permute-start.6 = (bf16[4,8,8,640]{3,2,1,0:T(8,128)(2,1)S(1)}, bf16[4,8,8,640]{3,2,1,0:T(8,128)(2,1)}, u32[]{:S(2)}, u32[]{:S(2)}) collective-permute-start(bf16[4,8,8,640]{3,2,1,0:T(8,128)(2,1)S(1)} %collective-permute-done.4.refs_4_), channel_id=1, source_target_pairs={{0,3},{1,0},{2,1},{3,2},{4,7},{5,4},{6,5},{7,6},{8,11},{9,8},{10,9... | collective-permute-start | bytes 983048 | tf_op jit(solution)/shard_map/ppermute | solution.py:244
  73.7 20.7 %collective-permute-start.5 = (bf16[4,8,8,640]{3,2,1,0:T(8,128)(2,1)S(1)}, bf16[4,8,8,640]{3,2,1,0:T(8,128)(2,1)}, u32[]{:S(2)}, u32[]{:S(2)}) collective-permute-start(bf16[4,8,8,640]{3,2,1,0:T(8,128)(2,1)S(1)} %collective-permute-done.1.refs_1_), channel_id=1, source_target_pairs={{0,1},{1,2},{2,3},{3,0},{4,5},{5,6},{6,7},{7,4},{8,9},{9,10},{10,1... | collective-permute-start | bytes 983048 | tf_op jit(solution)/shard_map/ppermute | solution.py:244
  75.6 21.2 %collective-permute-start.11 = (bf16[4,8,8,640]{3,2,1,0:T(8,128)(2,1)S(1)}, bf16[4,8,8,640]{3,2,1,0:T(8,128)(2,1)}, u32[]{:S(2)}, u32[]{:S(2)}) collective-permute-start(bf16[4,8,8,640]{3,2,1,0:T(8,128)(2,1)S(1)} %collective-permute-done.4.refs_4_), channel_id=1, source_target_pairs={{0,4},{4,0},{1,5},{5,1},{2,6},{6,2},{3,7},{7,3},{8,12},{12,8},{9,1... | collective-permute-start | bytes 983048 | tf_op jit(solution)/shard_map/ppermute | solution.py:257
  80.8 21.3 %collective-permute-start.7 = (bf16[8,8,8,640]{3,2,1,0:T(8,128)(2,1)S(1)}, bf16[8,8,8,640]{3,2,1,0:T(8,128)(2,1)S(1)}, u32[]{:S(2)}, u32[]{:S(2)}) collective-permute-start(bf16[8,8,8,640]{3,2,1,0:T(8,128)(2,1)S(1)} %bitcast.24), channel_id=1, source_target_pairs={{0,4},{4,0},{1,5},{5,1},{2,6},{6,2},{3,7},{7,3},{8,12},{12,8},{9,1... | collective-permute-start | bytes 1966088 | tf_op jit(solution)/shard_map/ppermute | solution.py:257
  82.8 16.0 %collective-permute-start.9 = (bf16[4,8,8,640]{3,2,1,0:T(8,128)(2,1)}, bf16[4,8,8,640]{3,2,1,0:T(8,128)(2,1)}, u32[]{:S(2)}, u32[]{:S(2)}) collective-permute-start(bf16[4,8,8,640]{3,2,1,0:T(8,128)(2,1)} %collective-permute-done.2.refs_2_), channel_id=1, source_target_pairs={{0,4},{4,0},{1,5},{5,1},{2,6},{6,2},{3,7},{7,3},{8,12},{12,8},{9,1... | collective-permute-start | bytes 983048 | tf_op jit(solution)/shard_map/ppermute | solution.py:257
  92.4 9.6 %collective-permute-start.8 = (bf16[4,8,8,640]{3,2,1,0:T(8,128)(2,1)S(1)}, bf16[4,8,8,640]{3,2,1,0:T(8,128)(2,1)S(1)}, u32[]{:S(2)}, u32[]{:S(2)}) collective-permute-start(bf16[4,8,8,640]{3,2,1,0:T(8,128)(2,1)S(1)} %collective-permute-done.1.refs_1_), channel_id=1, source_target_pairs={{0,4},{4,0},{1,5},{5,1},{2,6},{6,2},{3,7},{7,3},{8,12},{12,8},{9,1... | collective-permute-start | bytes 983048 | tf_op jit(solution)/shard_map/ppermute | solution.py:257
  94.4 7.7 %collective-permute-start.10 = (bf16[4,8,8,640]{3,2,1,0:T(8,128)(2,1)S(1)}, bf16[4,8,8,640]{3,2,1,0:T(8,128)(2,1)S(1)}, u32[]{:S(2)}, u32[]{:S(2)}) collective-permute-start(bf16[4,8,8,640]{3,2,1,0:T(8,128)(2,1)S(1)} %copy-done.5), channel_id=1, source_target_pairs={{0,4},{4,0},{1,5},{5,1},{2,6},{6,2},{3,7},{7,3},{8,12},{12,8},{9,1... | collective-permute-start | bytes 983048 | tf_op jit(solution)/shard_map/ppermute | solution.py:257
  96.8 5.3 %collective-permute-start.12 = (bf16[4,8,8,640]{3,2,1,0:T(8,128)(2,1)}, bf16[4,8,8,640]{3,2,1,0:T(8,128)(2,1)S(1)}, u32[]{:S(2)}, u32[]{:S(2)}) collective-permute-start(bf16[4,8,8,640]{3,2,1,0:T(8,128)(2,1)} %collective-permute-done.5.refs_5_), channel_id=1, source_target_pairs={{0,4},{4,0},{1,5},{5,1},{2,6},{6,2},{3,7},{7,3},{8,12},{12,8},{9,1... | collective-permute-start | bytes 983048 | tf_op jit(solution)/shard_map/ppermute | solution.py:257
  98.7 4.0 %collective-permute-start.13 = (bf16[4,8,8,640]{3,2,1,0:T(8,128)(2,1)}, bf16[4,8,8,640]{3,2,1,0:T(8,128)(2,1)}, u32[]{:S(2)}, u32[]{:S(2)}) collective-permute-start(bf16[4,8,8,640]{3,2,1,0:T(8,128)(2,1)} %collective-permute-done.6.refs_6_), channel_id=1, source_target_pairs={{0,4},{4,0},{1,5},{5,1},{2,6},{6,2},{3,7},{7,3},{8,12},{12,8},{9,1... | collective-permute-start | bytes 983048 | tf_op jit(solution)/shard_map/ppermute | solution.py:257
  120.5 24.7 %all-to-all-start.2 = ((f32[128,1,128]{2,1,0:T(1,128)}), f32[128,1,128]{2,1,0:T(1,128)S(1)}, u32[]{:S(2)}, u32[]{:S(2)}) async-start(f32[128,1,128]{2,1,0:T(1,128)} %bitcast.30), calls=%async_computation.2 | async-start | bytes 131072 | tf_op jit(solution)/shard_map/all_to_all | solution.py:357
  145.2 9.8 %collective-permute-start.14 = (f32[128,128]{1,0:T(8,128)S(1)}, f32[128,128]{1,0:T(8,128)S(1)}, u32[]{:S(2)}, u32[]{:S(2)}) collective-permute-start(f32[128,128]{1,0:T(8,128)S(1)} %bitcast.19), channel_id=1, source_target_pairs={{0,1},{1,2},{2,3},{3,4},{4,5},{5,6},{6,7},{7,8},{8,9},{9,10},{10,1... | collective-permute-start | bytes 196616 | tf_op jit(solution)/shard_map/ppermute | solution.py:222
  (8 other events, 55.5 us)

commit v6 on v5

--- a/solution.py
+++ b/solution.py
@@ -13,7 +13,7 @@
 SLICE = 256
 BLOCKS = 8
 SENT = 5
-PIECES = ((0, 0), (3, 0), (3, 1), (1, 0), (1, 1), (2, 0), (2, 1))
+PIECES = (0, 3, 1, 2)
 
 highest = lax.Precision.HIGHEST
 f32 = jnp.float32
@@ -75,12 +75,10 @@
     width = network.shape[4] // 2
 
     def fetch(k):
-        depth = shares[k].shape[0]
-        turn, late = PIECES[k % len(PIECES)]
         side = side_ref[0] if k < len(PIECES) else 1 - side_ref[0]
-        quarter = (side_ref[1] + turn) % 4
+        quarter = (side_ref[1] + PIECES[k % len(PIECES)]) % 4
         place = network.at[
-            pl.ds(late * (BLOCKS // 2), depth), :, side,
+            :, :, side,
             pl.ds(pl.multiple_of(quarter // 2 * half_rows, half_rows), half_rows),
             pl.ds(pl.multiple_of(quarter % 2 * width, width), width),
         ]
@@ -244,16 +242,13 @@
         return lax.ppermute(value, "blk", [(i, (i + step) % ring) for i in range(ring)])
 
     own, ready = lax.optimization_barrier((own, ready))
-    near, far = own[: depth // 2], own[depth // 2 :]
-    before_near, after_far = pass_on(near, 1), pass_on(far, -1)
-    pieces = [own, before_near, pass_on(far, 1), pass_on(near, -1), after_far]
-    pieces += [pass_on(before_near, 1), pass_on(after_far, -1)]
+    before, after = pass_on(own, 1), pass_on(own, -1)
+    pieces = [own, before, after, pass_on(before, 1)]
     return pieces, ready
 
 
 def swap_cores(pieces, ready):
-    last = list(lax.optimization_barrier((pieces[-2], pieces[-1], ready))[:2])
-    pieces = pieces[:-2] + last
+    pieces = pieces[:-1] + [lax.optimization_barrier((pieces[-1], ready))[0]]
     return pieces + [lax.ppermute(piece, "core", [(0, 1), (1, 0)]) for piece in pieces]
 
 
@@ -274,18 +269,6 @@
     send_pick = (worker_ids[:, None] == rve_worker[None, :]).astype(bf16)
     element_rows = jnp.concatenate([fiber_coeff, jnp.pad(strain, ((0, 0), (0, 128 - COMPS)))], axis=1)
     outgoing = jnp.dot(send_pick, element_rows).reshape(workers, 2, (nodes + 128) // 2)
-
-    corner_data = jnp.concatenate(
-        [
-            jnp.transpose(gradients.reshape(4, 3, elems), (1, 0, 2)).reshape(3, 4 * elems),
-            jnp.tile(volume, 4)[None, :],
-            (corners - device_rank * NODE_DEV).reshape(1, 4 * elems).astype(f32),
-            jnp.tile(rve_worker, 4)[None, :].astype(f32),
-            jnp.zeros((2, 4 * elems), f32),
-        ],
-        axis=0,
-    )
-    behind_data = from_behind(corner_data, ALL, 1)
 
     occupied = slot_element >= 0
     home = jnp.where(occupied, slot_element // (elems * columns), -1)
@@ -303,12 +286,12 @@
     pieces, ready = spread_network(
         compliance,
         (
-            outgoing, corner_data, behind_data, slot_pick, slot_pick.T, occupied.astype(jnp.int32)[:, None],
+            outgoing, slot_pick, slot_pick.T, occupied.astype(jnp.int32)[:, None],
             unit, loading_wide, loading_sums, place,
         ),
     )
     (
-        outgoing, corner_data, behind_data, slot_pick, slot_give, occupied_rows,
+        outgoing, slot_pick, slot_give, occupied_rows,
         unit, loading_wide, loading_sums, place,
     ) = ready
     arrived = lax.all_to_all(outgoing, RVE, split_axis=0, concat_axis=0, tiled=True).reshape(workers, nodes + 128)
@@ -355,8 +338,25 @@
     new_table = jnp.transpose(table, (1, 0, 2))
 
     returned = lax.all_to_all(backward, RVE, split_axis=0, concat_axis=0, tiled=True)
+    result, gradients, volume, corners, rve_worker = lax.optimization_barrier(
+        (result, gradients, volume, corners, rve_worker)
+    )
+    corner_data = jnp.concatenate(
+        [
+            jnp.transpose(gradients.reshape(4, 3, elems), (1, 0, 2)).reshape(3, 4 * elems),
+            jnp.tile(volume, 4)[None, :],
+            (corners - device_rank * NODE_DEV).reshape(1, 4 * elems).astype(f32),
+            jnp.tile(rve_worker, 4)[None, :].astype(f32),
+            jnp.zeros((2, 4 * elems), f32),
+        ],
+        axis=0,
+    )
+    behind_data = from_behind(corner_data, ALL, 1)
+
     fixed = jnp.pad(result[cap : cap + COMPS, 8 * COMPS + 1 : 8 * COMPS + 1 + COMPS], ((0, 0), (1, 1)))
-    fixed, returned = lax.optimization_barrier((fixed.reshape(8 * COMPS, 1), returned))
+    fixed, corner_data, behind_data, returned = lax.optimization_barrier(
+        (fixed.reshape(8 * COMPS, 1), corner_data, behind_data, returned)
+    )
     behind = from_behind(returned, ALL, 1)
     forces, blocks = pl.pallas_call(
         functools.partial(corner_kernel, scale=1.0 / (3 * nodes)),

time: 157 us -> 139 us (0.89)
  starting transfers between devices: 76.3 us -> 61.8 us
    ppermute x6 -> x3, starting transfers between devices: 19.2 us -> 9.19 us  [pass_on(): lax.ppermute(value, 'blk', [(i, (i + step) % ring) for i in range(ring)])]
    all_to_all x1, waiting for transfers between devices: 10 us -> 1.44 us  [body(): lax.all_to_all(backward, RVE, split_axis=0, concat_axis=0, tiled=True)]
    ppermute x7 -> x4, starting transfers between devices: 15.1 us -> 8.82 us  [swap_cores(): lax.ppermute(piece, 'core', [(0, 1), (1, 0)])]
    ppermute x6 -> x3, waiting for transfers between devices: 4.03 us -> 8.49 us  [pass_on(): lax.ppermute(value, 'blk', [(i, (i + step) % ring) for i in range(ring)])]
    ppermute x2, waiting for transfers between devices: 7.79 us -> 11.1 us  [from_behind(): return lax.ppermute(block, axis, route)]
  transfers between devices with their start and end apart: 18 -> 12, of which waited for: 6 -> 7; matrix products, arithmetic and copies ran while one was open for 7% -> 8% of each run, Pallas kernels for 3% -> 4%
where the time goes in v6:
time: 139 us; the launch traced here: 138 us
  starting transfers between devices  61.8 us (44%)
  waiting for transfers between devices  38.3 us (28%)
  Pallas kernels  23 us (17%)
  local copies, waits for them, and re-layouts  11.1 us (8%)
  other arithmetic  2.67 us (2%)
    pallas_call x1, Pallas kernels, body(): pl.pallas_call(solve_kernel, out_shape=(jax.ShapeDtypeStruct((3, cap, nod...  16.7 us
    all_to_all x1, waiting for transfers between devices, spread_network(): lax.all_to_all(jnp.broadcast_to(part[None], (depth * lines,) + part.shape...  16.3 us
    all_to_all x1, starting transfers between devices, spread_network(): lax.all_to_all(jnp.broadcast_to(part[None], (depth * lines,) + part.shape...  15.9 us
    all_to_all x1, starting transfers between devices, body(): lax.all_to_all(backward, RVE, split_axis=0, concat_axis=0, tiled=True)  13.7 us
    ppermute x2, waiting for transfers between devices, from_behind(): return lax.ppermute(block, axis, route)  11.1 us
    ppermute x3, starting transfers between devices, pass_on(): lax.ppermute(value, 'blk', [(i, (i + step) % ring) for i in range(ring)])  9.19 us
    ppermute x4, starting transfers between devices, swap_cores(): lax.ppermute(piece, 'core', [(0, 1), (1, 0)])  8.82 us
    ppermute x3, waiting for transfers between devices, pass_on(): lax.ppermute(value, 'blk', [(i, (i + step) % ring) for i in range(ring)])  8.49 us
  transfers between devices with their start and end apart: 12, of which 7 were waited for; matrix products, arithmetic and copies ran while one was open for 8% of the time, Pallas kernels for 4%

profile of v6, /device:TPU:64, one launch (start us, length us, event | category | flops | bytes accessed | tf_op | source)
XLA Modules:
  0.0 138.1 jit_solution(4120576121795057672)
XLA Ops:
  3.1 15.9 %all-to-all-start = ((bf16[64,8,640]{2,1,0:T(8,128)(2,1)}), bf16[64,8,640]{2,1,0:T(8,128)(2,1)S(1)}, u32[]{:S(2)}, u32[]{:S(2)}) async-start(bf16[64,8,640]{2,1,0:T(8,128)(2,1)} %broadcast_in_dim.11), calls=%async_computation | async-start | bytes 1310720 | tf_op jit(solution)/shard_map/all_to_all | solution.py:236
  19.3 1.3 pad.26.loading_ref
  23.8 16.3 %all-to-all-done = bf16[64,8,640]{2,1,0:T(8,128)(2,1)S(1)} async-done(((bf16[64,8,640]{2,1,0:T(8,128)(2,1)}), bf16[64,8,640]{2,1,0:T(8,128)(2,1)S(1)}, u32[]{:S(2)}, u32[]{:S(2)}) %all-to-all-start) | async-done | bytes 655392 | tf_op jit(solution)/shard_map/all_to_all | solution.py:236
  40.1 3.4 %collective-permute-start = (bf16[8,8,8,640]{3,2,1,0:T(8,128)(2,1)S(1)}, bf16[8,8,8,640]{3,2,1,0:T(8,128)(2,1)S(1)}, u32[]{:S(2)}, u32[]{:S(2)}) collective-permute-start(bf16[8,8,8,640]{3,2,1,0:T(8,128)(2,1)S(1)} %bitcast.23), channel_id=1, source_target_pairs={{0,1},{1,2},{2,3},{3,0},{4,5},{5,6},{6,7},{7,4},{8,9},{9,10},{10,1... | collective-permute-start | bytes 1966088 | tf_op jit(solution)/shard_map/ppermute | solution.py:242
  43.4 2.0 %copy.28 = bf16[128,2,1088]{2,1,0:T(2,128)(2,1)} copy(bf16[128,2,1088]{0,2,1:T(8,128)(2,1)S(1)} %bitcast.27) | data formatting | bytes 1114112 | tf_op jit(solution)/shard_map/optimization_barrier | solution.py:244
  45.4 7.3 %all-to-all-start.1 = ((bf16[128,2,1088]{2,1,0:T(2,128)(2,1)}), bf16[128,2,1088]{2,1,0:T(2,128)(2,1)S(1)}, u32[]{:S(2)}, u32[]{:S(2)}) async-start(bf16[128,2,1088]{2,1,0:T(2,128)(2,1)} %copy.28), calls=%async_computation.1 | async-start | bytes 1179648 | tf_op jit(solution)/shard_map/all_to_all | solution.py:297
  52.7 3.7 %collective-permute-start.1 = (bf16[8,8,8,640]{3,2,1,0:T(8,128)(2,1)S(1)}, bf16[8,8,8,640]{3,2,1,0:T(8,128)(2,1)S(1)}, u32[]{:S(2)}, u32[]{:S(2)}) collective-permute-start(bf16[8,8,8,640]{3,2,1,0:T(8,128)(2,1)S(1)} %bitcast.24), channel_id=1, source_target_pairs={{0,3},{1,0},{2,1},{3,2},{4,7},{5,4},{6,5},{7,6},{8,11},{9,8},{10,9... | collective-permute-start | bytes 1966088 | tf_op jit(solution)/shard_map/ppermute | solution.py:242
  56.4 1.0 collective-permute-done.refs_1_
  57.4 2.2 %collective-permute-start.2 = (bf16[8,8,8,640]{3,2,1,0:T(8,128)(2,1)S(1)}, bf16[8,8,8,640]{3,2,1,0:T(8,128)(2,1)}, u32[]{:S(2)}, u32[]{:S(2)}) collective-permute-start(bf16[8,8,8,640]{3,2,1,0:T(8,128)(2,1)S(1)} %collective-permute-done.refs_1_), channel_id=1, source_target_pairs={{0,1},{1,2},{2,3},{3,0},{4,5},{5,6},{6,7},{7,4},{8,9},{9,10},{10,1... | collective-permute-start | bytes 1966088 | tf_op jit(solution)/shard_map/ppermute | solution.py:242
  59.6 1.9 %collective-permute-start.3 = (bf16[8,8,8,640]{3,2,1,0:T(8,128)(2,1)S(1)}, bf16[8,8,8,640]{3,2,1,0:T(8,128)(2,1)}, u32[]{:S(2)}, u32[]{:S(2)}) collective-permute-start(bf16[8,8,8,640]{3,2,1,0:T(8,128)(2,1)S(1)} %bitcast.25), channel_id=1, source_target_pairs={{0,4},{4,0},{1,5},{5,1},{2,6},{6,2},{3,7},{7,3},{8,12},{12,8},{9,1... | collective-permute-start | bytes 1966088 | tf_op jit(solution)/shard_map/ppermute | solution.py:252
  61.5 2.4 %collective-permute-start.4 = (bf16[8,8,8,640]{3,2,1,0:T(8,128)(2,1)S(1)}, bf16[8,8,8,640]{3,2,1,0:T(8,128)(2,1)}, u32[]{:S(2)}, u32[]{:S(2)}) collective-permute-start(bf16[8,8,8,640]{3,2,1,0:T(8,128)(2,1)S(1)} %collective-permute-done.refs_1_), channel_id=1, source_target_pairs={{0,4},{4,0},{1,5},{5,1},{2,6},{6,2},{3,7},{7,3},{8,12},{12,8},{9,1... | collective-permute-start | bytes 1966088 | tf_op jit(solution)/shard_map/ppermute | solution.py:252
  63.9 7.5 %collective-permute-done.1.refs_2_ = bf16[8,8,8,640]{3,2,1,0:T(8,128)(2,1)S(1)} collective-permute-done((bf16[8,8,8,640]{3,2,1,0:T(8,128)(2,1)S(1)}, bf16[8,8,8,640]{3,2,1,0:T(8,128)(2,1)S(1)}, u32[]{:S(2)}, u32[]{:S(2)}) %collective-permute-start.1) | collective-permute-done | bytes 655392 | tf_op jit(solution)/shard_map/ppermute | solution.py:242
  71.4 1.9 %collective-permute-start.5 = (bf16[8,8,8,640]{3,2,1,0:T(8,128)(2,1)S(1)}, bf16[8,8,8,640]{3,2,1,0:T(8,128)(2,1)}, u32[]{:S(2)}, u32[]{:S(2)}) collective-permute-start(bf16[8,8,8,640]{3,2,1,0:T(8,128)(2,1)S(1)} %collective-permute-done.1.refs_2_), channel_id=1, source_target_pairs={{0,4},{4,0},{1,5},{5,1},{2,6},{6,2},{3,7},{7,3},{8,12},{12,8},{9,1... | collective-permute-start | bytes 1966088 | tf_op jit(solution)/shard_map/ppermute | solution.py:252
  74.3 1.1 copy.30.arrived_ref
  75.4 5.1 %prepare.1 = (bf16[264,3072]{1,0:T(8,128)(2,1)}, f32[3,88,2048]{2,1,0:T(8,128)}, f32[88,2048]{1,0:T(8,128)}) custom-call(bf16[88,128]{1,0:T(8,128)(2,1)} %get-tuple-element.34.pick_ref, f32[88,128]{1,0:T(8,128)} %get-tuple-element.35.unit_ref, bf16[128,2176]{1,0:T(8,128)(2,1)} %copy.30.arrived_ref, bf16[3,128,2048]{2,1,0:T(8,128)(2,1)} %pad.26.loading_ref, ...), custom_call_target="tpu_custom_call" | custom-call | tf_op jit(solution)/shard_map/prepare/pallas_call | solution.py:299
  80.5 2.6 %collective-permute-start.6 = (bf16[8,8,8,640]{3,2,1,0:T(8,128)(2,1)}, bf16[8,8,8,640]{3,2,1,0:T(8,128)(2,1)S(1)}, u32[]{:S(2)}, u32[]{:S(2)}) collective-permute-start(bf16[8,8,8,640]{3,2,1,0:T(8,128)(2,1)} %collective-permute-done.2.refs_3_), channel_id=1, source_target_pairs={{0,4},{4,0},{1,5},{5,1},{2,6},{6,2},{3,7},{7,3},{8,12},{12,8},{9,1... | collective-permute-start | bytes 1966088 | tf_op jit(solution)/shard_map/ppermute | solution.py:252
  85.7 16.7 %solve.1 = (f32[3,81,2048]{2,1,0:T(8,128)}, f32[88,128]{1,0:T(8,128)}, f32[128,128]{1,0:T(8,128)}) custom-call(s32[2]{0:T(128)} %pad_add_fusion.side_ref, bf16[128,88]{1,0:T(8,128)(2,1)} %fusion.8.pick_ref, bf16[128,2048]{1,0:T(8,128)(2,1)} %pad.28.loading_ref, s32[81,1]{1,0:T(8,128)} %copy.31.occupied_ref, bf16[264,3072]{1,0:T(8,128)(2,1)} %get-tuple-element.38.press_hbm, ...), custom_call_target="tpu_custom_call" | custom-call | tf_op jit(solution)/shard_map/solve/pallas_call | solution.py:312
  102.4 13.7 %all-to-all-start.2 = ((f32[128,1,128]{2,1,0:T(1,128)}), f32[128,1,128]{2,1,0:T(1,128)S(1)}, u32[]{:S(2)}, u32[]{:S(2)}) async-start(f32[128,1,128]{2,1,0:T(1,128)} %bitcast.31), calls=%async_computation.2 | async-start | bytes 131072 | tf_op jit(solution)/shard_map/all_to_all | solution.py:340
  116.5 3.4 %collective-permute-start.7 = (f32[8,108]{1,0:T(8,128)S(1)}, f32[8,108]{1,0:T(8,128)S(1)}, u32[]{:S(2)}, u32[]{:S(2)}) collective-permute-start(f32[8,108]{1,0:T(8,128)S(1)} %concatenate.11.own_data_ref), channel_id=1, source_target_pairs={{0,1},{1,2},{2,3},{3,4},{4,5},{5,6},{6,7},{7,8},{8,9},{9,10},{10,1... | collective-permute-start | bytes 10376 | tf_op jit(solution)/shard_map/ppermute | solution.py:220
  120.9 4.8 %collective-permute-done.7.behind_data_ref = f32[8,108]{1,0:T(8,128)S(1)} collective-permute-done((f32[8,108]{1,0:T(8,128)S(1)}, f32[8,108]{1,0:T(8,128)S(1)}, u32[]{:S(2)}, u32[]{:S(2)}) %collective-permute-start.7) | collective-permute-done | bytes 3488 | tf_op jit(solution)/shard_map/ppermute | solution.py:220
  125.7 1.4 %all-to-all-done.2 = f32[128,1,128]{2,1,0:T(1,128)S(1)} async-done(((f32[128,1,128]{2,1,0:T(1,128)}), f32[128,1,128]{2,1,0:T(1,128)S(1)}, u32[]{:S(2)}, u32[]{:S(2)}) %all-to-all-start.2) | async-done | bytes 65568 | tf_op jit(solution)/shard_map/all_to_all | solution.py:340
  127.1 3.4 %collective-permute-start.8 = (f32[128,128]{1,0:T(8,128)S(1)}, f32[128,128]{1,0:T(8,128)S(1)}, u32[]{:S(2)}, u32[]{:S(2)}) collective-permute-start(f32[128,128]{1,0:T(8,128)S(1)} %bitcast.19), channel_id=1, source_target_pairs={{0,1},{1,2},{2,3},{3,4},{4,5},{5,6},{6,7},{7,8},{8,9},{9,10},{10,1... | collective-permute-start | bytes 196616 | tf_op jit(solution)/shard_map/ppermute | solution.py:220
  130.6 6.3 %collective-permute-done.8.behind_ref = f32[128,128]{1,0:T(8,128)S(1)} collective-permute-done((f32[128,128]{1,0:T(8,128)S(1)}, f32[128,128]{1,0:T(8,128)S(1)}, u32[]{:S(2)}, u32[]{:S(2)}) %collective-permute-start.8) | collective-permute-done | bytes 65568 | tf_op jit(solution)/shard_map/ppermute | solution.py:220
  136.9 1.2 corners.1
  (63 shorter events, 10.7 us)
Async XLA Ops:
  0.6 18.4 %copy-start.11 = (s32[81]{0:T(128)S(1)}, s32[81]{0:T(128)}, u32[]{:S(2)}) copy-start(s32[81]{0:T(128)} %param.17) | copy-start | bytes 976
  0.6 18.4 %copy-start.7 = (bf16[27,6]{0,1:T(8,128)(2,1)S(1)}, bf16[27,6]{0,1:T(8,128)(2,1)}, u32[]{:S(2)}) copy-start(bf16[27,6]{0,1:T(8,128)(2,1)} %param.11) | copy-start | bytes 976
  0.7 18.5 %copy-start.5 = (bf16[6,3,2048]{2,1,0:T(4,128)(2,1)S(1)}, bf16[6,3,2048]{2,1,0:T(4,128)(2,1)}, u32[]{:S(2)}) copy-start(bf16[6,3,2048]{2,1,0:T(4,128)(2,1)} %param.19) | copy-start | bytes 221188
  3.1 20.3 %copy-start.4 = (bf16[27,2048]{1,0:T(8,128)(2,1)S(1)}, bf16[27,2048]{1,0:T(8,128)(2,1)}, u32[]{:S(2)}) copy-start(bf16[27,2048]{1,0:T(8,128)(2,1)} %param.12) | copy-start | bytes 331780
  3.1 20.3 %copy-start.9 = (s32[27]{0:T(128)S(1)}, s32[27]{0:T(128)}, u32[]{:S(2)}) copy-start(s32[27]{0:T(128)} %param.16) | copy-start | bytes 328
  3.1 37.0 %all-to-all-start = ((bf16[64,8,640]{2,1,0:T(8,128)(2,1)}), bf16[64,8,640]{2,1,0:T(8,128)(2,1)S(1)}, u32[]{:S(2)}, u32[]{:S(2)}) async-start(bf16[64,8,640]{2,1,0:T(8,128)(2,1)} %broadcast_in_dim.11), calls=%async_computation | async-start | bytes 1310720 | tf_op jit(solution)/shard_map/all_to_all | solution.py:236
  40.1 35.3 %copy-start = (bf16[64,8,640]{2,1,0:T(8,128)(2,1)}, bf16[64,8,640]{2,1,0:T(8,128)(2,1)S(1)}, u32[]{:S(2)}) copy-start(bf16[64,8,640]{2,1,0:T(8,128)(2,1)S(1)} %all-to-all-done) | copy-start | bytes 1966084
  40.1 17.3 %collective-permute-start = (bf16[8,8,8,640]{3,2,1,0:T(8,128)(2,1)S(1)}, bf16[8,8,8,640]{3,2,1,0:T(8,128)(2,1)S(1)}, u32[]{:S(2)}, u32[]{:S(2)}) collective-permute-start(bf16[8,8,8,640]{3,2,1,0:T(8,128)(2,1)S(1)} %bitcast.23), channel_id=1, source_target_pairs={{0,1},{1,2},{2,3},{3,0},{4,5},{5,6},{6,7},{7,4},{8,9},{9,10},{10,1... | collective-permute-start | bytes 1966088 | tf_op jit(solution)/shard_map/ppermute | solution.py:242
  45.4 27.9 %all-to-all-start.1 = ((bf16[128,2,1088]{2,1,0:T(2,128)(2,1)}), bf16[128,2,1088]{2,1,0:T(2,128)(2,1)S(1)}, u32[]{:S(2)}, u32[]{:S(2)}) async-start(bf16[128,2,1088]{2,1,0:T(2,128)(2,1)} %copy.28), calls=%async_computation.1 | async-start | bytes 1179648 | tf_op jit(solution)/shard_map/all_to_all | solution.py:297
  52.7 18.7 %collective-permute-start.1 = (bf16[8,8,8,640]{3,2,1,0:T(8,128)(2,1)S(1)}, bf16[8,8,8,640]{3,2,1,0:T(8,128)(2,1)S(1)}, u32[]{:S(2)}, u32[]{:S(2)}) collective-permute-start(bf16[8,8,8,640]{3,2,1,0:T(8,128)(2,1)S(1)} %bitcast.24), channel_id=1, source_target_pairs={{0,3},{1,0},{2,1},{3,2},{4,7},{5,4},{6,5},{7,6},{8,11},{9,8},{10,9... | collective-permute-start | bytes 1966088 | tf_op jit(solution)/shard_map/ppermute | solution.py:242
  57.4 23.1 %copy-start.1 = (bf16[8,8,8,640]{3,2,1,0:T(8,128)(2,1)}, bf16[8,8,8,640]{3,2,1,0:T(8,128)(2,1)S(1)}, u32[]{:S(2)}) copy-start(bf16[8,8,8,640]{3,2,1,0:T(8,128)(2,1)S(1)} %collective-permute-done.refs_1_) | copy-start | bytes 1966084
  57.4 23.1 %collective-permute-start.2 = (bf16[8,8,8,640]{3,2,1,0:T(8,128)(2,1)S(1)}, bf16[8,8,8,640]{3,2,1,0:T(8,128)(2,1)}, u32[]{:S(2)}, u32[]{:S(2)}) collective-permute-start(bf16[8,8,8,640]{3,2,1,0:T(8,128)(2,1)S(1)} %collective-permute-done.refs_1_), channel_id=1, source_target_pairs={{0,1},{1,2},{2,3},{3,0},{4,5},{5,6},{6,7},{7,4},{8,9},{9,10},{10,1... | collective-permute-start | bytes 1966088 | tf_op jit(solution)/shard_map/ppermute | solution.py:242
  59.6 24.2 %collective-permute-start.3 = (bf16[8,8,8,640]{3,2,1,0:T(8,128)(2,1)S(1)}, bf16[8,8,8,640]{3,2,1,0:T(8,128)(2,1)}, u32[]{:S(2)}, u32[]{:S(2)}) collective-permute-start(bf16[8,8,8,640]{3,2,1,0:T(8,128)(2,1)S(1)} %bitcast.25), channel_id=1, source_target_pairs={{0,4},{4,0},{1,5},{5,1},{2,6},{6,2},{3,7},{7,3},{8,12},{12,8},{9,1... | collective-permute-start | bytes 1966088 | tf_op jit(solution)/shard_map/ppermute | solution.py:252
  61.5 22.3 %collective-permute-start.4 = (bf16[8,8,8,640]{3,2,1,0:T(8,128)(2,1)S(1)}, bf16[8,8,8,640]{3,2,1,0:T(8,128)(2,1)}, u32[]{:S(2)}, u32[]{:S(2)}) collective-permute-start(bf16[8,8,8,640]{3,2,1,0:T(8,128)(2,1)S(1)} %collective-permute-done.refs_1_), channel_id=1, source_target_pairs={{0,4},{4,0},{1,5},{5,1},{2,6},{6,2},{3,7},{7,3},{8,12},{12,8},{9,1... | collective-permute-start | bytes 1966088 | tf_op jit(solution)/shard_map/ppermute | solution.py:252
  71.4 9.1 %copy-start.2 = (bf16[8,8,8,640]{3,2,1,0:T(8,128)(2,1)}, bf16[8,8,8,640]{3,2,1,0:T(8,128)(2,1)S(1)}, u32[]{:S(2)}) copy-start(bf16[8,8,8,640]{3,2,1,0:T(8,128)(2,1)S(1)} %collective-permute-done.1.refs_2_) | copy-start | bytes 1966084
  71.4 12.4 %collective-permute-start.5 = (bf16[8,8,8,640]{3,2,1,0:T(8,128)(2,1)S(1)}, bf16[8,8,8,640]{3,2,1,0:T(8,128)(2,1)}, u32[]{:S(2)}, u32[]{:S(2)}) collective-permute-start(bf16[8,8,8,640]{3,2,1,0:T(8,128)(2,1)S(1)} %collective-permute-done.1.refs_2_), channel_id=1, source_target_pairs={{0,4},{4,0},{1,5},{5,1},{2,6},{6,2},{3,7},{7,3},{8,12},{12,8},{9,1... | collective-permute-start | bytes 1966088 | tf_op jit(solution)/shard_map/ppermute | solution.py:252
  80.5 4.3 %collective-permute-start.6 = (bf16[8,8,8,640]{3,2,1,0:T(8,128)(2,1)}, bf16[8,8,8,640]{3,2,1,0:T(8,128)(2,1)S(1)}, u32[]{:S(2)}, u32[]{:S(2)}) collective-permute-start(bf16[8,8,8,640]{3,2,1,0:T(8,128)(2,1)} %collective-permute-done.2.refs_3_), channel_id=1, source_target_pairs={{0,4},{4,0},{1,5},{5,1},{2,6},{6,2},{3,7},{7,3},{8,12},{12,8},{9,1... | collective-permute-start | bytes 1966088 | tf_op jit(solution)/shard_map/ppermute | solution.py:252
  84.8 0.8 copy-start.3
  85.7 30.5 %copy-start.8 = (s32[4,27]{1,0:T(4,128)S(1)}, s32[4,27]{1,0:T(4,128)}, u32[]{:S(2)}) copy-start(s32[4,27]{1,0:T(4,128)} %param.15) | copy-start | bytes 1300
  85.7 30.6 %copy-start.10 = (f32[27]{0:T(128)S(1)}, f32[27]{0:T(128)}, u32[]{:S(2)}) copy-start(f32[27]{0:T(128)} %param.14) | copy-start | bytes 328
  85.7 30.7 %copy-start.6 = (f32[12,27]{1,0:T(8,128)S(1)}, f32[12,27]{1,0:T(8,128)}, u32[]{:S(2)}) copy-start(f32[12,27]{1,0:T(8,128)} %param.13) | copy-start | bytes 3892
  102.4 24.7 %all-to-all-start.2 = ((f32[128,1,128]{2,1,0:T(1,128)}), f32[128,1,128]{2,1,0:T(1,128)S(1)}, u32[]{:S(2)}, u32[]{:S(2)}) async-start(f32[128,1,128]{2,1,0:T(1,128)} %bitcast.31), calls=%async_computation.2 | async-start | bytes 131072 | tf_op jit(solution)/shard_map/all_to_all | solution.py:340
  116.5 9.2 %collective-permute-start.7 = (f32[8,108]{1,0:T(8,128)S(1)}, f32[8,108]{1,0:T(8,128)S(1)}, u32[]{:S(2)}, u32[]{:S(2)}) collective-permute-start(f32[8,108]{1,0:T(8,128)S(1)} %concatenate.11.own_data_ref), channel_id=1, source_target_pairs={{0,1},{1,2},{2,3},{3,4},{4,5},{5,6},{6,7},{7,8},{8,9},{9,10},{10,1... | collective-permute-start | bytes 10376 | tf_op jit(solution)/shard_map/ppermute | solution.py:220
  127.1 9.8 %collective-permute-start.8 = (f32[128,128]{1,0:T(8,128)S(1)}, f32[128,128]{1,0:T(8,128)S(1)}, u32[]{:S(2)}, u32[]{:S(2)}) collective-permute-start(f32[128,128]{1,0:T(8,128)S(1)} %bitcast.19), channel_id=1, source_target_pairs={{0,1},{1,2},{2,3},{3,4},{4,5},{5,6},{6,7},{7,8},{8,9},{9,10},{10,1... | collective-permute-start | bytes 196616 | tf_op jit(solution)/shard_map/ppermute | solution.py:220

commit v7 on v6

--- a/solution.py
+++ b/solution.py
@@ -26,6 +26,10 @@
 
 def dot_nn(left, right):
     return lax.dot_general(left, right, (((1,), (0,)), ((), ())), preferred_element_type=f32)
+
+
+def dot_tn(left, right):
+    return lax.dot_general(left, right, (((0,), (0,)), ((), ())), preferred_element_type=f32)
 
 
 def dot_nt(left, right):
@@ -61,11 +65,11 @@
 
 
 def solve_kernel(
-    side_ref, pick_ref, loading_ref, occupied_ref, press_hbm, forcing_hbm, fiber_hbm, state_hbm, *refs,
+    side_ref, pick_ref, loading_hbm, press_hbm, forcing_hbm, fiber_hbm, state_hbm, *refs,
 ):
     shares = refs[: 2 * len(PIECES)]
     (
-        table_hbm, result_ref, back_ref, network, pressure, forcing, fiber, table, damp_sum, stress_sum,
+        table_hbm, result_ref, back_ref, network, pressure, forcing, fiber, table, loading, damp_sum, stress_sum,
         net_sems, in_sems, out_sems,
     ) = refs[2 * len(PIECES) :]
     rows = fiber.shape[0]
@@ -89,6 +93,7 @@
         pltpu.make_async_copy(forcing_hbm, forcing, in_sems.at[1]),
         pltpu.make_async_copy(fiber_hbm, fiber, in_sems.at[2]),
         pltpu.make_async_copy(state_hbm, table, in_sems.at[3]),
+        pltpu.make_async_copy(loading_hbm, loading, in_sems.at[4]),
     )
     inputs[0].start()
     for k in range(2 * len(PIECES)):
@@ -107,6 +112,7 @@
             out_sems.at[n],
         )
 
+    occupied = jnp.sum(pick_ref[...].astype(f32), axis=1, keepdims=True)[0:cap] > 0.0
     damp_sum[...] = jnp.zeros_like(damp_sum)
     stress_sum[...] = jnp.zeros_like(stress_sum)
     inputs[0].wait()
@@ -136,11 +142,12 @@
                 continue
             if step == 0:
                 inputs[3].wait()
+                inputs[4].wait()
             products = []
             for a in range(3):
                 low = a * rows
                 table[a, :, cols] = jnp.where(
-                    occupied_ref[...] > 0, moved[low : low + cap], table[a, :, cols]
+                    occupied, moved[low : low + cap], table[a, :, cols]
                 )
                 basis = moved[low + rows - 8 : low + rows]
                 products += [basis * basis[k : k + 1] for k in range(1, COMPS + 1)]
@@ -151,7 +158,7 @@
             damp_sum[...] += dot_nt(damped, weights)
             head = moved.astype(bf16)
             rest = (moved - head.astype(f32)).astype(bf16)
-            load = loading_ref[:, cols]
+            load = loading[:, cols]
             stress_sum[...] += dot_nt(head, load) + dot_nt(rest, load)
 
     def gathered(sums, shift):
@@ -169,7 +176,7 @@
     result_ref[...] = result
     pick = pick_ref[...]
     head, middle, rest = three_parts(result)
-    back_ref[...] = dot_nn(pick, head) + (dot_nn(pick, middle) + dot_nn(pick, rest))
+    back_ref[...] = dot_tn(pick, head) + (dot_tn(pick, middle) + dot_tn(pick, rest))
     for n in range(BLOCKS):
         stored(n).wait()
 
@@ -286,12 +293,12 @@
     pieces, ready = spread_network(
         compliance,
         (
-            outgoing, slot_pick, slot_pick.T, occupied.astype(jnp.int32)[:, None],
+            outgoing, slot_pick,
             unit, loading_wide, loading_sums, place,
         ),
     )
     (
-        outgoing, slot_pick, slot_give, occupied_rows,
+        outgoing, slot_pick,
         unit, loading_wide, loading_sums, place,
     ) = ready
     arrived = lax.all_to_all(outgoing, RVE, split_axis=0, concat_axis=0, tiled=True).reshape(workers, nodes + 128)
@@ -306,7 +313,7 @@
         scratch_shapes=[pltpu.VMEM((rows, SLICE), f32)],
         name="prepare",
     )(slot_pick, unit, arrived, loading_wide, states)
-    shares = swap_cores(pieces, press)
+    shares = swap_cores(pieces, arrived)
     vmem = pl.BlockSpec(memory_space=pltpu.VMEM)
     hbm = pl.BlockSpec(memory_space=pltpu.HBM)
     table, result, backward = pl.pallas_call(
@@ -316,7 +323,7 @@
             jax.ShapeDtypeStruct((rows, 128), f32),
             jax.ShapeDtypeStruct((workers, 128), f32),
         ),
-        in_specs=[pl.BlockSpec(memory_space=pltpu.SMEM)] + [vmem] * 3 + [hbm] * (4 + 2 * len(PIECES)),
+        in_specs=[pl.BlockSpec(memory_space=pltpu.SMEM)] + [vmem] + [hbm] * (5 + 2 * len(PIECES)),
         out_specs=(hbm, vmem, vmem),
         scratch_shapes=[
             pltpu.VMEM((BLOCKS, lax.axis_size("y"), 2, compliance.shape[0], SENT * SLICE), bf16),
@@ -324,16 +331,16 @@
             pltpu.VMEM((3, rows, nodes), f32),
             pltpu.VMEM((rows, nodes), f32),
             pltpu.VMEM((3, cap, nodes), f32),
+            pltpu.VMEM((128, nodes), bf16),
             pltpu.VMEM((3 * rows, 256), f32),
             pltpu.VMEM((3 * rows, 128), f32),
             pltpu.SemaphoreType.DMA((2 * len(PIECES),)),
-            pltpu.SemaphoreType.DMA((4,)),
+            pltpu.SemaphoreType.DMA((5,)),
             pltpu.SemaphoreType.DMA((BLOCKS,)),
         ],
         name="solve",
     )(
-        place, slot_give, loading_sums,
-        occupied_rows, press, forcing, fiber, states, *shares,
+        place, slot_pick, loading_sums, press, forcing, fiber, states, *shares,
     )
     new_table = jnp.transpose(table, (1, 0, 2))
 

time: 139 us -> 138 us (level)
  waiting for transfers between devices: 38.3 us -> 42.7 us
  starting transfers between devices: 61.8 us -> 58.5 us
  local copies, waits for them, and re-layouts: 11.1 us -> 9.5 us
    ppermute x2, waiting for transfers between devices: 11.1 us -> 14 us  [from_behind(): return lax.ppermute(block, axis, route)]
    ppermute x2, starting transfers between devices: 6.85 us -> 3.92 us  [from_behind(): return lax.ppermute(block, axis, route)]
    ppermute x3, waiting for transfers between devices: 8.49 us -> 10.3 us  [pass_on(): lax.ppermute(value, 'blk', [(i, (i + step) % ring) for i in range(ring)])]
  transfers between devices with their start and end apart: 12 -> 12, of which waited for: 7 -> 7; matrix products, arithmetic and copies ran while one was open for 8% -> 7% of each run, Pallas kernels for 4% -> 4%
where the time goes in v7:
time: 138 us; the launch traced here: 137 us
  starting transfers between devices  58.5 us (42%)
  waiting for transfers between devices  42.7 us (31%)
  Pallas kernels  22.8 us (17%)
  local copies, waits for them, and re-layouts  9.5 us (7%)
  other arithmetic  2.12 us (2%)
    all_to_all x1, waiting for transfers between devices, spread_network(): lax.all_to_all(jnp.broadcast_to(part[None], (depth * lines,) + part.shape...  16.9 us
    pallas_call x1, Pallas kernels, body(): pl.pallas_call(solve_kernel, out_shape=(jax.ShapeDtypeStruct((3, cap, nod...  16.5 us
    all_to_all x1, starting transfers between devices, spread_network(): lax.all_to_all(jnp.broadcast_to(part[None], (depth * lines,) + part.shape...  15.9 us
    ppermute x2, waiting for transfers between devices, from_behind(): return lax.ppermute(block, axis, route)  14 us
    all_to_all x1, starting transfers between devices, body(): lax.all_to_all(backward, RVE, split_axis=0, concat_axis=0, tiled=True)  13.8 us
    ppermute x3, waiting for transfers between devices, pass_on(): lax.ppermute(value, 'blk', [(i, (i + step) % ring) for i in range(ring)])  10.3 us
    ppermute x3, starting transfers between devices, pass_on(): lax.ppermute(value, 'blk', [(i, (i + step) % ring) for i in range(ring)])  9.19 us
    ppermute x4, starting transfers between devices, swap_cores(): lax.ppermute(piece, 'core', [(0, 1), (1, 0)])  8.33 us
  transfers between devices with their start and end apart: 12, of which 7 were waited for; matrix products, arithmetic and copies ran while one was open for 7% of the time, Pallas kernels for 4%

profile of v7, /device:TPU:64, one launch (start us, length us, event | category | flops | bytes accessed | tf_op | source)
XLA Modules:
  0.0 136.9 jit_solution(447801803707719169)
XLA Ops:
  3.1 15.9 %all-to-all-start = ((bf16[64,8,640]{2,1,0:T(8,128)(2,1)}), bf16[64,8,640]{2,1,0:T(8,128)(2,1)S(1)}, u32[]{:S(2)}, u32[]{:S(2)}) async-start(bf16[64,8,640]{2,1,0:T(8,128)(2,1)} %broadcast_in_dim.6), calls=%async_computation | async-start | bytes 1310720 | tf_op jit(solution)/shard_map/all_to_all | solution.py:243
  19.3 1.3 pad.26.loading_ref
  23.2 16.9 %all-to-all-done = bf16[64,8,640]{2,1,0:T(8,128)(2,1)S(1)} async-done(((bf16[64,8,640]{2,1,0:T(8,128)(2,1)}), bf16[64,8,640]{2,1,0:T(8,128)(2,1)S(1)}, u32[]{:S(2)}, u32[]{:S(2)}) %all-to-all-start) | async-done | bytes 655392 | tf_op jit(solution)/shard_map/all_to_all | solution.py:243
  40.1 3.4 %collective-permute-start = (bf16[8,8,8,640]{3,2,1,0:T(8,128)(2,1)S(1)}, bf16[8,8,8,640]{3,2,1,0:T(8,128)(2,1)S(1)}, u32[]{:S(2)}, u32[]{:S(2)}) collective-permute-start(bf16[8,8,8,640]{3,2,1,0:T(8,128)(2,1)S(1)} %bitcast.21), channel_id=1, source_target_pairs={{0,1},{1,2},{2,3},{3,0},{4,5},{5,6},{6,7},{7,4},{8,9},{9,10},{10,1... | collective-permute-start | bytes 1966088 | tf_op jit(solution)/shard_map/ppermute | solution.py:249
  43.4 2.0 %copy.26 = bf16[128,2,1088]{2,1,0:T(2,128)(2,1)} copy(bf16[128,2,1088]{0,2,1:T(8,128)(2,1)S(1)} %bitcast.26) | data formatting | bytes 1114112 | tf_op jit(solution)/shard_map/optimization_barrier | solution.py:251
  45.4 7.3 %all-to-all-start.1 = ((bf16[128,2,1088]{2,1,0:T(2,128)(2,1)}), bf16[128,2,1088]{2,1,0:T(2,128)(2,1)S(1)}, u32[]{:S(2)}, u32[]{:S(2)}) async-start(bf16[128,2,1088]{2,1,0:T(2,128)(2,1)} %copy.26), calls=%async_computation.1 | async-start | bytes 1179648 | tf_op jit(solution)/shard_map/all_to_all | solution.py:304
  52.7 3.7 %collective-permute-start.1 = (bf16[8,8,8,640]{3,2,1,0:T(8,128)(2,1)S(1)}, bf16[8,8,8,640]{3,2,1,0:T(8,128)(2,1)S(1)}, u32[]{:S(2)}, u32[]{:S(2)}) collective-permute-start(bf16[8,8,8,640]{3,2,1,0:T(8,128)(2,1)S(1)} %bitcast.22), channel_id=1, source_target_pairs={{0,3},{1,0},{2,1},{3,2},{4,7},{5,4},{6,5},{7,6},{8,11},{9,8},{10,9... | collective-permute-start | bytes 1966088 | tf_op jit(solution)/shard_map/ppermute | solution.py:249
  57.4 2.2 %collective-permute-start.2 = (bf16[8,8,8,640]{3,2,1,0:T(8,128)(2,1)S(1)}, bf16[8,8,8,640]{3,2,1,0:T(8,128)(2,1)}, u32[]{:S(2)}, u32[]{:S(2)}) collective-permute-start(bf16[8,8,8,640]{3,2,1,0:T(8,128)(2,1)S(1)} %collective-permute-done.refs_1_), channel_id=1, source_target_pairs={{0,1},{1,2},{2,3},{3,0},{4,5},{5,6},{6,7},{7,4},{8,9},{9,10},{10,1... | collective-permute-start | bytes 1966088 | tf_op jit(solution)/shard_map/ppermute | solution.py:249
  59.6 1.9 %collective-permute-start.3 = (bf16[8,8,8,640]{3,2,1,0:T(8,128)(2,1)S(1)}, bf16[8,8,8,640]{3,2,1,0:T(8,128)(2,1)}, u32[]{:S(2)}, u32[]{:S(2)}) collective-permute-start(bf16[8,8,8,640]{3,2,1,0:T(8,128)(2,1)S(1)} %bitcast.23), channel_id=1, source_target_pairs={{0,4},{4,0},{1,5},{5,1},{2,6},{6,2},{3,7},{7,3},{8,12},{12,8},{9,1... | collective-permute-start | bytes 1966088 | tf_op jit(solution)/shard_map/ppermute | solution.py:259
  61.5 2.4 %collective-permute-start.4 = (bf16[8,8,8,640]{3,2,1,0:T(8,128)(2,1)S(1)}, bf16[8,8,8,640]{3,2,1,0:T(8,128)(2,1)}, u32[]{:S(2)}, u32[]{:S(2)}) collective-permute-start(bf16[8,8,8,640]{3,2,1,0:T(8,128)(2,1)S(1)} %collective-permute-done.refs_1_), channel_id=1, source_target_pairs={{0,4},{4,0},{1,5},{5,1},{2,6},{6,2},{3,7},{7,3},{8,12},{12,8},{9,1... | collective-permute-start | bytes 1966088 | tf_op jit(solution)/shard_map/ppermute | solution.py:259
  63.9 7.5 %collective-permute-done.1.refs_2_ = bf16[8,8,8,640]{3,2,1,0:T(8,128)(2,1)S(1)} collective-permute-done((bf16[8,8,8,640]{3,2,1,0:T(8,128)(2,1)S(1)}, bf16[8,8,8,640]{3,2,1,0:T(8,128)(2,1)S(1)}, u32[]{:S(2)}, u32[]{:S(2)}) %collective-permute-start.1) | collective-permute-done | bytes 655392 | tf_op jit(solution)/shard_map/ppermute | solution.py:249
  71.4 1.9 %collective-permute-start.5 = (bf16[8,8,8,640]{3,2,1,0:T(8,128)(2,1)S(1)}, bf16[8,8,8,640]{3,2,1,0:T(8,128)(2,1)}, u32[]{:S(2)}, u32[]{:S(2)}) collective-permute-start(bf16[8,8,8,640]{3,2,1,0:T(8,128)(2,1)S(1)} %collective-permute-done.1.refs_2_), channel_id=1, source_target_pairs={{0,4},{4,0},{1,5},{5,1},{2,6},{6,2},{3,7},{7,3},{8,12},{12,8},{9,1... | collective-permute-start | bytes 1966088 | tf_op jit(solution)/shard_map/ppermute | solution.py:259
  74.3 1.9 %collective-permute-done.2.refs_3_ = bf16[8,8,8,640]{3,2,1,0:T(8,128)(2,1)} collective-permute-done((bf16[8,8,8,640]{3,2,1,0:T(8,128)(2,1)S(1)}, bf16[8,8,8,640]{3,2,1,0:T(8,128)(2,1)}, u32[]{:S(2)}, u32[]{:S(2)}) %collective-permute-start.2) | collective-permute-done | bytes 655392 | tf_op jit(solution)/shard_map/ppermute | solution.py:249
  76.2 2.1 %collective-permute-start.6 = (bf16[8,8,8,640]{3,2,1,0:T(8,128)(2,1)}, bf16[8,8,8,640]{3,2,1,0:T(8,128)(2,1)}, u32[]{:S(2)}, u32[]{:S(2)}) collective-permute-start(bf16[8,8,8,640]{3,2,1,0:T(8,128)(2,1)} %collective-permute-done.2.refs_3_), channel_id=1, source_target_pairs={{0,4},{4,0},{1,5},{5,1},{2,6},{6,2},{3,7},{7,3},{8,12},{12,8},{9,1... | collective-permute-start | bytes 1966088 | tf_op jit(solution)/shard_map/ppermute | solution.py:259
  78.3 1.1 copy.28.arrived_ref
  79.4 5.1 %prepare.1 = (bf16[264,3072]{1,0:T(8,128)(2,1)}, f32[3,88,2048]{2,1,0:T(8,128)}, f32[88,2048]{1,0:T(8,128)}) custom-call(bf16[88,128]{1,0:T(8,128)(2,1)} %get-tuple-element.29.pick_ref, f32[88,128]{1,0:T(8,128)} %get-tuple-element.31.unit_ref, bf16[128,2176]{1,0:T(8,128)(2,1)} %copy.28.arrived_ref, bf16[3,128,2048]{2,1,0:T(8,128)(2,1)} %pad.26.loading_ref, ...), custom_call_target="tpu_custom_call" | custom-call | tf_op jit(solution)/shard_map/prepare/pallas_call | solution.py:306
  84.6 16.5 %solve.1 = (f32[3,81,2048]{2,1,0:T(8,128)}, f32[88,128]{1,0:T(8,128)}, f32[128,128]{1,0:T(8,128)}) custom-call(s32[2]{0:T(128)} %pad_add_fusion.side_ref, bf16[88,128]{1,0:T(8,128)(2,1)} %get-tuple-element.29.pick_ref, bf16[128,2048]{1,0:T(8,128)(2,1)} %pad.28.loading_hbm, bf16[264,3072]{1,0:T(8,128)(2,1)} %get-tuple-element.34.press_hbm, ...), custom_call_target="tpu_custom_call" | custom-call | tf_op jit(solution)/shard_map/solve/pallas_call | solution.py:319
  101.1 13.8 %all-to-all-start.2 = ((f32[128,1,128]{2,1,0:T(1,128)}), f32[128,1,128]{2,1,0:T(1,128)S(1)}, u32[]{:S(2)}, u32[]{:S(2)}) async-start(f32[128,1,128]{2,1,0:T(1,128)} %bitcast.29), calls=%async_computation.2 | async-start | bytes 131072 | tf_op jit(solution)/shard_map/all_to_all | solution.py:347
  115.3 2.0 %collective-permute-start.7 = (f32[8,108]{1,0:T(8,128)S(1)}, f32[8,108]{1,0:T(8,128)S(1)}, u32[]{:S(2)}, u32[]{:S(2)}) collective-permute-start(f32[8,108]{1,0:T(8,128)S(1)} %concatenate.11.own_data_ref), channel_id=1, source_target_pairs={{0,1},{1,2},{2,3},{3,4},{4,5},{5,6},{6,7},{7,8},{8,9},{9,10},{10,1... | collective-permute-start | bytes 10376 | tf_op jit(solution)/shard_map/ppermute | solution.py:227
  118.2 6.3 %collective-permute-done.7.behind_data_ref = f32[8,108]{1,0:T(8,128)S(1)} collective-permute-done((f32[8,108]{1,0:T(8,128)S(1)}, f32[8,108]{1,0:T(8,128)S(1)}, u32[]{:S(2)}, u32[]{:S(2)}) %collective-permute-start.7) | collective-permute-done | bytes 3488 | tf_op jit(solution)/shard_map/ppermute | solution.py:227
  124.4 1.4 %all-to-all-done.2 = f32[128,1,128]{2,1,0:T(1,128)S(1)} async-done(((f32[128,1,128]{2,1,0:T(1,128)}), f32[128,1,128]{2,1,0:T(1,128)S(1)}, u32[]{:S(2)}, u32[]{:S(2)}) %all-to-all-start.2) | async-done | bytes 65568 | tf_op jit(solution)/shard_map/all_to_all | solution.py:347
  125.9 2.0 %collective-permute-start.8 = (f32[128,128]{1,0:T(8,128)S(1)}, f32[128,128]{1,0:T(8,128)S(1)}, u32[]{:S(2)}, u32[]{:S(2)}) collective-permute-start(f32[128,128]{1,0:T(8,128)S(1)} %bitcast.17), channel_id=1, source_target_pairs={{0,1},{1,2},{2,3},{3,4},{4,5},{5,6},{6,7},{7,8},{8,9},{9,10},{10,1... | collective-permute-start | bytes 196616 | tf_op jit(solution)/shard_map/ppermute | solution.py:227
  128.0 7.7 %collective-permute-done.8.behind_ref = f32[128,128]{1,0:T(8,128)S(1)} collective-permute-done((f32[128,128]{1,0:T(8,128)S(1)}, f32[128,128]{1,0:T(8,128)S(1)}, u32[]{:S(2)}, u32[]{:S(2)}) %collective-permute-start.8) | collective-permute-done | bytes 65568 | tf_op jit(solution)/shard_map/ppermute | solution.py:227
  135.7 1.2 corners.1
  (58 shorter events, 8.6 us)
Async XLA Ops:
  0.6 18.4 %copy-start.10 = (s32[81]{0:T(128)S(1)}, s32[81]{0:T(128)}, u32[]{:S(2)}) copy-start(s32[81]{0:T(128)} %param.17) | copy-start | bytes 976
  0.6 18.4 %copy-start.6 = (bf16[27,6]{0,1:T(8,128)(2,1)S(1)}, bf16[27,6]{0,1:T(8,128)(2,1)}, u32[]{:S(2)}) copy-start(bf16[27,6]{0,1:T(8,128)(2,1)} %param.11) | copy-start | bytes 976
  0.7 18.5 %copy-start.4 = (bf16[6,3,2048]{2,1,0:T(4,128)(2,1)S(1)}, bf16[6,3,2048]{2,1,0:T(4,128)(2,1)}, u32[]{:S(2)}) copy-start(bf16[6,3,2048]{2,1,0:T(4,128)(2,1)} %param.19) | copy-start | bytes 221188
  3.1 19.7 %copy-start.3 = (bf16[27,2048]{1,0:T(8,128)(2,1)S(1)}, bf16[27,2048]{1,0:T(8,128)(2,1)}, u32[]{:S(2)}) copy-start(bf16[27,2048]{1,0:T(8,128)(2,1)} %param.12) | copy-start | bytes 331780
  3.1 19.7 %copy-start.8 = (s32[27]{0:T(128)S(1)}, s32[27]{0:T(128)}, u32[]{:S(2)}) copy-start(s32[27]{0:T(128)} %param.16) | copy-start | bytes 328
  3.1 37.0 %all-to-all-start = ((bf16[64,8,640]{2,1,0:T(8,128)(2,1)}), bf16[64,8,640]{2,1,0:T(8,128)(2,1)S(1)}, u32[]{:S(2)}, u32[]{:S(2)}) async-start(bf16[64,8,640]{2,1,0:T(8,128)(2,1)} %broadcast_in_dim.6), calls=%async_computation | async-start | bytes 1310720 | tf_op jit(solution)/shard_map/all_to_all | solution.py:243
  40.1 39.3 %copy-start = (bf16[64,8,640]{2,1,0:T(8,128)(2,1)}, bf16[64,8,640]{2,1,0:T(8,128)(2,1)S(1)}, u32[]{:S(2)}) copy-start(bf16[64,8,640]{2,1,0:T(8,128)(2,1)S(1)} %all-to-all-done) | copy-start | bytes 1966084
  40.1 17.3 %collective-permute-start = (bf16[8,8,8,640]{3,2,1,0:T(8,128)(2,1)S(1)}, bf16[8,8,8,640]{3,2,1,0:T(8,128)(2,1)S(1)}, u32[]{:S(2)}, u32[]{:S(2)}) collective-permute-start(bf16[8,8,8,640]{3,2,1,0:T(8,128)(2,1)S(1)} %bitcast.21), channel_id=1, source_target_pairs={{0,1},{1,2},{2,3},{3,0},{4,5},{5,6},{6,7},{7,4},{8,9},{9,10},{10,1... | collective-permute-start | bytes 1966088 | tf_op jit(solution)/shard_map/ppermute | solution.py:249
  45.4 27.9 %all-to-all-start.1 = ((bf16[128,2,1088]{2,1,0:T(2,128)(2,1)}), bf16[128,2,1088]{2,1,0:T(2,128)(2,1)S(1)}, u32[]{:S(2)}, u32[]{:S(2)}) async-start(bf16[128,2,1088]{2,1,0:T(2,128)(2,1)} %copy.26), calls=%async_computation.1 | async-start | bytes 1179648 | tf_op jit(solution)/shard_map/all_to_all | solution.py:304
  52.7 18.7 %collective-permute-start.1 = (bf16[8,8,8,640]{3,2,1,0:T(8,128)(2,1)S(1)}, bf16[8,8,8,640]{3,2,1,0:T(8,128)(2,1)S(1)}, u32[]{:S(2)}, u32[]{:S(2)}) collective-permute-start(bf16[8,8,8,640]{3,2,1,0:T(8,128)(2,1)S(1)} %bitcast.22), channel_id=1, source_target_pairs={{0,3},{1,0},{2,1},{3,2},{4,7},{5,4},{6,5},{7,6},{8,11},{9,8},{10,9... | collective-permute-start | bytes 1966088 | tf_op jit(solution)/shard_map/ppermute | solution.py:249
  57.4 27.1 %copy-start.1 = (bf16[8,8,8,640]{3,2,1,0:T(8,128)(2,1)}, bf16[8,8,8,640]{3,2,1,0:T(8,128)(2,1)S(1)}, u32[]{:S(2)}) copy-start(bf16[8,8,8,640]{3,2,1,0:T(8,128)(2,1)S(1)} %collective-permute-done.refs_1_) | copy-start | bytes 1966084
  57.4 18.8 %collective-permute-start.2 = (bf16[8,8,8,640]{3,2,1,0:T(8,128)(2,1)S(1)}, bf16[8,8,8,640]{3,2,1,0:T(8,128)(2,1)}, u32[]{:S(2)}, u32[]{:S(2)}) collective-permute-start(bf16[8,8,8,640]{3,2,1,0:T(8,128)(2,1)S(1)} %collective-permute-done.refs_1_), channel_id=1, source_target_pairs={{0,1},{1,2},{2,3},{3,0},{4,5},{5,6},{6,7},{7,4},{8,9},{9,10},{10,1... | collective-permute-start | bytes 1966088 | tf_op jit(solution)/shard_map/ppermute | solution.py:249
  59.6 24.9 %collective-permute-start.3 = (bf16[8,8,8,640]{3,2,1,0:T(8,128)(2,1)S(1)}, bf16[8,8,8,640]{3,2,1,0:T(8,128)(2,1)}, u32[]{:S(2)}, u32[]{:S(2)}) collective-permute-start(bf16[8,8,8,640]{3,2,1,0:T(8,128)(2,1)S(1)} %bitcast.23), channel_id=1, source_target_pairs={{0,4},{4,0},{1,5},{5,1},{2,6},{6,2},{3,7},{7,3},{8,12},{12,8},{9,1... | collective-permute-start | bytes 1966088 | tf_op jit(solution)/shard_map/ppermute | solution.py:259
  61.5 23.0 %collective-permute-start.4 = (bf16[8,8,8,640]{3,2,1,0:T(8,128)(2,1)S(1)}, bf16[8,8,8,640]{3,2,1,0:T(8,128)(2,1)}, u32[]{:S(2)}, u32[]{:S(2)}) collective-permute-start(bf16[8,8,8,640]{3,2,1,0:T(8,128)(2,1)S(1)} %collective-permute-done.refs_1_), channel_id=1, source_target_pairs={{0,4},{4,0},{1,5},{5,1},{2,6},{6,2},{3,7},{7,3},{8,12},{12,8},{9,1... | collective-permute-start | bytes 1966088 | tf_op jit(solution)/shard_map/ppermute | solution.py:259
  71.4 13.1 %copy-start.2 = (bf16[8,8,8,640]{3,2,1,0:T(8,128)(2,1)}, bf16[8,8,8,640]{3,2,1,0:T(8,128)(2,1)S(1)}, u32[]{:S(2)}) copy-start(bf16[8,8,8,640]{3,2,1,0:T(8,128)(2,1)S(1)} %collective-permute-done.1.refs_2_) | copy-start | bytes 1966084
  71.4 13.1 %collective-permute-start.5 = (bf16[8,8,8,640]{3,2,1,0:T(8,128)(2,1)S(1)}, bf16[8,8,8,640]{3,2,1,0:T(8,128)(2,1)}, u32[]{:S(2)}, u32[]{:S(2)}) collective-permute-start(bf16[8,8,8,640]{3,2,1,0:T(8,128)(2,1)S(1)} %collective-permute-done.1.refs_2_), channel_id=1, source_target_pairs={{0,4},{4,0},{1,5},{5,1},{2,6},{6,2},{3,7},{7,3},{8,12},{12,8},{9,1... | collective-permute-start | bytes 1966088 | tf_op jit(solution)/shard_map/ppermute | solution.py:259
  76.2 8.4 %collective-permute-start.6 = (bf16[8,8,8,640]{3,2,1,0:T(8,128)(2,1)}, bf16[8,8,8,640]{3,2,1,0:T(8,128)(2,1)}, u32[]{:S(2)}, u32[]{:S(2)}) collective-permute-start(bf16[8,8,8,640]{3,2,1,0:T(8,128)(2,1)} %collective-permute-done.2.refs_3_), channel_id=1, source_target_pairs={{0,4},{4,0},{1,5},{5,1},{2,6},{6,2},{3,7},{7,3},{8,12},{12,8},{9,1... | collective-permute-start | bytes 1966088 | tf_op jit(solution)/shard_map/ppermute | solution.py:259
  84.5 30.4 %copy-start.7 = (s32[4,27]{1,0:T(4,128)S(1)}, s32[4,27]{1,0:T(4,128)}, u32[]{:S(2)}) copy-start(s32[4,27]{1,0:T(4,128)} %param.15) | copy-start | bytes 1300
  84.5 30.5 %copy-start.9 = (f32[27]{0:T(128)S(1)}, f32[27]{0:T(128)}, u32[]{:S(2)}) copy-start(f32[27]{0:T(128)} %param.14) | copy-start | bytes 328
  84.6 30.6 %copy-start.5 = (f32[12,27]{1,0:T(8,128)S(1)}, f32[12,27]{1,0:T(8,128)}, u32[]{:S(2)}) copy-start(f32[12,27]{1,0:T(8,128)} %param.13) | copy-start | bytes 3892
  101.1 24.8 %all-to-all-start.2 = ((f32[128,1,128]{2,1,0:T(1,128)}), f32[128,1,128]{2,1,0:T(1,128)S(1)}, u32[]{:S(2)}, u32[]{:S(2)}) async-start(f32[128,1,128]{2,1,0:T(1,128)} %bitcast.29), calls=%async_computation.2 | async-start | bytes 131072 | tf_op jit(solution)/shard_map/all_to_all | solution.py:347
  115.3 9.1 %collective-permute-start.7 = (f32[8,108]{1,0:T(8,128)S(1)}, f32[8,108]{1,0:T(8,128)S(1)}, u32[]{:S(2)}, u32[]{:S(2)}) collective-permute-start(f32[8,108]{1,0:T(8,128)S(1)} %concatenate.11.own_data_ref), channel_id=1, source_target_pairs={{0,1},{1,2},{2,3},{3,4},{4,5},{5,6},{6,7},{7,8},{8,9},{9,10},{10,1... | collective-permute-start | bytes 10376 | tf_op jit(solution)/shard_map/ppermute | solution.py:227
  125.9 9.8 %collective-permute-start.8 = (f32[128,128]{1,0:T(8,128)S(1)}, f32[128,128]{1,0:T(8,128)S(1)}, u32[]{:S(2)}, u32[]{:S(2)}) collective-permute-start(f32[128,128]{1,0:T(8,128)S(1)} %bitcast.17), channel_id=1, source_target_pairs={{0,1},{1,2},{2,3},{3,4},{4,5},{5,6},{6,7},{7,8},{8,9},{9,10},{10,1... | collective-permute-start | bytes 196616 | tf_op jit(solution)/shard_map/ppermute | solution.py:227

commit v8 on v7

--- a/solution.py
+++ b/solution.py
@@ -43,25 +43,21 @@
     return head, middle, (rest - middle.astype(f32)).astype(bf16)
 
 
-def prepare_kernel(pick_ref, unit_ref, arrived_ref, loading_ref, state_ref, press_ref, forcing_ref, fiber_ref, still):
+def prepare_kernel(
+    pick_ref, unit_ref, strain_ref, arrived_ref, loading_ref, state_ref, press_ref, forcing_ref, fiber_ref, still
+):
     cap = state_ref.shape[1]
     rows = pick_ref.shape[0]
-    nodes = state_ref.shape[2]
     pick = pick_ref[...]
-    strain = (dot_nn(pick, arrived_ref[:, nodes:]) + unit_ref[...]).astype(bf16)
+    strain = (dot_nn(pick, strain_ref[...]) + unit_ref[...]).astype(bf16)[:, : loading_ref.shape[1]]
+    fiber = dot_nn(pick, arrived_ref[...])
+    fiber_ref[...] = fiber
     still[...] = jnp.zeros_like(still)
-    for start in range(0, nodes, SLICE):
-        cols = pl.ds(start, SLICE)
-        fiber = dot_nn(pick, arrived_ref[:, cols])
-        fiber_ref[:, cols] = fiber
-        for a in range(3):
-            still[0:cap, :] = state_ref[a, :, cols]
-            forcing = dot_nn(strain, loading_ref[a, :, cols])
-            forcing_ref[a, :, cols] = forcing
-            first = (forcing - fiber * jnp.tanh(still[...])).astype(bf16)
-            press_ref[a * rows : (a + 1) * rows, cols] = first
-            if nodes + start < press_ref.shape[1]:
-                press_ref[a * rows : (a + 1) * rows, pl.ds(nodes + start, SLICE)] = first
+    for a in range(3):
+        still[0:cap, :] = state_ref[a]
+        forcing = dot_nn(strain, loading_ref[a])
+        forcing_ref[a] = forcing
+        press_ref[a * rows : (a + 1) * rows, :] = (forcing - fiber * jnp.tanh(still[...])).astype(bf16)
 
 
 def solve_kernel(
@@ -89,13 +85,18 @@
         return pltpu.make_async_copy(shares[k], place, net_sems.at[k])
 
     inputs = (
-        pltpu.make_async_copy(press_hbm, pressure.at[0], in_sems.at[0]),
+        pltpu.make_async_copy(press_hbm, pressure.at[0, :, pl.ds(0, nodes)], in_sems.at[0]),
         pltpu.make_async_copy(forcing_hbm, forcing, in_sems.at[1]),
         pltpu.make_async_copy(fiber_hbm, fiber, in_sems.at[2]),
         pltpu.make_async_copy(state_hbm, table, in_sems.at[3]),
         pltpu.make_async_copy(loading_hbm, loading, in_sems.at[4]),
     )
+    over = pressure.shape[2] - nodes
+    wrap = pltpu.make_async_copy(
+        press_hbm.at[:, pl.ds(0, over)], pressure.at[0, :, pl.ds(nodes, over)], in_sems.at[5]
+    )
     inputs[0].start()
+    wrap.start()
     for k in range(2 * len(PIECES)):
         fetch(k).start()
     for copy in inputs[1:]:
@@ -116,10 +117,24 @@
     damp_sum[...] = jnp.zeros_like(damp_sum)
     stress_sum[...] = jnp.zeros_like(stress_sum)
     inputs[0].wait()
+    wrap.wait()
     for k in range(2 * len(PIECES)):
         fetch(k).wait()
+
+    def advance(iteration, n, moved):
+        cols = pl.ds(n * SLICE, SLICE)
+        damping = fiber[:, cols]
+        bend = jnp.tanh(moved)
+        for a in range(3):
+            block = slice(a * rows, (a + 1) * rows)
+            value = (forcing[a, :, cols] - damping * bend[block]).astype(bf16)
+            pressure[iteration + 1, block, cols] = value
+            if n < SENT - 1:
+                pressure[iteration + 1, block, pl.ds(nodes + n * SLICE, SLICE)] = value
+
     for iteration in range(ITERS):
         source = pressure.at[iteration]
+        held = []
         for step in range(BLOCKS):
             n = step
             cols = pl.ds(n * SLICE, SLICE)
@@ -127,19 +142,18 @@
             for d in range(1, BLOCKS - SENT + 1):
                 i = (n - d) % BLOCKS
                 moved += dot_nn(source[:, pl.ds(i * SLICE, SLICE)], net(i, d, 1))
-            if iteration == 0 and step == 0:
-                inputs[1].wait()
-                inputs[2].wait()
+            if iteration < ITERS - 1:
+                held.append((n, moved))
+                if iteration == 0 and step == 1:
+                    inputs[1].wait()
+                    inputs[2].wait()
+                if iteration > 0 or step > 0:
+                    for k, value in held:
+                        advance(iteration, k, value)
+                    held = []
+                continue
             damping = fiber[:, cols]
             bend = jnp.tanh(moved)
-            if iteration < ITERS - 1:
-                for a in range(3):
-                    block = slice(a * rows, (a + 1) * rows)
-                    value = (forcing[a, :, cols] - damping * bend[block]).astype(bf16)
-                    pressure[iteration + 1, block, cols] = value
-                    if n < SENT - 1:
-                        pressure[iteration + 1, block, pl.ds(nodes + n * SLICE, SLICE)] = value
-                continue
             if step == 0:
                 inputs[3].wait()
                 inputs[4].wait()
@@ -283,7 +297,7 @@
     slot_pick = (home_wide[:, None] == worker_ids[None, :]).astype(bf16)
     unit = (jnp.arange(rows)[:, None] - cap == jnp.arange(128)[None, :]).astype(f32)
     loading_rows = jnp.transpose(loading, (1, 0, 2))
-    loading_wide = jnp.pad(loading_rows, ((0, 0), (0, 128 - COMPS), (0, 0)))
+    loading_wide = jnp.pad(loading_rows, ((0, 0), (0, 16 - COMPS), (0, 0)))
     loading_sums = jnp.pad(loading_rows, ((0, 0), (1, 1), (0, 0))).reshape(24, nodes)
     loading_sums = jnp.pad(loading_sums, ((8 * COMPS, 128 - 24 - 8 * COMPS), (0, 0)))
     states = jnp.transpose(state_table, (1, 0, 2))
@@ -305,14 +319,28 @@
 
     press, forcing, fiber = pl.pallas_call(
         prepare_kernel,
+        grid=(nodes // SLICE,),
+        in_specs=[
+            pl.BlockSpec((rows, workers), lambda i: (0, 0)),
+            pl.BlockSpec((rows, 128), lambda i: (0, 0)),
+            pl.BlockSpec((workers, 128), lambda i: (0, nodes // 128)),
+            pl.BlockSpec((workers, SLICE), lambda i: (0, i)),
+            pl.BlockSpec((3, 16, SLICE), lambda i: (0, 0, i)),
+            pl.BlockSpec((3, cap, SLICE), lambda i: (0, 0, i)),
+        ],
+        out_specs=(
+            pl.BlockSpec((3 * rows, SLICE), lambda i: (0, i)),
+            pl.BlockSpec((3, rows, SLICE), lambda i: (0, 0, i)),
+            pl.BlockSpec((rows, SLICE), lambda i: (0, i)),
+        ),
         out_shape=(
-            jax.ShapeDtypeStruct((3 * rows, wide), bf16),
+            jax.ShapeDtypeStruct((3 * rows, nodes), bf16),
             jax.ShapeDtypeStruct((3, rows, nodes), f32),
             jax.ShapeDtypeStruct((rows, nodes), f32),
         ),
         scratch_shapes=[pltpu.VMEM((rows, SLICE), f32)],
         name="prepare",
-    )(slot_pick, unit, arrived, loading_wide, states)
+    )(slot_pick, unit, arrived, arrived, loading_wide, states)
     shares = swap_cores(pieces, arrived)
     vmem = pl.BlockSpec(memory_space=pltpu.VMEM)
     hbm = pl.BlockSpec(memory_space=pltpu.HBM)
@@ -335,7 +363,7 @@
             pltpu.VMEM((3 * rows, 256), f32),
             pltpu.VMEM((3 * rows, 128), f32),
             pltpu.SemaphoreType.DMA((2 * len(PIECES),)),
-            pltpu.SemaphoreType.DMA((5,)),
+            pltpu.SemaphoreType.DMA((6,)),
             pltpu.SemaphoreType.DMA((BLOCKS,)),
         ],
         name="solve",

time: 138 us -> 140 us (1.014)
  Pallas kernels: 22.8 us -> 25.2 us
    pallas_call x1, Pallas kernels: 5.12 us -> 7.44 us  [body(): pl.pallas_call(prepare_kernel, grid=(nodes // SLICE,), in_specs=[pl.Block...]
  transfers between devices with their start and end apart: 12 -> 12, of which waited for: 7 -> 7; matrix products, arithmetic and copies ran while one was open for 7% -> 6% of each run, Pallas kernels for 4% -> 5%
where the time goes in v8:
time: 140 us; the launch traced here: 139 us
  starting transfers between devices  58.4 us (42%)
  waiting for transfers between devices  43.4 us (31%)
  Pallas kernels  25.2 us (18%)
  local copies, waits for them, and re-layouts  8.85 us (6%)
  other arithmetic  2.01 us (1%)
    all_to_all x1, waiting for transfers between devices, spread_network(): lax.all_to_all(jnp.broadcast_to(part[None], (depth * lines,) + part.shape...  17.6 us
    pallas_call x1, Pallas kernels, body(): pl.pallas_call(solve_kernel, out_shape=(jax.ShapeDtypeStruct((3, cap, nod...  16.5 us
    all_to_all x1, starting transfers between devices, spread_network(): lax.all_to_all(jnp.broadcast_to(part[None], (depth * lines,) + part.shape...  15.8 us
    ppermute x2, waiting for transfers between devices, from_behind(): return lax.ppermute(block, axis, route)  14 us
    all_to_all x1, starting transfers between devices, body(): lax.all_to_all(backward, RVE, split_axis=0, concat_axis=0, tiled=True)  13.8 us
    ppermute x3, waiting for transfers between devices, pass_on(): lax.ppermute(value, 'blk', [(i, (i + step) % ring) for i in range(ring)])  10.3 us
    ppermute x3, starting transfers between devices, pass_on(): lax.ppermute(value, 'blk', [(i, (i + step) % ring) for i in range(ring)])  9.19 us
    ppermute x4, starting transfers between devices, swap_cores(): lax.ppermute(piece, 'core', [(0, 1), (1, 0)])  8.33 us
  transfers between devices with their start and end apart: 12, of which 7 were waited for; matrix products, arithmetic and copies ran while one was open for 6% of the time, Pallas kernels for 5%

profile of v8, /device:TPU:64, one launch (start us, length us, event | category | flops | bytes accessed | tf_op | source)
XLA Modules:
  0.0 139.1 jit_solution(2694931347002639178)
XLA Ops:
  3.2 15.8 %all-to-all-start = ((bf16[64,8,640]{2,1,0:T(8,128)(2,1)}), bf16[64,8,640]{2,1,0:T(8,128)(2,1)S(1)}, u32[]{:S(2)}, u32[]{:S(2)}) async-start(bf16[64,8,640]{2,1,0:T(8,128)(2,1)} %broadcast_in_dim.6), calls=%async_computation | async-start | bytes 1310720 | tf_op jit(solution)/shard_map/all_to_all | solution.py:257
  22.4 17.6 %all-to-all-done = bf16[64,8,640]{2,1,0:T(8,128)(2,1)S(1)} async-done(((bf16[64,8,640]{2,1,0:T(8,128)(2,1)}), bf16[64,8,640]{2,1,0:T(8,128)(2,1)S(1)}, u32[]{:S(2)}, u32[]{:S(2)}) %all-to-all-start) | async-done | bytes 655392 | tf_op jit(solution)/shard_map/all_to_all | solution.py:257
  40.0 3.4 %collective-permute-start = (bf16[8,8,8,640]{3,2,1,0:T(8,128)(2,1)S(1)}, bf16[8,8,8,640]{3,2,1,0:T(8,128)(2,1)S(1)}, u32[]{:S(2)}, u32[]{:S(2)}) collective-permute-start(bf16[8,8,8,640]{3,2,1,0:T(8,128)(2,1)S(1)} %bitcast.21), channel_id=1, source_target_pairs={{0,1},{1,2},{2,3},{3,0},{4,5},{5,6},{6,7},{7,4},{8,9},{9,10},{10,1... | collective-permute-start | bytes 1966088 | tf_op jit(solution)/shard_map/ppermute | solution.py:263
  43.4 1.9 %copy.27 = bf16[128,2,1088]{2,1,0:T(2,128)(2,1)} copy(bf16[128,2,1088]{0,2,1:T(8,128)(2,1)S(1)} %bitcast.26) | data formatting | bytes 1114112 | tf_op jit(solution)/shard_map/optimization_barrier | solution.py:265
  45.3 7.3 %all-to-all-start.1 = ((bf16[128,2,1088]{2,1,0:T(2,128)(2,1)}), bf16[128,2,1088]{2,1,0:T(2,128)(2,1)S(1)}, u32[]{:S(2)}, u32[]{:S(2)}) async-start(bf16[128,2,1088]{2,1,0:T(2,128)(2,1)} %copy.27), calls=%async_computation.1 | async-start | bytes 1179648 | tf_op jit(solution)/shard_map/all_to_all | solution.py:318
  52.6 3.7 %collective-permute-start.1 = (bf16[8,8,8,640]{3,2,1,0:T(8,128)(2,1)S(1)}, bf16[8,8,8,640]{3,2,1,0:T(8,128)(2,1)S(1)}, u32[]{:S(2)}, u32[]{:S(2)}) collective-permute-start(bf16[8,8,8,640]{3,2,1,0:T(8,128)(2,1)S(1)} %bitcast.22), channel_id=1, source_target_pairs={{0,3},{1,0},{2,1},{3,2},{4,7},{5,4},{6,5},{7,6},{8,11},{9,8},{10,9... | collective-permute-start | bytes 1966088 | tf_op jit(solution)/shard_map/ppermute | solution.py:263
  56.3 1.0 collective-permute-done.refs_1_
  57.3 2.2 %collective-permute-start.2 = (bf16[8,8,8,640]{3,2,1,0:T(8,128)(2,1)S(1)}, bf16[8,8,8,640]{3,2,1,0:T(8,128)(2,1)}, u32[]{:S(2)}, u32[]{:S(2)}) collective-permute-start(bf16[8,8,8,640]{3,2,1,0:T(8,128)(2,1)S(1)} %collective-permute-done.refs_1_), channel_id=1, source_target_pairs={{0,1},{1,2},{2,3},{3,0},{4,5},{5,6},{6,7},{7,4},{8,9},{9,10},{10,1... | collective-permute-start | bytes 1966088 | tf_op jit(solution)/shard_map/ppermute | solution.py:263
  59.5 1.9 %collective-permute-start.3 = (bf16[8,8,8,640]{3,2,1,0:T(8,128)(2,1)S(1)}, bf16[8,8,8,640]{3,2,1,0:T(8,128)(2,1)}, u32[]{:S(2)}, u32[]{:S(2)}) collective-permute-start(bf16[8,8,8,640]{3,2,1,0:T(8,128)(2,1)S(1)} %bitcast.23), channel_id=1, source_target_pairs={{0,4},{4,0},{1,5},{5,1},{2,6},{6,2},{3,7},{7,3},{8,12},{12,8},{9,1... | collective-permute-start | bytes 1966088 | tf_op jit(solution)/shard_map/ppermute | solution.py:273
  61.4 2.4 %collective-permute-start.4 = (bf16[8,8,8,640]{3,2,1,0:T(8,128)(2,1)S(1)}, bf16[8,8,8,640]{3,2,1,0:T(8,128)(2,1)}, u32[]{:S(2)}, u32[]{:S(2)}) collective-permute-start(bf16[8,8,8,640]{3,2,1,0:T(8,128)(2,1)S(1)} %collective-permute-done.refs_1_), channel_id=1, source_target_pairs={{0,4},{4,0},{1,5},{5,1},{2,6},{6,2},{3,7},{7,3},{8,12},{12,8},{9,1... | collective-permute-start | bytes 1966088 | tf_op jit(solution)/shard_map/ppermute | solution.py:273
  63.8 7.4 %collective-permute-done.1.refs_2_ = bf16[8,8,8,640]{3,2,1,0:T(8,128)(2,1)S(1)} collective-permute-done((bf16[8,8,8,640]{3,2,1,0:T(8,128)(2,1)S(1)}, bf16[8,8,8,640]{3,2,1,0:T(8,128)(2,1)S(1)}, u32[]{:S(2)}, u32[]{:S(2)}) %collective-permute-start.1) | collective-permute-done | bytes 655392 | tf_op jit(solution)/shard_map/ppermute | solution.py:263
  71.3 1.9 %collective-permute-start.5 = (bf16[8,8,8,640]{3,2,1,0:T(8,128)(2,1)S(1)}, bf16[8,8,8,640]{3,2,1,0:T(8,128)(2,1)}, u32[]{:S(2)}, u32[]{:S(2)}) collective-permute-start(bf16[8,8,8,640]{3,2,1,0:T(8,128)(2,1)S(1)} %collective-permute-done.1.refs_2_), channel_id=1, source_target_pairs={{0,4},{4,0},{1,5},{5,1},{2,6},{6,2},{3,7},{7,3},{8,12},{12,8},{9,1... | collective-permute-start | bytes 1966088 | tf_op jit(solution)/shard_map/ppermute | solution.py:273
  74.2 1.9 %collective-permute-done.2.refs_3_ = bf16[8,8,8,640]{3,2,1,0:T(8,128)(2,1)} collective-permute-done((bf16[8,8,8,640]{3,2,1,0:T(8,128)(2,1)S(1)}, bf16[8,8,8,640]{3,2,1,0:T(8,128)(2,1)}, u32[]{:S(2)}, u32[]{:S(2)}) %collective-permute-start.2) | collective-permute-done | bytes 655392 | tf_op jit(solution)/shard_map/ppermute | solution.py:263
  76.0 2.1 %collective-permute-start.6 = (bf16[8,8,8,640]{3,2,1,0:T(8,128)(2,1)}, bf16[8,8,8,640]{3,2,1,0:T(8,128)(2,1)}, u32[]{:S(2)}, u32[]{:S(2)}) collective-permute-start(bf16[8,8,8,640]{3,2,1,0:T(8,128)(2,1)} %collective-permute-done.2.refs_3_), channel_id=1, source_target_pairs={{0,4},{4,0},{1,5},{5,1},{2,6},{6,2},{3,7},{7,3},{8,12},{12,8},{9,1... | collective-permute-start | bytes 1966088 | tf_op jit(solution)/shard_map/ppermute | solution.py:273
  78.1 1.1 copy.29.strain_ref.arrived_ref
  79.2 7.4 %prepare.1 = (bf16[264,2048]{1,0:T(8,128)(2,1)}, f32[3,88,2048]{2,1,0:T(8,128)}, f32[88,2048]{1,0:T(8,128)}) custom-call(bf16[88,128]{1,0:T(8,128)(2,1)} %get-tuple-element.29.pick_ref, f32[88,128]{1,0:T(8,128)} %get-tuple-element.31.unit_ref, bf16[128,2176]{1,0:T(8,128)(2,1)} %copy.29.strain_ref.arrived_ref, bf16[128,2176]{1,0:T(8,128)(2,1)} %copy.29.strain_ref.arrived_ref, ...), custom_call_target="tpu_custom_call" | custom-call | tf_op jit(solution)/shard_map/prepare/pallas_call | solution.py:320
  86.7 16.5 %solve.1 = (f32[3,81,2048]{2,1,0:T(8,128)}, f32[88,128]{1,0:T(8,128)}, f32[128,128]{1,0:T(8,128)}) custom-call(s32[2]{0:T(128)} %pad_add_fusion.side_ref, bf16[88,128]{1,0:T(8,128)(2,1)} %get-tuple-element.29.pick_ref, bf16[128,2048]{1,0:T(8,128)(2,1)} %pad.28.loading_hbm, bf16[264,2048]{1,0:T(8,128)(2,1)} %get-tuple-element.34.press_hbm, ...), custom_call_target="tpu_custom_call" | custom-call | tf_op jit(solution)/shard_map/solve/pallas_call | solution.py:347
  103.3 13.8 %all-to-all-start.2 = ((f32[128,1,128]{2,1,0:T(1,128)}), f32[128,1,128]{2,1,0:T(1,128)S(1)}, u32[]{:S(2)}, u32[]{:S(2)}) async-start(f32[128,1,128]{2,1,0:T(1,128)} %bitcast.29), calls=%async_computation.2 | async-start | bytes 131072 | tf_op jit(solution)/shard_map/all_to_all | solution.py:375
  117.5 2.0 %collective-permute-start.7 = (f32[8,108]{1,0:T(8,128)S(1)}, f32[8,108]{1,0:T(8,128)S(1)}, u32[]{:S(2)}, u32[]{:S(2)}) collective-permute-start(f32[8,108]{1,0:T(8,128)S(1)} %concatenate.11.own_data_ref), channel_id=1, source_target_pairs={{0,1},{1,2},{2,3},{3,4},{4,5},{5,6},{6,7},{7,8},{8,9},{9,10},{10,1... | collective-permute-start | bytes 10376 | tf_op jit(solution)/shard_map/ppermute | solution.py:241
  120.4 6.3 %collective-permute-done.7.behind_data_ref = f32[8,108]{1,0:T(8,128)S(1)} collective-permute-done((f32[8,108]{1,0:T(8,128)S(1)}, f32[8,108]{1,0:T(8,128)S(1)}, u32[]{:S(2)}, u32[]{:S(2)}) %collective-permute-start.7) | collective-permute-done | bytes 3488 | tf_op jit(solution)/shard_map/ppermute | solution.py:241
  126.7 1.5 %all-to-all-done.2 = f32[128,1,128]{2,1,0:T(1,128)S(1)} async-done(((f32[128,1,128]{2,1,0:T(1,128)}), f32[128,1,128]{2,1,0:T(1,128)S(1)}, u32[]{:S(2)}, u32[]{:S(2)}) %all-to-all-start.2) | async-done | bytes 65568 | tf_op jit(solution)/shard_map/all_to_all | solution.py:375
  128.1 2.0 %collective-permute-start.8 = (f32[128,128]{1,0:T(8,128)S(1)}, f32[128,128]{1,0:T(8,128)S(1)}, u32[]{:S(2)}, u32[]{:S(2)}) collective-permute-start(f32[128,128]{1,0:T(8,128)S(1)} %bitcast.17), channel_id=1, source_target_pairs={{0,1},{1,2},{2,3},{3,4},{4,5},{5,6},{6,7},{7,8},{8,9},{9,10},{10,1... | collective-permute-start | bytes 196616 | tf_op jit(solution)/shard_map/ppermute | solution.py:241
  130.2 7.7 %collective-permute-done.8.behind_ref = f32[128,128]{1,0:T(8,128)S(1)} collective-permute-done((f32[128,128]{1,0:T(8,128)S(1)}, f32[128,128]{1,0:T(8,128)S(1)}, u32[]{:S(2)}, u32[]{:S(2)}) %collective-permute-start.8) | collective-permute-done | bytes 65568 | tf_op jit(solution)/shard_map/ppermute | solution.py:241
  137.9 1.2 corners.1
  (58 shorter events, 8.2 us)
Async XLA Ops:
  0.6 18.3 %copy-start.10 = (s32[81]{0:T(128)S(1)}, s32[81]{0:T(128)}, u32[]{:S(2)}) copy-start(s32[81]{0:T(128)} %param.17) | copy-start | bytes 976
  0.6 18.4 %copy-start.6 = (bf16[27,6]{0,1:T(8,128)(2,1)S(1)}, bf16[27,6]{0,1:T(8,128)(2,1)}, u32[]{:S(2)}) copy-start(bf16[27,6]{0,1:T(8,128)(2,1)} %param.11) | copy-start | bytes 976
  0.7 18.5 %copy-start.4 = (bf16[6,3,2048]{2,1,0:T(4,128)(2,1)S(1)}, bf16[6,3,2048]{2,1,0:T(4,128)(2,1)}, u32[]{:S(2)}) copy-start(bf16[6,3,2048]{2,1,0:T(4,128)(2,1)} %param.19) | copy-start | bytes 221188
  0.7 21.4 %copy-start.8 = (s32[27]{0:T(128)S(1)}, s32[27]{0:T(128)}, u32[]{:S(2)}) copy-start(s32[27]{0:T(128)} %param.16) | copy-start | bytes 328
  0.7 21.4 %copy-start.3 = (bf16[27,2048]{1,0:T(8,128)(2,1)S(1)}, bf16[27,2048]{1,0:T(8,128)(2,1)}, u32[]{:S(2)}) copy-start(bf16[27,2048]{1,0:T(8,128)(2,1)} %param.12) | copy-start | bytes 331780
  3.2 36.8 %all-to-all-start = ((bf16[64,8,640]{2,1,0:T(8,128)(2,1)}), bf16[64,8,640]{2,1,0:T(8,128)(2,1)S(1)}, u32[]{:S(2)}, u32[]{:S(2)}) async-start(bf16[64,8,640]{2,1,0:T(8,128)(2,1)} %broadcast_in_dim.6), calls=%async_computation | async-start | bytes 1310720 | tf_op jit(solution)/shard_map/all_to_all | solution.py:257
  40.0 39.2 %copy-start = (bf16[64,8,640]{2,1,0:T(8,128)(2,1)}, bf16[64,8,640]{2,1,0:T(8,128)(2,1)S(1)}, u32[]{:S(2)}) copy-start(bf16[64,8,640]{2,1,0:T(8,128)(2,1)S(1)} %all-to-all-done) | copy-start | bytes 1966084
  40.0 17.3 %collective-permute-start = (bf16[8,8,8,640]{3,2,1,0:T(8,128)(2,1)S(1)}, bf16[8,8,8,640]{3,2,1,0:T(8,128)(2,1)S(1)}, u32[]{:S(2)}, u32[]{:S(2)}) collective-permute-start(bf16[8,8,8,640]{3,2,1,0:T(8,128)(2,1)S(1)} %bitcast.21), channel_id=1, source_target_pairs={{0,1},{1,2},{2,3},{3,0},{4,5},{5,6},{6,7},{7,4},{8,9},{9,10},{10,1... | collective-permute-start | bytes 1966088 | tf_op jit(solution)/shard_map/ppermute | solution.py:263
  45.3 27.9 %all-to-all-start.1 = ((bf16[128,2,1088]{2,1,0:T(2,128)(2,1)}), bf16[128,2,1088]{2,1,0:T(2,128)(2,1)S(1)}, u32[]{:S(2)}, u32[]{:S(2)}) async-start(bf16[128,2,1088]{2,1,0:T(2,128)(2,1)} %copy.27), calls=%async_computation.1 | async-start | bytes 1179648 | tf_op jit(solution)/shard_map/all_to_all | solution.py:318
  52.6 18.7 %collective-permute-start.1 = (bf16[8,8,8,640]{3,2,1,0:T(8,128)(2,1)S(1)}, bf16[8,8,8,640]{3,2,1,0:T(8,128)(2,1)S(1)}, u32[]{:S(2)}, u32[]{:S(2)}) collective-permute-start(bf16[8,8,8,640]{3,2,1,0:T(8,128)(2,1)S(1)} %bitcast.22), channel_id=1, source_target_pairs={{0,3},{1,0},{2,1},{3,2},{4,7},{5,4},{6,5},{7,6},{8,11},{9,8},{10,9... | collective-permute-start | bytes 1966088 | tf_op jit(solution)/shard_map/ppermute | solution.py:263
  57.3 29.3 %copy-start.1 = (bf16[8,8,8,640]{3,2,1,0:T(8,128)(2,1)}, bf16[8,8,8,640]{3,2,1,0:T(8,128)(2,1)S(1)}, u32[]{:S(2)}) copy-start(bf16[8,8,8,640]{3,2,1,0:T(8,128)(2,1)S(1)} %collective-permute-done.refs_1_) | copy-start | bytes 1966084
  57.3 18.7 %collective-permute-start.2 = (bf16[8,8,8,640]{3,2,1,0:T(8,128)(2,1)S(1)}, bf16[8,8,8,640]{3,2,1,0:T(8,128)(2,1)}, u32[]{:S(2)}, u32[]{:S(2)}) collective-permute-start(bf16[8,8,8,640]{3,2,1,0:T(8,128)(2,1)S(1)} %collective-permute-done.refs_1_), channel_id=1, source_target_pairs={{0,1},{1,2},{2,3},{3,0},{4,5},{5,6},{6,7},{7,4},{8,9},{9,10},{10,1... | collective-permute-start | bytes 1966088 | tf_op jit(solution)/shard_map/ppermute | solution.py:263
  59.5 27.2 %collective-permute-start.3 = (bf16[8,8,8,640]{3,2,1,0:T(8,128)(2,1)S(1)}, bf16[8,8,8,640]{3,2,1,0:T(8,128)(2,1)}, u32[]{:S(2)}, u32[]{:S(2)}) collective-permute-start(bf16[8,8,8,640]{3,2,1,0:T(8,128)(2,1)S(1)} %bitcast.23), channel_id=1, source_target_pairs={{0,4},{4,0},{1,5},{5,1},{2,6},{6,2},{3,7},{7,3},{8,12},{12,8},{9,1... | collective-permute-start | bytes 1966088 | tf_op jit(solution)/shard_map/ppermute | solution.py:273
  61.4 25.3 %collective-permute-start.4 = (bf16[8,8,8,640]{3,2,1,0:T(8,128)(2,1)S(1)}, bf16[8,8,8,640]{3,2,1,0:T(8,128)(2,1)}, u32[]{:S(2)}, u32[]{:S(2)}) collective-permute-start(bf16[8,8,8,640]{3,2,1,0:T(8,128)(2,1)S(1)} %collective-permute-done.refs_1_), channel_id=1, source_target_pairs={{0,4},{4,0},{1,5},{5,1},{2,6},{6,2},{3,7},{7,3},{8,12},{12,8},{9,1... | collective-permute-start | bytes 1966088 | tf_op jit(solution)/shard_map/ppermute | solution.py:273
  71.3 15.4 %copy-start.2 = (bf16[8,8,8,640]{3,2,1,0:T(8,128)(2,1)}, bf16[8,8,8,640]{3,2,1,0:T(8,128)(2,1)S(1)}, u32[]{:S(2)}) copy-start(bf16[8,8,8,640]{3,2,1,0:T(8,128)(2,1)S(1)} %collective-permute-done.1.refs_2_) | copy-start | bytes 1966084
  71.3 15.4 %collective-permute-start.5 = (bf16[8,8,8,640]{3,2,1,0:T(8,128)(2,1)S(1)}, bf16[8,8,8,640]{3,2,1,0:T(8,128)(2,1)}, u32[]{:S(2)}, u32[]{:S(2)}) collective-permute-start(bf16[8,8,8,640]{3,2,1,0:T(8,128)(2,1)S(1)} %collective-permute-done.1.refs_2_), channel_id=1, source_target_pairs={{0,4},{4,0},{1,5},{5,1},{2,6},{6,2},{3,7},{7,3},{8,12},{12,8},{9,1... | collective-permute-start | bytes 1966088 | tf_op jit(solution)/shard_map/ppermute | solution.py:273
  76.0 10.7 %collective-permute-start.6 = (bf16[8,8,8,640]{3,2,1,0:T(8,128)(2,1)}, bf16[8,8,8,640]{3,2,1,0:T(8,128)(2,1)}, u32[]{:S(2)}, u32[]{:S(2)}) collective-permute-start(bf16[8,8,8,640]{3,2,1,0:T(8,128)(2,1)} %collective-permute-done.2.refs_3_), channel_id=1, source_target_pairs={{0,4},{4,0},{1,5},{5,1},{2,6},{6,2},{3,7},{7,3},{8,12},{12,8},{9,1... | collective-permute-start | bytes 1966088 | tf_op jit(solution)/shard_map/ppermute | solution.py:273
  86.7 30.5 %copy-start.7 = (s32[4,27]{1,0:T(4,128)S(1)}, s32[4,27]{1,0:T(4,128)}, u32[]{:S(2)}) copy-start(s32[4,27]{1,0:T(4,128)} %param.15) | copy-start | bytes 1300
  86.7 30.6 %copy-start.9 = (f32[27]{0:T(128)S(1)}, f32[27]{0:T(128)}, u32[]{:S(2)}) copy-start(f32[27]{0:T(128)} %param.14) | copy-start | bytes 328
  86.7 30.7 %copy-start.5 = (f32[12,27]{1,0:T(8,128)S(1)}, f32[12,27]{1,0:T(8,128)}, u32[]{:S(2)}) copy-start(f32[12,27]{1,0:T(8,128)} %param.13) | copy-start | bytes 3892
  103.3 24.8 %all-to-all-start.2 = ((f32[128,1,128]{2,1,0:T(1,128)}), f32[128,1,128]{2,1,0:T(1,128)S(1)}, u32[]{:S(2)}, u32[]{:S(2)}) async-start(f32[128,1,128]{2,1,0:T(1,128)} %bitcast.29), calls=%async_computation.2 | async-start | bytes 131072 | tf_op jit(solution)/shard_map/all_to_all | solution.py:375
  117.5 9.1 %collective-permute-start.7 = (f32[8,108]{1,0:T(8,128)S(1)}, f32[8,108]{1,0:T(8,128)S(1)}, u32[]{:S(2)}, u32[]{:S(2)}) collective-permute-start(f32[8,108]{1,0:T(8,128)S(1)} %concatenate.11.own_data_ref), channel_id=1, source_target_pairs={{0,1},{1,2},{2,3},{3,4},{4,5},{5,6},{6,7},{7,8},{8,9},{9,10},{10,1... | collective-permute-start | bytes 10376 | tf_op jit(solution)/shard_map/ppermute | solution.py:241
  128.1 9.8 %collective-permute-start.8 = (f32[128,128]{1,0:T(8,128)S(1)}, f32[128,128]{1,0:T(8,128)S(1)}, u32[]{:S(2)}, u32[]{:S(2)}) collective-permute-start(f32[128,128]{1,0:T(8,128)S(1)} %bitcast.17), channel_id=1, source_target_pairs={{0,1},{1,2},{2,3},{3,4},{4,5},{5,6},{6,7},{7,8},{8,9},{9,10},{10,1... | collective-permute-start | bytes 196616 | tf_op jit(solution)/shard_map/ppermute | solution.py:241

commit v9 on v8

--- a/solution.py
+++ b/solution.py
@@ -44,20 +44,25 @@
 
 
 def prepare_kernel(
-    pick_ref, unit_ref, strain_ref, arrived_ref, loading_ref, state_ref, press_ref, forcing_ref, fiber_ref, still
+    pick_ref, unit_ref, arrived_ref, loading_ref, state_ref, press_ref, forcing_ref, fiber_ref, still
 ):
     cap = state_ref.shape[1]
     rows = pick_ref.shape[0]
+    nodes = state_ref.shape[2]
     pick = pick_ref[...]
-    strain = (dot_nn(pick, strain_ref[...]) + unit_ref[...]).astype(bf16)[:, : loading_ref.shape[1]]
-    fiber = dot_nn(pick, arrived_ref[...])
-    fiber_ref[...] = fiber
+    strain = (dot_nn(pick, arrived_ref[:, nodes:]) + unit_ref[...]).astype(bf16)[:, : loading_ref.shape[1]]
     still[...] = jnp.zeros_like(still)
-    for a in range(3):
-        still[0:cap, :] = state_ref[a]
-        forcing = dot_nn(strain, loading_ref[a])
-        forcing_ref[a] = forcing
-        press_ref[a * rows : (a + 1) * rows, :] = (forcing - fiber * jnp.tanh(still[...])).astype(bf16)
+    for start in range(0, nodes, SLICE):
+        cols = pl.ds(start, SLICE)
+        fiber = dot_nn(pick, arrived_ref[:, cols])
+        fiber_ref[:, cols] = fiber
+        for a in range(3):
+            still[0:cap, :] = state_ref[a, :, cols]
+            forcing = dot_nn(strain, loading_ref[a, :, cols])
+            forcing_ref[a, :, cols] = forcing
+            press_ref[a * rows : (a + 1) * rows, cols] = (
+                forcing - fiber * jnp.tanh(still[...])
+            ).astype(bf16)
 
 
 def solve_kernel(
@@ -319,20 +324,6 @@
 
     press, forcing, fiber = pl.pallas_call(
         prepare_kernel,
-        grid=(nodes // SLICE,),
-        in_specs=[
-            pl.BlockSpec((rows, workers), lambda i: (0, 0)),
-            pl.BlockSpec((rows, 128), lambda i: (0, 0)),
-            pl.BlockSpec((workers, 128), lambda i: (0, nodes // 128)),
-            pl.BlockSpec((workers, SLICE), lambda i: (0, i)),
-            pl.BlockSpec((3, 16, SLICE), lambda i: (0, 0, i)),
-            pl.BlockSpec((3, cap, SLICE), lambda i: (0, 0, i)),
-        ],
-        out_specs=(
-            pl.BlockSpec((3 * rows, SLICE), lambda i: (0, i)),
-            pl.BlockSpec((3, rows, SLICE), lambda i: (0, 0, i)),
-            pl.BlockSpec((rows, SLICE), lambda i: (0, i)),
-        ),
         out_shape=(
             jax.ShapeDtypeStruct((3 * rows, nodes), bf16),
             jax.ShapeDtypeStruct((3, rows, nodes), f32),
@@ -340,7 +331,7 @@
         ),
         scratch_shapes=[pltpu.VMEM((rows, SLICE), f32)],
         name="prepare",
-    )(slot_pick, unit, arrived, arrived, loading_wide, states)
+    )(slot_pick, unit, arrived, loading_wide, states)
     shares = swap_cores(pieces, arrived)
     vmem = pl.BlockSpec(memory_space=pltpu.VMEM)
     hbm = pl.BlockSpec(memory_space=pltpu.HBM)

time: 140 us -> 137 us (0.979)
  Pallas kernels: 25.2 us -> 22.3 us
    pallas_call x1, Pallas kernels: 7.44 us -> 4.54 us  [body(): pl.pallas_call(prepare_kernel, out_shape=(jax.ShapeDtypeStruct((3 * rows,...]
  transfers between devices with their start and end apart: 12 -> 12, of which waited for: 7 -> 7; matrix products, arithmetic and copies ran while one was open for 6% -> 6% of each run, Pallas kernels for 5% -> 3%
where the time goes in v9:
time: 137 us; the launch traced here: 136 us
  starting transfers between devices  58.4 us (43%)
  waiting for transfers between devices  43.4 us (32%)
  Pallas kernels  22.3 us (16%)
  local copies, waits for them, and re-layouts  8.85 us (6%)
  other arithmetic  2.01 us (1%)
    all_to_all x1, waiting for transfers between devices, spread_network(): lax.all_to_all(jnp.broadcast_to(part[None], (depth * lines,) + part.shape...  17.6 us
    pallas_call x1, Pallas kernels, body(): pl.pallas_call(solve_kernel, out_shape=(jax.ShapeDtypeStruct((3, cap, nod...  16.5 us
    all_to_all x1, starting transfers between devices, spread_network(): lax.all_to_all(jnp.broadcast_to(part[None], (depth * lines,) + part.shape...  15.8 us
    ppermute x2, waiting for transfers between devices, from_behind(): return lax.ppermute(block, axis, route)  14 us
    all_to_all x1, starting transfers between devices, body(): lax.all_to_all(backward, RVE, split_axis=0, concat_axis=0, tiled=True)  13.8 us
    ppermute x3, waiting for transfers between devices, pass_on(): lax.ppermute(value, 'blk', [(i, (i + step) % ring) for i in range(ring)])  10.3 us
    ppermute x3, starting transfers between devices, pass_on(): lax.ppermute(value, 'blk', [(i, (i + step) % ring) for i in range(ring)])  9.19 us
    ppermute x4, starting transfers between devices, swap_cores(): lax.ppermute(piece, 'core', [(0, 1), (1, 0)])  8.33 us
  transfers between devices with their start and end apart: 12, of which 7 were waited for; matrix products, arithmetic and copies ran while one was open for 6% of the time, Pallas kernels for 3%

profile of v9, /device:TPU:64, one launch (start us, length us, event | category | flops | bytes accessed | tf_op | source)
XLA Modules:
  0.0 136.2 jit_solution(15594482643246469496)
XLA Ops:
  3.2 15.8 %all-to-all-start = ((bf16[64,8,640]{2,1,0:T(8,128)(2,1)}), bf16[64,8,640]{2,1,0:T(8,128)(2,1)S(1)}, u32[]{:S(2)}, u32[]{:S(2)}) async-start(bf16[64,8,640]{2,1,0:T(8,128)(2,1)} %broadcast_in_dim.6), calls=%async_computation | async-start | bytes 1310720 | tf_op jit(solution)/shard_map/all_to_all | solution.py:262
  22.4 17.6 %all-to-all-done = bf16[64,8,640]{2,1,0:T(8,128)(2,1)S(1)} async-done(((bf16[64,8,640]{2,1,0:T(8,128)(2,1)}), bf16[64,8,640]{2,1,0:T(8,128)(2,1)S(1)}, u32[]{:S(2)}, u32[]{:S(2)}) %all-to-all-start) | async-done | bytes 655392 | tf_op jit(solution)/shard_map/all_to_all | solution.py:262
  40.0 3.4 %collective-permute-start = (bf16[8,8,8,640]{3,2,1,0:T(8,128)(2,1)S(1)}, bf16[8,8,8,640]{3,2,1,0:T(8,128)(2,1)S(1)}, u32[]{:S(2)}, u32[]{:S(2)}) collective-permute-start(bf16[8,8,8,640]{3,2,1,0:T(8,128)(2,1)S(1)} %bitcast.21), channel_id=1, source_target_pairs={{0,1},{1,2},{2,3},{3,0},{4,5},{5,6},{6,7},{7,4},{8,9},{9,10},{10,1... | collective-permute-start | bytes 1966088 | tf_op jit(solution)/shard_map/ppermute | solution.py:268
  43.4 1.9 %copy.26 = bf16[128,2,1088]{2,1,0:T(2,128)(2,1)} copy(bf16[128,2,1088]{0,2,1:T(8,128)(2,1)S(1)} %bitcast.26) | data formatting | bytes 1114112 | tf_op jit(solution)/shard_map/optimization_barrier | solution.py:270
  45.3 7.3 %all-to-all-start.1 = ((bf16[128,2,1088]{2,1,0:T(2,128)(2,1)}), bf16[128,2,1088]{2,1,0:T(2,128)(2,1)S(1)}, u32[]{:S(2)}, u32[]{:S(2)}) async-start(bf16[128,2,1088]{2,1,0:T(2,128)(2,1)} %copy.26), calls=%async_computation.1 | async-start | bytes 1179648 | tf_op jit(solution)/shard_map/all_to_all | solution.py:323
  52.6 3.7 %collective-permute-start.1 = (bf16[8,8,8,640]{3,2,1,0:T(8,128)(2,1)S(1)}, bf16[8,8,8,640]{3,2,1,0:T(8,128)(2,1)S(1)}, u32[]{:S(2)}, u32[]{:S(2)}) collective-permute-start(bf16[8,8,8,640]{3,2,1,0:T(8,128)(2,1)S(1)} %bitcast.22), channel_id=1, source_target_pairs={{0,3},{1,0},{2,1},{3,2},{4,7},{5,4},{6,5},{7,6},{8,11},{9,8},{10,9... | collective-permute-start | bytes 1966088 | tf_op jit(solution)/shard_map/ppermute | solution.py:268
  56.3 1.0 collective-permute-done.refs_1_
  57.3 2.2 %collective-permute-start.2 = (bf16[8,8,8,640]{3,2,1,0:T(8,128)(2,1)S(1)}, bf16[8,8,8,640]{3,2,1,0:T(8,128)(2,1)}, u32[]{:S(2)}, u32[]{:S(2)}) collective-permute-start(bf16[8,8,8,640]{3,2,1,0:T(8,128)(2,1)S(1)} %collective-permute-done.refs_1_), channel_id=1, source_target_pairs={{0,1},{1,2},{2,3},{3,0},{4,5},{5,6},{6,7},{7,4},{8,9},{9,10},{10,1... | collective-permute-start | bytes 1966088 | tf_op jit(solution)/shard_map/ppermute | solution.py:268
  59.5 1.9 %collective-permute-start.3 = (bf16[8,8,8,640]{3,2,1,0:T(8,128)(2,1)S(1)}, bf16[8,8,8,640]{3,2,1,0:T(8,128)(2,1)}, u32[]{:S(2)}, u32[]{:S(2)}) collective-permute-start(bf16[8,8,8,640]{3,2,1,0:T(8,128)(2,1)S(1)} %bitcast.23), channel_id=1, source_target_pairs={{0,4},{4,0},{1,5},{5,1},{2,6},{6,2},{3,7},{7,3},{8,12},{12,8},{9,1... | collective-permute-start | bytes 1966088 | tf_op jit(solution)/shard_map/ppermute | solution.py:278
  61.4 2.4 %collective-permute-start.4 = (bf16[8,8,8,640]{3,2,1,0:T(8,128)(2,1)S(1)}, bf16[8,8,8,640]{3,2,1,0:T(8,128)(2,1)}, u32[]{:S(2)}, u32[]{:S(2)}) collective-permute-start(bf16[8,8,8,640]{3,2,1,0:T(8,128)(2,1)S(1)} %collective-permute-done.refs_1_), channel_id=1, source_target_pairs={{0,4},{4,0},{1,5},{5,1},{2,6},{6,2},{3,7},{7,3},{8,12},{12,8},{9,1... | collective-permute-start | bytes 1966088 | tf_op jit(solution)/shard_map/ppermute | solution.py:278
  63.8 7.4 %collective-permute-done.1.refs_2_ = bf16[8,8,8,640]{3,2,1,0:T(8,128)(2,1)S(1)} collective-permute-done((bf16[8,8,8,640]{3,2,1,0:T(8,128)(2,1)S(1)}, bf16[8,8,8,640]{3,2,1,0:T(8,128)(2,1)S(1)}, u32[]{:S(2)}, u32[]{:S(2)}) %collective-permute-start.1) | collective-permute-done | bytes 655392 | tf_op jit(solution)/shard_map/ppermute | solution.py:268
  71.3 1.9 %collective-permute-start.5 = (bf16[8,8,8,640]{3,2,1,0:T(8,128)(2,1)S(1)}, bf16[8,8,8,640]{3,2,1,0:T(8,128)(2,1)}, u32[]{:S(2)}, u32[]{:S(2)}) collective-permute-start(bf16[8,8,8,640]{3,2,1,0:T(8,128)(2,1)S(1)} %collective-permute-done.1.refs_2_), channel_id=1, source_target_pairs={{0,4},{4,0},{1,5},{5,1},{2,6},{6,2},{3,7},{7,3},{8,12},{12,8},{9,1... | collective-permute-start | bytes 1966088 | tf_op jit(solution)/shard_map/ppermute | solution.py:278
  74.2 1.9 %collective-permute-done.2.refs_3_ = bf16[8,8,8,640]{3,2,1,0:T(8,128)(2,1)} collective-permute-done((bf16[8,8,8,640]{3,2,1,0:T(8,128)(2,1)S(1)}, bf16[8,8,8,640]{3,2,1,0:T(8,128)(2,1)}, u32[]{:S(2)}, u32[]{:S(2)}) %collective-permute-start.2) | collective-permute-done | bytes 655392 | tf_op jit(solution)/shard_map/ppermute | solution.py:268
  76.0 2.1 %collective-permute-start.6 = (bf16[8,8,8,640]{3,2,1,0:T(8,128)(2,1)}, bf16[8,8,8,640]{3,2,1,0:T(8,128)(2,1)}, u32[]{:S(2)}, u32[]{:S(2)}) collective-permute-start(bf16[8,8,8,640]{3,2,1,0:T(8,128)(2,1)} %collective-permute-done.2.refs_3_), channel_id=1, source_target_pairs={{0,4},{4,0},{1,5},{5,1},{2,6},{6,2},{3,7},{7,3},{8,12},{12,8},{9,1... | collective-permute-start | bytes 1966088 | tf_op jit(solution)/shard_map/ppermute | solution.py:278
  78.1 1.1 copy.28.arrived_ref
  79.2 4.5 %prepare.1 = (bf16[264,2048]{1,0:T(8,128)(2,1)}, f32[3,88,2048]{2,1,0:T(8,128)}, f32[88,2048]{1,0:T(8,128)}) custom-call(bf16[88,128]{1,0:T(8,128)(2,1)} %get-tuple-element.29.pick_ref, f32[88,128]{1,0:T(8,128)} %get-tuple-element.31.unit_ref, bf16[128,2176]{1,0:T(8,128)(2,1)} %copy.28.arrived_ref, bf16[3,16,2048]{2,1,0:T(8,128)(2,1)} %pad.26.loading_ref, ...), custom_call_target="tpu_custom_call" | custom-call | tf_op jit(solution)/shard_map/prepare/pallas_call | solution.py:325
  83.8 16.5 %solve.1 = (f32[3,81,2048]{2,1,0:T(8,128)}, f32[88,128]{1,0:T(8,128)}, f32[128,128]{1,0:T(8,128)}) custom-call(s32[2]{0:T(128)} %pad_add_fusion.side_ref, bf16[88,128]{1,0:T(8,128)(2,1)} %get-tuple-element.29.pick_ref, bf16[128,2048]{1,0:T(8,128)(2,1)} %pad.28.loading_hbm, bf16[264,2048]{1,0:T(8,128)(2,1)} %get-tuple-element.34.press_hbm, ...), custom_call_target="tpu_custom_call" | custom-call | tf_op jit(solution)/shard_map/solve/pallas_call | solution.py:338
  100.4 13.8 %all-to-all-start.2 = ((f32[128,1,128]{2,1,0:T(1,128)}), f32[128,1,128]{2,1,0:T(1,128)S(1)}, u32[]{:S(2)}, u32[]{:S(2)}) async-start(f32[128,1,128]{2,1,0:T(1,128)} %bitcast.29), calls=%async_computation.2 | async-start | bytes 131072 | tf_op jit(solution)/shard_map/all_to_all | solution.py:366
  114.6 2.0 %collective-permute-start.7 = (f32[8,108]{1,0:T(8,128)S(1)}, f32[8,108]{1,0:T(8,128)S(1)}, u32[]{:S(2)}, u32[]{:S(2)}) collective-permute-start(f32[8,108]{1,0:T(8,128)S(1)} %concatenate.11.own_data_ref), channel_id=1, source_target_pairs={{0,1},{1,2},{2,3},{3,4},{4,5},{5,6},{6,7},{7,8},{8,9},{9,10},{10,1... | collective-permute-start | bytes 10376 | tf_op jit(solution)/shard_map/ppermute | solution.py:246
  117.5 6.3 %collective-permute-done.7.behind_data_ref = f32[8,108]{1,0:T(8,128)S(1)} collective-permute-done((f32[8,108]{1,0:T(8,128)S(1)}, f32[8,108]{1,0:T(8,128)S(1)}, u32[]{:S(2)}, u32[]{:S(2)}) %collective-permute-start.7) | collective-permute-done | bytes 3488 | tf_op jit(solution)/shard_map/ppermute | solution.py:246
  123.8 1.5 %all-to-all-done.2 = f32[128,1,128]{2,1,0:T(1,128)S(1)} async-done(((f32[128,1,128]{2,1,0:T(1,128)}), f32[128,1,128]{2,1,0:T(1,128)S(1)}, u32[]{:S(2)}, u32[]{:S(2)}) %all-to-all-start.2) | async-done | bytes 65568 | tf_op jit(solution)/shard_map/all_to_all | solution.py:366
  125.2 2.0 %collective-permute-start.8 = (f32[128,128]{1,0:T(8,128)S(1)}, f32[128,128]{1,0:T(8,128)S(1)}, u32[]{:S(2)}, u32[]{:S(2)}) collective-permute-start(f32[128,128]{1,0:T(8,128)S(1)} %bitcast.17), channel_id=1, source_target_pairs={{0,1},{1,2},{2,3},{3,4},{4,5},{5,6},{6,7},{7,8},{8,9},{9,10},{10,1... | collective-permute-start | bytes 196616 | tf_op jit(solution)/shard_map/ppermute | solution.py:246
  127.3 7.7 %collective-permute-done.8.behind_ref = f32[128,128]{1,0:T(8,128)S(1)} collective-permute-done((f32[128,128]{1,0:T(8,128)S(1)}, f32[128,128]{1,0:T(8,128)S(1)}, u32[]{:S(2)}, u32[]{:S(2)}) %collective-permute-start.8) | collective-permute-done | bytes 65568 | tf_op jit(solution)/shard_map/ppermute | solution.py:246
  135.0 1.2 corners.1
  (58 shorter events, 8.2 us)
Async XLA Ops:
  0.6 18.3 %copy-start.10 = (s32[81]{0:T(128)S(1)}, s32[81]{0:T(128)}, u32[]{:S(2)}) copy-start(s32[81]{0:T(128)} %param.17) | copy-start | bytes 976
  0.6 18.4 %copy-start.6 = (bf16[27,6]{0,1:T(8,128)(2,1)S(1)}, bf16[27,6]{0,1:T(8,128)(2,1)}, u32[]{:S(2)}) copy-start(bf16[27,6]{0,1:T(8,128)(2,1)} %param.11) | copy-start | bytes 976
  0.7 18.5 %copy-start.4 = (bf16[6,3,2048]{2,1,0:T(4,128)(2,1)S(1)}, bf16[6,3,2048]{2,1,0:T(4,128)(2,1)}, u32[]{:S(2)}) copy-start(bf16[6,3,2048]{2,1,0:T(4,128)(2,1)} %param.19) | copy-start | bytes 221188
  0.7 21.4 %copy-start.8 = (s32[27]{0:T(128)S(1)}, s32[27]{0:T(128)}, u32[]{:S(2)}) copy-start(s32[27]{0:T(128)} %param.16) | copy-start | bytes 328
  0.7 21.4 %copy-start.3 = (bf16[27,2048]{1,0:T(8,128)(2,1)S(1)}, bf16[27,2048]{1,0:T(8,128)(2,1)}, u32[]{:S(2)}) copy-start(bf16[27,2048]{1,0:T(8,128)(2,1)} %param.12) | copy-start | bytes 331780
  3.2 36.8 %all-to-all-start = ((bf16[64,8,640]{2,1,0:T(8,128)(2,1)}), bf16[64,8,640]{2,1,0:T(8,128)(2,1)S(1)}, u32[]{:S(2)}, u32[]{:S(2)}) async-start(bf16[64,8,640]{2,1,0:T(8,128)(2,1)} %broadcast_in_dim.6), calls=%async_computation | async-start | bytes 1310720 | tf_op jit(solution)/shard_map/all_to_all | solution.py:262
  40.0 39.2 %copy-start = (bf16[64,8,640]{2,1,0:T(8,128)(2,1)}, bf16[64,8,640]{2,1,0:T(8,128)(2,1)S(1)}, u32[]{:S(2)}) copy-start(bf16[64,8,640]{2,1,0:T(8,128)(2,1)S(1)} %all-to-all-done) | copy-start | bytes 1966084
  40.0 17.3 %collective-permute-start = (bf16[8,8,8,640]{3,2,1,0:T(8,128)(2,1)S(1)}, bf16[8,8,8,640]{3,2,1,0:T(8,128)(2,1)S(1)}, u32[]{:S(2)}, u32[]{:S(2)}) collective-permute-start(bf16[8,8,8,640]{3,2,1,0:T(8,128)(2,1)S(1)} %bitcast.21), channel_id=1, source_target_pairs={{0,1},{1,2},{2,3},{3,0},{4,5},{5,6},{6,7},{7,4},{8,9},{9,10},{10,1... | collective-permute-start | bytes 1966088 | tf_op jit(solution)/shard_map/ppermute | solution.py:268
  45.3 27.9 %all-to-all-start.1 = ((bf16[128,2,1088]{2,1,0:T(2,128)(2,1)}), bf16[128,2,1088]{2,1,0:T(2,128)(2,1)S(1)}, u32[]{:S(2)}, u32[]{:S(2)}) async-start(bf16[128,2,1088]{2,1,0:T(2,128)(2,1)} %copy.26), calls=%async_computation.1 | async-start | bytes 1179648 | tf_op jit(solution)/shard_map/all_to_all | solution.py:323
  52.6 18.7 %collective-permute-start.1 = (bf16[8,8,8,640]{3,2,1,0:T(8,128)(2,1)S(1)}, bf16[8,8,8,640]{3,2,1,0:T(8,128)(2,1)S(1)}, u32[]{:S(2)}, u32[]{:S(2)}) collective-permute-start(bf16[8,8,8,640]{3,2,1,0:T(8,128)(2,1)S(1)} %bitcast.22), channel_id=1, source_target_pairs={{0,3},{1,0},{2,1},{3,2},{4,7},{5,4},{6,5},{7,6},{8,11},{9,8},{10,9... | collective-permute-start | bytes 1966088 | tf_op jit(solution)/shard_map/ppermute | solution.py:268
  57.3 26.4 %copy-start.1 = (bf16[8,8,8,640]{3,2,1,0:T(8,128)(2,1)}, bf16[8,8,8,640]{3,2,1,0:T(8,128)(2,1)S(1)}, u32[]{:S(2)}) copy-start(bf16[8,8,8,640]{3,2,1,0:T(8,128)(2,1)S(1)} %collective-permute-done.refs_1_) | copy-start | bytes 1966084
  57.3 18.7 %collective-permute-start.2 = (bf16[8,8,8,640]{3,2,1,0:T(8,128)(2,1)S(1)}, bf16[8,8,8,640]{3,2,1,0:T(8,128)(2,1)}, u32[]{:S(2)}, u32[]{:S(2)}) collective-permute-start(bf16[8,8,8,640]{3,2,1,0:T(8,128)(2,1)S(1)} %collective-permute-done.refs_1_), channel_id=1, source_target_pairs={{0,1},{1,2},{2,3},{3,0},{4,5},{5,6},{6,7},{7,4},{8,9},{9,10},{10,1... | collective-permute-start | bytes 1966088 | tf_op jit(solution)/shard_map/ppermute | solution.py:268
  59.5 24.3 %collective-permute-start.3 = (bf16[8,8,8,640]{3,2,1,0:T(8,128)(2,1)S(1)}, bf16[8,8,8,640]{3,2,1,0:T(8,128)(2,1)}, u32[]{:S(2)}, u32[]{:S(2)}) collective-permute-start(bf16[8,8,8,640]{3,2,1,0:T(8,128)(2,1)S(1)} %bitcast.23), channel_id=1, source_target_pairs={{0,4},{4,0},{1,5},{5,1},{2,6},{6,2},{3,7},{7,3},{8,12},{12,8},{9,1... | collective-permute-start | bytes 1966088 | tf_op jit(solution)/shard_map/ppermute | solution.py:278
  61.4 22.3 %collective-permute-start.4 = (bf16[8,8,8,640]{3,2,1,0:T(8,128)(2,1)S(1)}, bf16[8,8,8,640]{3,2,1,0:T(8,128)(2,1)}, u32[]{:S(2)}, u32[]{:S(2)}) collective-permute-start(bf16[8,8,8,640]{3,2,1,0:T(8,128)(2,1)S(1)} %collective-permute-done.refs_1_), channel_id=1, source_target_pairs={{0,4},{4,0},{1,5},{5,1},{2,6},{6,2},{3,7},{7,3},{8,12},{12,8},{9,1... | collective-permute-start | bytes 1966088 | tf_op jit(solution)/shard_map/ppermute | solution.py:278
  71.3 12.5 %copy-start.2 = (bf16[8,8,8,640]{3,2,1,0:T(8,128)(2,1)}, bf16[8,8,8,640]{3,2,1,0:T(8,128)(2,1)S(1)}, u32[]{:S(2)}) copy-start(bf16[8,8,8,640]{3,2,1,0:T(8,128)(2,1)S(1)} %collective-permute-done.1.refs_2_) | copy-start | bytes 1966084
  71.3 12.5 %collective-permute-start.5 = (bf16[8,8,8,640]{3,2,1,0:T(8,128)(2,1)S(1)}, bf16[8,8,8,640]{3,2,1,0:T(8,128)(2,1)}, u32[]{:S(2)}, u32[]{:S(2)}) collective-permute-start(bf16[8,8,8,640]{3,2,1,0:T(8,128)(2,1)S(1)} %collective-permute-done.1.refs_2_), channel_id=1, source_target_pairs={{0,4},{4,0},{1,5},{5,1},{2,6},{6,2},{3,7},{7,3},{8,12},{12,8},{9,1... | collective-permute-start | bytes 1966088 | tf_op jit(solution)/shard_map/ppermute | solution.py:278
  76.0 7.8 %collective-permute-start.6 = (bf16[8,8,8,640]{3,2,1,0:T(8,128)(2,1)}, bf16[8,8,8,640]{3,2,1,0:T(8,128)(2,1)}, u32[]{:S(2)}, u32[]{:S(2)}) collective-permute-start(bf16[8,8,8,640]{3,2,1,0:T(8,128)(2,1)} %collective-permute-done.2.refs_3_), channel_id=1, source_target_pairs={{0,4},{4,0},{1,5},{5,1},{2,6},{6,2},{3,7},{7,3},{8,12},{12,8},{9,1... | collective-permute-start | bytes 1966088 | tf_op jit(solution)/shard_map/ppermute | solution.py:278
  83.8 30.5 %copy-start.7 = (s32[4,27]{1,0:T(4,128)S(1)}, s32[4,27]{1,0:T(4,128)}, u32[]{:S(2)}) copy-start(s32[4,27]{1,0:T(4,128)} %param.15) | copy-start | bytes 1300
  83.8 30.6 %copy-start.9 = (f32[27]{0:T(128)S(1)}, f32[27]{0:T(128)}, u32[]{:S(2)}) copy-start(f32[27]{0:T(128)} %param.14) | copy-start | bytes 328
  83.8 30.7 %copy-start.5 = (f32[12,27]{1,0:T(8,128)S(1)}, f32[12,27]{1,0:T(8,128)}, u32[]{:S(2)}) copy-start(f32[12,27]{1,0:T(8,128)} %param.13) | copy-start | bytes 3892
  100.4 24.8 %all-to-all-start.2 = ((f32[128,1,128]{2,1,0:T(1,128)}), f32[128,1,128]{2,1,0:T(1,128)S(1)}, u32[]{:S(2)}, u32[]{:S(2)}) async-start(f32[128,1,128]{2,1,0:T(1,128)} %bitcast.29), calls=%async_computation.2 | async-start | bytes 131072 | tf_op jit(solution)/shard_map/all_to_all | solution.py:366
  114.6 9.1 %collective-permute-start.7 = (f32[8,108]{1,0:T(8,128)S(1)}, f32[8,108]{1,0:T(8,128)S(1)}, u32[]{:S(2)}, u32[]{:S(2)}) collective-permute-start(f32[8,108]{1,0:T(8,128)S(1)} %concatenate.11.own_data_ref), channel_id=1, source_target_pairs={{0,1},{1,2},{2,3},{3,4},{4,5},{5,6},{6,7},{7,8},{8,9},{9,10},{10,1... | collective-permute-start | bytes 10376 | tf_op jit(solution)/shard_map/ppermute | solution.py:246
  125.2 9.8 %collective-permute-start.8 = (f32[128,128]{1,0:T(8,128)S(1)}, f32[128,128]{1,0:T(8,128)S(1)}, u32[]{:S(2)}, u32[]{:S(2)}) collective-permute-start(f32[128,128]{1,0:T(8,128)S(1)} %bitcast.17), channel_id=1, source_target_pairs={{0,1},{1,2},{2,3},{3,4},{4,5},{5,6},{6,7},{7,8},{8,9},{9,10},{10,1... | collective-permute-start | bytes 196616 | tf_op jit(solution)/shard_map/ppermute | solution.py:246
